TPU v7x, 32 devices: a whole 2x2x4 slice. The times are simulated.
32 devices in a mesh: row: 8 (over y, x, core), col: 4 (over z).
Axes of the slice: x: 2, y: 2, z: 4, core: 2. Of those that a mesh axis runs over, the one named last changes fastest.
Arguments:
- legendre: bfloat16 [4, 128, 89, 8, 128], P(None, 'col', None, 'row'), may hold values from -6 to 6
- longitude: float32 [512], replicated, may hold values from -3.140625 to 3.140625
- obs_weight: float32 [512], replicated, may hold values from 0.1 to 1.9
- span_weight: float32 [8], replicated, may hold values from 0.3 to 3
- span_of: int32 [512], replicated, may hold values from 0 to 7
- tile_order: int32 [712], replicated, may hold values from 0 to 711, each once
- slab_start: int32 [1], replicated, may hold values from 0 to 704
- resident: float32 [89, 8, 4, 128, 128], P(None, 'row', 'col'), may hold values from -6 to 6
Outputs:
- updated: float32 [89, 8, 4, 128, 128], P(None, 'row', 'col')
Inputs may be any that keep to these rules, and one draw needn't show every extreme that they name: tile_order is a permutation of the slot positions.
All inputs are finite; a program needn't handle non-finite values.
Results may differ from a plain program's by a relative error of at most 0.00074.
Values may be sent and summed in bfloat16 or wider, within the bound.
No kernel may reach another device: no remote copies, remote signals or barrier semaphores. Data moves between devices by JAX's collectives and lax.ppermute only.
A program may use at most 64 MiB of HBM per device.

v0:
```python
import math

import jax
import jax.numpy as jnp
from jax import lax
from jax.sharding import PartitionSpec as P

DEGREE = 300
UNK = 90600


def lookup_weights(obs_weight, span_weight, span_of):
    group_count = span_weight.shape[0]
    matches = span_of[:, None] == jnp.arange(group_count, dtype=jnp.int32)[None, :]
    factor = jnp.sum(jnp.where(matches, span_weight[None, :], 0.0), axis=1)
    return obs_weight * factor * (0.25 / math.sqrt(obs_weight.shape[0]))


def locate(tile_order, targets):
    places = jnp.arange(tile_order.shape[0], dtype=jnp.int32)
    return jnp.sum(jnp.where(tile_order[None, :] == targets[:, None], places[None, :], 0), axis=1)


def contract_rows(left_side, right_side):
    return lax.dot_general(
        left_side, right_side, (((0,), (0,)), ((), ())), preferred_element_type=jnp.float32
    )


def per_device(
    legendre, longitude, obs_weight, span_weight, span_of, tile_order, slab_start, resident
):
    block_count, shard_rows, slot_count, _, tile_size = legendre.shape
    row_count = lax.axis_size("row")
    col_count = lax.axis_size("col")
    row_index = lax.axis_index("row")
    col_index = lax.axis_index("col")
    block_rows = shard_rows * col_count
    order_map = tile_order.reshape(slot_count, row_count)
    own_tiles = lax.dynamic_slice_in_dim(order_map, row_index, 1, 1)[:, 0]
    unknown = own_tiles[:, None] * tile_size + jnp.arange(tile_size, dtype=jnp.int32)[None, :]
    orders = (unknown % (DEGREE + 1)).astype(jnp.float32).reshape(1, slot_count * tile_size)
    is_valid = (unknown < UNK).reshape(1, slot_count * tile_size)
    targets = slab_start[0] + jnp.arange(col_count, dtype=jnp.int32)
    positions = locate(tile_order, targets)
    target = targets[col_index]
    root_row = positions[col_index] % row_count
    root_slots = positions // row_count
    root_slot = root_slots[col_index]
    is_root = row_index == root_row
    weights = lookup_weights(obs_weight, span_weight, span_of).reshape(block_count, block_rows)
    angles = longitude.reshape(block_count, block_rows)
    in_lower = own_tiles >= target
    zero_piece = jnp.zeros((), jnp.bfloat16)
    all_values = legendre.reshape(block_count * shard_rows, slot_count * tile_size)
    own_angles = lax.dynamic_slice_in_dim(angles, col_index * shard_rows, shard_rows, 1)
    own_angles = own_angles.reshape(block_count * shard_rows)
    design_all = jnp.where(
        is_valid, all_values.astype(jnp.float32) * jnp.cos(own_angles[:, None] * orders), 0.0
    ).astype(jnp.bfloat16)
    design_all = design_all.reshape(block_count, shard_rows, slot_count * tile_size)
    gathered = lax.all_gather(design_all, "col", axis=1, tiled=True)
    gathered = gathered.reshape(block_count * block_rows, slot_count * tile_size)
    candidate = lax.dynamic_slice_in_dim(gathered, root_slot * tile_size, tile_size, 1)
    column = lax.psum(jnp.where(is_root, candidate, zero_piece), "row").astype(jnp.float32)
    weighted = (weights.reshape(block_count * block_rows)[:, None] * column).astype(jnp.bfloat16)
    running = contract_rows(gathered, weighted)
    update = jnp.where(
        in_lower[:, None, None], running.reshape(slot_count, tile_size, tile_size), 0.0
    )
    return resident + update.reshape(resident.shape)


def solution(mesh):
    placed = (
        P(None, "col", None, "row", None),
        P(),
        P(),
        P(),
        P(),
        P(),
        P(),
        P(None, "row", "col", None, None),
    )
    return jax.shard_map(
        per_device,
        mesh=mesh,
        in_specs=placed,
        out_specs=P(None, "row", "col", None, None),
        check_vma=False,
    )
```

profile of v0, /device:TPU:0, one launch (start us, length us, event | category | flops | bytes accessed | tf_op | source)
XLA Modules:
  0.0 322.1 jit_solution(3542823524447298766)
XLA Ops:
  6.5 0.0 copy-start
  6.5 0.0 all-gather.2.cloned.1.call-start
  6.5 0.8 reshape.90
  7.3 0.2 multiply_reduce_fusion
  7.5 0.1 fusion.4
  7.6 0.1 fusion.8
  7.7 5.5 %copy.20 = f32[4,32,89,1,128]{4,2,1,0,3:T(8,128)} copy(bf16[4,32,89,1,128]{4,1,3,2,0:T(8,128)(2,1)} %param.8) | data formatting | bytes 8749056 | tf_op jit(solution)/shard_map/convert_element_type | solution.py:59
  13.2 7.2 %reshape.94 = f32[4,32,11392]{2,1,0:T(8,128)} reshape(f32[4,32,89,1,128]{4,2,1,0,3:T(8,128)} %copy.20) | data formatting | bytes 11665408 | tf_op jit(solution)/shard_map/convert_element_type | solution.py:59
  20.4 0.0 copy-done
  20.4 0.1 constant_dynamic-slice_fusion
  20.5 0.0 copy-start.1
  20.5 0.0 copy-start.3
  20.5 0.0 copy-start.4
  20.5 22.0 %select_convert_fusion = bf16[4,32,11392]{2,1,0:T(8,128)(2,1)} fusion(f32[4,32,11392]{2,1,0:T(8,128)} %reshape.94, f32[11392]{0:T(1024)S(1)} %fusion.4, f32[4,32]{1,0:T(4,128)S(1)} %constant_dynamic-slice_fusion, pred[11392]{0:T(1024)(128)(4,1)S(1)} %fusion.8), kind=kLoop, calls=%fused_computation.2 | loop fusion | flops 5832704 | bytes 8806528 | tf_op jit(solution)/shard_map/convert_element_type | solution.py:60
  42.6 0.0 all-gather.2.cloned.1.call-update
  42.6 0.0 all-reduce.2.cloned.1.call-start
  43.3 0.0 copy-done.1
  43.3 0.2 select_reduce_fusion.1
  43.5 0.6 dynamic_slice.21
  46.0 0.6 dynamic_slice.22
  47.3 0.0 copy-done.3
  47.3 0.0 copy-done.4
  47.3 0.1 select_reduce_fusion
  47.4 201.2 %all-gather.2.cloned.1.call-done = bf16[4,128,11392]{2,1,0:T(8,128)(2,1)} async-done(((bf16[4,32,11392]{2,1,0:T(8,128)(2,1)}), bf16[4,128,11392]{2,1,0:T(8,128)(2,1)}) %all-gather.2.cloned.1.call-update) | async-done | bytes 11665424 | tf_op jit(solution)/shard_map/all_gather | solution.py:62
  248.6 1.6 dynamic-slice_select_fusion
  250.2 0.0 all-reduce.2.cloned.1.call-update
  250.3 0.0 copy-done.2
  250.3 0.6 dynamic_slice.19
  250.9 0.8 compare_reduce_fusion
  251.7 16.2 %copy.21 = bf16[11392,512]{1,0:T(8,128)(2,1)} copy(bf16[11392,512]{0,1:T(8,128)(2,1)} %bitcast.39) | data formatting | bytes 23330816 | tf_op jit(solution)/shard_map/dot_general | solution.py:25
  267.9 35.4 %all-reduce.2.cloned.1.call-done = bf16[512,128]{1,0:T(8,128)(2,1)} async-done(((bf16[512,128]{1,0:T(8,128)(2,1)}), bf16[512,128]{1,0:T(8,128)(2,1)}) %all-reduce.2.cloned.1.call-update) | async-done | bytes 131088 | tf_op jit(solution)/shard_map/psum | solution.py:65
  303.3 11.9 %fusion = f32[89,1,1,128,128]{4,3,2,1,0:T(8,128)} fusion(f32[89,1,1,128,128]{4,3,2,1,0:T(8,128)} %param.15, pred[89]{0:T(512)(128)(4,1)S(1)} %compare_reduce_fusion, bf16[89,128,512]{2,1,0:T(8,128)(2,1)} %bitcast.37, bf16[512,128]{1,0:T(8,128)(2,1)} %all-reduce.2.cloned.1.call-done, f32[512]{0:T(512)S(1)} %multiply_multiply_fusion), kind=kOutput, calls=%fused_computation.1 | convolution fusion | flops 1496285184 | bytes 23464024 | tf_op jit(solution)/shard_map/dot_general | solution.py:25
  (4 shorter events, 0.0 us)
Async XLA Ops:
  6.5 13.9 %copy-start = (f32[512]{0:T(512)S(1)}, f32[512]{0:T(512)}, u32[]{:S(2)}) copy-start(f32[512]{0:T(512)} %param.9) | copy-start | bytes 6148
  6.5 242.1 %all-gather.2.cloned.1.call-start = ((), (), s32[]{:S(2)}) async-start(), calls=%async_computation | async-start | bytes 14581760 | tf_op jit(solution)/shard_map/all_gather | solution.py:62
  20.5 22.8 %copy-start.1 = (s32[712]{0:T(1024)S(1)}, s32[712]{0:T(1024)}, u32[]{:S(2)}) copy-start(s32[712]{0:T(1024)} %param.13) | copy-start | bytes 8548
  20.5 26.8 %copy-start.3 = (s32[512]{0:T(512)S(1)}, s32[512]{0:T(512)}, u32[]{:S(2)}) copy-start(s32[512]{0:T(512)} %param.12) | copy-start | bytes 6148
  20.5 26.8 %copy-start.4 = (f32[8]{0:T(128)S(1)}, f32[8]{0:T(128)}, u32[]{:S(2)}) copy-start(f32[8]{0:T(128)} %param.11) | copy-start | bytes 100
  20.5 229.8 %copy-start.2 = (f32[512]{0:T(512)S(1)}, f32[512]{0:T(512)}, u32[]{:S(2)}) copy-start(f32[512]{0:T(512)} %param.10) | copy-start | bytes 6148
  42.6 260.7 %all-reduce.2.cloned.1.call-start = ((), (), s32[]{:S(2)}) async-start(), calls=%async_computation.1 | async-start | bytes 262144 | tf_op jit(solution)/shard_map/psum | solution.py:65
Sparse Core Ops, SparseCore 0:
  42.7 205.8 all-gather.1
  251.7 51.6 all-reduce.1
where the time goes:
time: 323 us; the launch traced here: 322 us
  waiting for transfers between devices  237 us (73%)
  local copies, waits for them, and re-layouts  31.5 us (10%)
  other arithmetic  25.1 us (8%)
  between operations  16.8 us (5%)
  matrix products  11.9 us (4%)
    all_gather x1, waiting for transfers between devices, per_device(): gathered = lax.all_gather(design_all, 'col', axis=1, tiled=True)  201 us
    psum x1, waiting for transfers between devices, per_device(): lax.psum(jnp.where(is_root, candidate, zero_piece), 'row')  35.4 us
    convert_element_type x1, other arithmetic, per_device(): design_all = jnp.where(is_valid, all_values.astype(jnp.float32) * jnp.cos...  22 us
    dot_general x1, local copies, waits for them, and re-layouts, contract_rows(): lax.dot_general(left_side, right_side, (((0,), (0,)), ((), ())), preferre...  16.2 us
    convert_element_type x2, local copies, waits for them, and re-layouts, per_device(): all_values.astype(jnp.float32) * jnp.cos(own_angles[:, None] * orders)  12.7 us
    dot_general x1, matrix products, contract_rows(): lax.dot_general(left_side, right_side, (((0,), (0,)), ((), ())), preferre...  11.9 us
  transfers between devices with their start and end apart: 2, of which 2 were waited for; matrix products, arithmetic and copies ran while one was open for 6% of the time, Pallas kernels for 0%

commit v1 on v0

v1 whole, which is shorter than its diff:
```python
import functools
import math

import jax
import jax.numpy as jnp
from jax import lax
from jax.experimental import pallas as pl
from jax.experimental.pallas import tpu as pltpu
from jax.sharding import PartitionSpec as P


DEGREE = 300
UNK = 90600
PERIOD = DEGREE + 1


def whole(space=pltpu.VMEM):
    return pl.BlockSpec(memory_space=space)


def lookup_weights(obs_weight, span_weight, span_of):
    group_count = span_weight.shape[0]
    matches = span_of[:, None] == jnp.arange(group_count, dtype=jnp.int32)[None, :]
    factor = jnp.sum(jnp.where(matches, span_weight[None, :], 0.0), axis=1)
    return obs_weight * factor * (0.25 / math.sqrt(obs_weight.shape[0]))


def first_counts(slot_count):
    return max(2, (slot_count * 16) // 100), max(2, (slot_count * 9) // 100)


def rest_counts(slot_count):
    most = slot_count - first_counts(slot_count)[0]
    counts = [count for count in (0,) + tuple(range(8, most, 11)) if count <= most - 6]
    return counts + [most]


def chunk_sizes(total, second):
    if total <= second + 1:
        return [total] if total else []
    if total <= second + 12:
        return [second, total - second]
    left = total - second - 6
    count = -(-left // 22)
    return [second] + [left * (k + 1) // count - left * k // count for k in range(count)] + [6]


def design_tile(tile, slot, legendre, table):
    blocks, _, rows, lanes = legendre.shape
    start = lax.rem(tile * lanes, PERIOD)
    base = start // lanes
    shift = start - base * lanes
    turn = lax.rem(lanes - shift, lanes)
    lane = lax.broadcasted_iota(jnp.int32, (blocks * rows, lanes), 1)
    low = pltpu.roll(table[base], turn, 1)
    high = pltpu.roll(table[base + 1], turn, 1)
    wave = jnp.where(lane < lanes - shift, low, high)
    values = legendre[:, slot].astype(jnp.float32).reshape(blocks * rows, lanes)
    result = jnp.where(lane < UNK - tile * lanes, values * wave, 0.0)
    return result.astype(jnp.bfloat16)


def plan_kernel(
    counts, first, row_count, slab_start, order, legendre, table, weight,
    listed, info, output,
):
    lanes = legendre.shape[3]
    total = order.shape[0]
    width = listed.shape[1]
    start = slab_start[0]
    row = lax.axis_index("row")
    col = lax.axis_index("col")
    tiles = order[...].reshape(1, total)
    spot = lax.broadcasted_iota(jnp.int32, (1, total), 1)
    needed = (tiles >= start) & (tiles * lanes < UNK)
    rows = lax.broadcasted_iota(jnp.int32, (row_count, total), 0)
    matches = jnp.broadcast_to(jnp.where(needed, 1, 0), rows.shape)
    matches = jnp.where(lax.rem(spot, row_count) == rows, matches, 0)
    most = jnp.max(jnp.sum(matches, axis=1))
    choice = jnp.int32(0)
    for below in counts[:-1]:
        choice += jnp.where(most > first + below, 1, 0)

    mine = lax.rem(spot, row_count) == row
    own = jnp.where(needed & mine, 1.0, 0.0)
    before = jnp.dot(
        jnp.broadcast_to(own, (8, total)).astype(jnp.bfloat16),
        (
            lax.broadcasted_iota(jnp.int32, (total, total), 0)
            < lax.broadcasted_iota(jnp.int32, (total, total), 1)
        ).astype(jnp.float32).astype(jnp.bfloat16),
        preferred_element_type=jnp.float32,
    )[:1]
    slot = (spot // row_count).astype(jnp.float32)
    target = jnp.where(needed, before, jnp.sum(own) + slot - before)
    target = jnp.where(mine, target, -1.0)
    ids = lax.broadcasted_iota(jnp.int32, (width, total), 0).astype(jnp.float32)
    hits = jnp.where(ids == target, 1.0, 0.0)
    pair = lax.broadcasted_iota(jnp.int32, (8, total), 0)
    pair = jnp.where(pair == 0, slot, tiles.astype(jnp.float32))
    found = lax.dot_general(
        pair, hits, (((1,), (1,)), ((), ())),
        precision=lax.Precision.HIGHEST, preferred_element_type=jnp.float32,
    )
    listed[...] = found.astype(jnp.int32)
    info[...] = jnp.broadcast_to(choice, info.shape)

    col_count = output.shape[0]
    half = col_count // 2
    is_right = col >= half
    for place in range(col_count):
        near_left = place if place < half else col_count - 1 - (place - half)
        near_right = col_count - 1 - near_left
        tile = start + jnp.where(is_right, near_right, near_left)
        position = jnp.sum(jnp.where(tiles == tile, spot, 0))
        column = design_tile(tile, position // row_count, legendre, table)
        column = weight[...] * column.astype(jnp.float32)
        column = jnp.where(lax.rem(position, row_count) == row, column, 0.0)
        output[place] = column.astype(jnp.bfloat16)


def design_kernel(offset, listed, legendre, table, output):
    def step(index, carry):
        output[index] = design_tile(
            listed[1, offset + index], listed[0, offset + index], legendre, table
        )
        return carry

    lax.fori_loop(0, output.shape[0], step, 0)


def factor_kernel(inner, half, *refs):
    streams, output = refs[:-1], refs[-1]
    rows, lanes = streams[0].shape[1:]
    col = lax.axis_index("col")
    spot = jnp.where(col >= half, 2 * half - 1 - col, col)
    for index, stream in enumerate(streams):
        here = pl.ds(index * rows, rows)
        output[here, :lanes] = stream[spot]
        if 1 <= index <= inner:
            output[here, lanes:] = jnp.zeros_like(stream[0])
        else:
            output[here, lanes:] = stream[0]


def stacked(streams, first, width):
    return jnp.concatenate(
        [jnp.concatenate([s[first + k] for s in streams], 0) for k in range(width)], 1
    )


def product_kernel(factor, *refs):
    streams, own, end = refs[:-2], refs[-2], refs[-1]
    lanes = own.shape[1]
    size = own.shape[0]

    def piece(first, width):
        both = lax.dot_general(
            stacked(streams, first, width), factor[...],
            (((0,), (0,)), ((), ())), preferred_element_type=jnp.float32,
        )
        for k in range(width):
            own[first + k] = both[k * lanes : (k + 1) * lanes, :lanes]
            end[first + k] = both[k * lanes : (k + 1) * lanes, lanes:]

    def step(index, carry):
        piece(2 * index, 2)
        return carry

    lax.fori_loop(0, size // 2, step, 0)
    if size % 2:
        piece(size - 1, 1)


def copy_kernel(offset, listed, resident, output, held, ins, outs):
    size = held.shape[0]

    def fetch(index):
        slot = listed[0, offset + index]
        return pltpu.make_async_copy(resident.at[slot], held.at[index], ins.at[index])

    def store(index):
        slot = listed[0, offset + index]
        return pltpu.make_async_copy(held.at[index], output.at[slot], outs.at[index])

    @pl.loop(0, size)
    def _(index):
        fetch(index).start()

    @pl.loop(0, size)
    def _(index):
        fetch(index).wait()
        store(index).start()

    @pl.loop(0, size)
    def _(index):
        store(index).wait()


def update_kernel(
    offset, listed, slab_start, own, extra, resident, *refs,
):
    output, own_held, extra_held, old, new, ins, outs, more = refs[-8:]
    size = old.shape[0]
    lanes = old.shape[1]
    column = slab_start[0] + lax.axis_index("col")
    own_copy = pltpu.make_async_copy(own, own_held, more.at[0])
    extra_copy = pltpu.make_async_copy(extra, extra_held, more.at[1])

    def fetch(index):
        return pltpu.make_async_copy(
            resident.at[listed[0, offset + index]], old.at[index], ins.at[index]
        )

    def store(index):
        return pltpu.make_async_copy(
            new.at[index], output.at[listed[0, offset + index]], outs.at[index]
        )

    own_copy.start()
    extra_copy.start()

    @pl.loop(0, size)
    def _(index):
        fetch(index).start()

    own_copy.wait()
    extra_copy.wait()

    @pl.loop(0, size)
    def _(index):
        fetch(index).wait()
        tile = listed[1, offset + index]
        keep = (tile >= column) & (tile * lanes < UNK)
        change = own_held[index] + extra_held[index]
        new[index] = old[index] + jnp.where(keep, change, 0.0)
        store(index).start()

    @pl.loop(0, size)
    def _(index):
        store(index).wait()


def per_device(
    legendre, longitude, obs_weight, span_weight, span_of, tile_order, slab_start, resident
):
    block_count, shard_rows, slot_count, _, lanes = legendre.shape
    row_count = lax.axis_size("row")
    col_count = lax.axis_size("col")
    col_index = lax.axis_index("col")
    half = col_count // 2
    block_rows = shard_rows * col_count
    own_rows = block_count * shard_rows
    inner = half - 1
    bf16 = jnp.bfloat16
    smem, vmem, anywhere = whole(pltpu.SMEM), whole(), whole(pl.ANY)

    def mirrored(pairs):
        other = [(col_count - 1 - a, col_count - 1 - b) for a, b in pairs]
        return pairs + other

    inward = mirrored([(i, i + 1) for i in range(half - 1)])
    middles = [mirrored([(half - 1 - t, half)]) for t in range(half)]
    outward = mirrored([(i, i - 1) for i in range(2, half)])
    last_hop = mirrored([(1, 0)])

    def shift(value, pairs, axis="col"):
        return lax.ppermute(value, axis, pairs)

    def streams_of(whole_item, near, far):
        ins = []
        for _ in range(inner):
            ins.append(shift(ins[-1] if ins else whole_item, inward))
        mids = [shift(far(whole_item), pairs) for pairs in middles]
        froms = []
        for t in range(col_count - 2):
            piece = mids[t] if t < half else None
            if outward:
                moved = near(whole_item) if t == 0 else froms[-1]
                moved = shift(moved, outward)
                piece = moved if piece is None else piece + moved
            froms.append(piece)
        return [near(item) for item in [whole_item] + ins], froms

    def same(item):
        return item

    def own_part(values):
        values = values.reshape(block_count, block_rows)
        return lax.dynamic_slice_in_dim(values, col_index * shard_rows, shard_rows, 1)

    weights = own_part(lookup_weights(obs_weight, span_weight, span_of))
    weights = jnp.broadcast_to(weights.reshape(own_rows, 1), (own_rows, lanes))
    pages = PERIOD // lanes + 2
    lane_orders = jnp.arange(pages * lanes, dtype=jnp.int32) % PERIOD
    lane_orders = lane_orders.astype(jnp.float32).reshape(pages, 1, lanes)
    table = jnp.cos(own_part(longitude).reshape(1, own_rows, 1) * lane_orders)

    values = legendre.transpose(0, 2, 3, 1, 4).reshape(block_count, slot_count, shard_rows, lanes)
    old = resident.reshape(slot_count, lanes, lanes)
    first, second = first_counts(slot_count)
    counts = rest_counts(slot_count)
    tile_shape = (own_rows, lanes)

    def tiles_of(size):
        return jax.ShapeDtypeStruct((size,) + tile_shape, bf16)

    def held(size):
        return pltpu.VMEM((size, lanes, lanes), jnp.float32)

    def sems(size):
        return pltpu.SemaphoreType.DMA((size,))

    def design(offset, size, listed, values, table):
        return pl.pallas_call(
            functools.partial(design_kernel, offset),
            out_shape=tiles_of(size),
            in_specs=[smem] + [vmem] * 2,
            out_specs=vmem,
            name="design",
        )(listed, values, table)

    listed, info, both = pl.pallas_call(
        functools.partial(plan_kernel, counts, first, row_count),
        out_shape=[
            jax.ShapeDtypeStruct((8, -(-slot_count // 128) * 128), jnp.int32),
            jax.ShapeDtypeStruct((1, 128), jnp.int32),
            tiles_of(col_count),
        ],
        in_specs=[smem] + [vmem] * 4,
        out_specs=[vmem] * 3,
        name="plan",
    )(slab_start, tile_order, values, table, weights)

    own_first = design(0, first, listed, values, table)
    nears, froms = streams_of(own_first, same, same)
    streams_first = nears + froms
    bit = 1
    while bit < row_count:
        pairs = [(r, r ^ bit) for r in range(row_count)]
        both = both + shift(both, pairs, "row")
        bit *= 2
    nears, froms = streams_of(both, lambda x: x[:half], lambda x: x[half:])
    factors = nears + froms
    factor = pl.pallas_call(
        functools.partial(factor_kernel, inner, half),
        out_shape=jax.ShapeDtypeStruct((len(factors) * own_rows, 2 * lanes), bf16),
        in_specs=[vmem] * len(factors),
        out_specs=vmem,
        name="factor",
    )(*factors)

    def copy_rest(offset, listed, old):
        size = slot_count - offset
        if not size:
            return []
        output = pl.pallas_call(
            functools.partial(copy_kernel, offset),
            in_specs=[smem, anywhere],
            out_specs=anywhere,
            out_shape=jax.ShapeDtypeStruct(old.shape, old.dtype),
            scratch_shapes=[held(size), sems(size), sems(size)],
        )(listed, old)
        return [output]

    def multiply(factor, streams):
        product = jax.ShapeDtypeStruct((streams[0].shape[0], lanes, lanes), jnp.float32)
        return pl.pallas_call(
            product_kernel,
            out_shape=[product, product],
            in_specs=[vmem] * (1 + len(streams)),
            out_specs=[vmem] * 2,
            name="product",
        )(factor, *streams)

    def update(offset, listed, slab_start, own, extra, old, previous):
        size = own.shape[0]
        return pl.pallas_call(
            functools.partial(update_kernel, offset),
            in_specs=[smem] * 2 + [anywhere] * (3 + len(previous)),
            out_specs=anywhere,
            out_shape=jax.ShapeDtypeStruct(old.shape, old.dtype),
            scratch_shapes=[held(size)] * 4 + [sems(size), sems(size), sems(2)],
            input_output_aliases={5: 0} if previous else {},
            name="update",
        )(listed, slab_start, own, extra, old, *previous)

    def branch(total):
        def run(factor, streams_first, listed, slab_start, old, values, table):
            output = copy_rest(first + total, listed, old)
            waiting, offset = [], 0
            for k, size in enumerate([first] + chunk_sizes(total, second)):
                streams = streams_first
                if k > 0:
                    piece = design(offset, size, listed, values, table)
                    nears, froms = streams_of(piece, same, same)
                    streams = nears + froms
                own, end = multiply(factor, streams)
                waiting.append((k, offset, own, shift(end, last_hop)))
                offset += size
            for k, offset, own, extra in waiting:
                output = [update(offset, listed, slab_start, own, extra, old, output)]
            return output[0]

        return run

    output = lax.switch(
        info[0, 0],
        [branch(total) for total in counts],
        factor, streams_first, listed, slab_start, old, values, table,
    )
    return output.reshape(resident.shape)


def solution(mesh):
    placed = (
        P(None, "col", None, "row", None),
        P(),
        P(),
        P(),
        P(),
        P(),
        P(),
        P(None, "row", "col", None, None),
    )
    return jax.shard_map(
        per_device,
        mesh=mesh,
        in_specs=placed,
        out_specs=P(None, "row", "col", None, None),
        check_vma=False,
    )
```

time: 323 us -> 127 us (0.39)
  waiting for transfers between devices: 237 us -> 28 us
  starting transfers between devices: 0.04 us -> 44.8 us
  Pallas kernels: 0 us -> 40.4 us
  local copies, waits for them, and re-layouts: 31.5 us -> 6.71 us
  other arithmetic: 25.1 us -> 4.48 us
  between operations: 16.8 us -> 1.55 us
  matrix products: 11.9 us -> 0 us
    all_gather x1 -> x0, waiting for transfers between devices: 201 us -> none  [per_device(): gathered = lax.all_gather(design_all, 'col', axis=1, tiled=True)]
    ppermute x0 -> x18, starting transfers between devices: none -> 44.8 us  [shift(): return lax.ppermute(value, axis, pairs)]
    pallas_call x0 -> x12, Pallas kernels: none -> 40.4 us  [the longest x3 12 us: multiply(): pl.pallas_call(product_kernel, out_shape=[product, product], in_specs=[vm...]
    psum x1 -> x0, waiting for transfers between devices: 35.4 us -> none  [per_device(): lax.psum(jnp.where(is_root, candidate, zero_piece), 'row')]
    ppermute x0 -> x18, waiting for transfers between devices: none -> 28 us  [shift(): return lax.ppermute(value, axis, pairs)]
    convert_element_type x2 -> x1, other arithmetic: 22.2 us -> 0.02 us  [per_device(): lane_orders = lane_orders.astype(jnp.float32).reshape(pages, 1, lanes)]
    dot_general x1 -> x0, local copies, waits for them, and re-layouts: 16.2 us -> none  [contract_rows(): lax.dot_general(left_side, right_side, (((0,), (0,)), ((), ())), preferre...]
    convert_element_type x2 -> x0, local copies, waits for them, and re-layouts: 12.7 us -> none  [per_device(): all_values.astype(jnp.float32) * jnp.cos(own_angles[:, None] * orders)]
  transfers between devices with their start and end apart: 2 -> 18, of which waited for: 2 -> 5; matrix products, arithmetic and copies ran while one was open for 6% -> 2% of each run, Pallas kernels for 0% -> 24%
where the time goes in v1:
time: 127 us; the launch traced here: 126 us
  starting transfers between devices  44.8 us (35%)
  Pallas kernels  40.4 us (32%)
  waiting for transfers between devices  28 us (22%)
  local copies, waits for them, and re-layouts  6.71 us (5%)
  other arithmetic  4.48 us (4%)
  between operations  1.55 us (1%)
    ppermute x18, starting transfers between devices, shift(): return lax.ppermute(value, axis, pairs)  44.8 us
    ppermute x18, waiting for transfers between devices, shift(): return lax.ppermute(value, axis, pairs)  28 us
    pallas_call x3, Pallas kernels, multiply(): pl.pallas_call(product_kernel, out_shape=[product, product], in_specs=[vm...  12 us
    pallas_call x3, Pallas kernels, update(): pl.pallas_call(functools.partial(update_kernel, offset), in_specs=[smem]...  10.9 us
    pallas_call x3, Pallas kernels, design(): pl.pallas_call(functools.partial(design_kernel, offset), out_shape=tiles_...  8.06 us
    pallas_call x1, Pallas kernels, copy_rest(): pl.pallas_call(functools.partial(copy_kernel, offset), in_specs=[smem, an...  5.14 us
    pallas_call x1, Pallas kernels, per_device(): pl.pallas_call(functools.partial(plan_kernel, counts, first, row_count),...  3.3 us
    cond x10, local copies, waits for them, and re-layouts  3.15 us
  transfers between devices with their start and end apart: 18, of which 5 were waited for; matrix products, arithmetic and copies ran while one was open for 2% of the time, Pallas kernels for 24%

profile of v1, /device:TPU:0, one launch (start us, length us, event | category | flops | bytes accessed | tf_op | source)
XLA Modules:
  0.0 126.4 jit_solution(6146627992104908175)
XLA Ops:
  4.9 3.3 %plan.1 = (s32[8,128]{1,0:T(8,128)S(1)}, s32[1,128]{1,0:T(1,128)}, bf16[4,128,128]{2,1,0:T(8,128)(2,1)}) custom-call(s32[1]{0:T(128)S(6)} %copy.99.slab_start, s32[712]{0:T(1024)} %order.1, bf16[4,89,32,128]{3,2,1,0:T(8,128)(2,1)} %bitcast.51, f32[4,128,128]{2,1,0:T(8,128)S(1)} %multiply_cosine_fusion.table, f32[128,128]{1,0:T(8,128)} %broadcast_in_dim.25.weight), custom_call_target="tpu_custom_call" | custom-call | tf_op jit(solution)/shard_map/plan/pallas_call | solution.py:323
  8.6 1.2 collective-permute-done.104
  10.8 2.9 %collective-permute-start.105 = (bf16[4,128,128]{2,1,0:T(8,128)(2,1)S(1)}, bf16[4,128,128]{2,1,0:T(8,128)(2,1)}, u32[]{:S(2)}, u32[]{:S(2)}) collective-permute-start(bf16[4,128,128]{2,1,0:T(8,128)(2,1)S(1)} %add.30), channel_id=1, source_target_pairs={{0,8},{4,12},{8,0},{12,4},{16,24},{20,28},{24,16},{28,20},{1,9},{5... | collective-permute-start | bytes 393224 | tf_op jit(solution)/shard_map/ppermute | solution.py:268
  13.7 3.1 %design.49 = bf16[14,128,128]{2,1,0:T(8,128)(2,1)} custom-call(s32[8,128]{1,0:T(8,128)S(1)} %get-tuple-element.318.listed, bf16[4,89,32,128]{3,2,1,0:T(8,128)(2,1)S(1)} %bitcast.52, f32[4,128,128]{2,1,0:T(8,128)S(1)} %multiply_cosine_fusion.table), custom_call_target="tpu_custom_call" | custom-call | tf_op jit(solution)/shard_map/design/pallas_call | solution.py:315
  16.8 4.3 %collective-permute-start.110 = (bf16[14,128,128]{2,1,0:T(8,128)(2,1)}, bf16[14,128,128]{2,1,0:T(8,128)(2,1)}, u32[]{:S(2)}, u32[]{:S(2)}) collective-permute-start(bf16[14,128,128]{2,1,0:T(8,128)(2,1)} %design.49), channel_id=1, source_target_pairs={{0,1},{3,2},{4,5},{7,6},{8,9},{11,10},{12,13},{15,14},{16,17},{19,... | collective-permute-start | bytes 1376264 | tf_op jit(solution)/shard_map/ppermute | solution.py:268
  21.0 1.5 %collective-permute-start.111 = (bf16[14,128,128]{2,1,0:T(8,128)(2,1)}, bf16[14,128,128]{2,1,0:T(8,128)(2,1)}, u32[]{:S(2)}, u32[]{:S(2)}) collective-permute-start(bf16[14,128,128]{2,1,0:T(8,128)(2,1)} %design.49), channel_id=1, source_target_pairs={{1,2},{2,1},{5,6},{6,5},{9,10},{10,9},{13,14},{14,13},{17,18},{18,... | collective-permute-start | bytes 1376264 | tf_op jit(solution)/shard_map/ppermute | solution.py:268
  22.5 3.2 %collective-permute-start.112 = (bf16[14,128,128]{2,1,0:T(8,128)(2,1)}, bf16[14,128,128]{2,1,0:T(8,128)(2,1)}, u32[]{:S(2)}, u32[]{:S(2)}) collective-permute-start(bf16[14,128,128]{2,1,0:T(8,128)(2,1)} %design.49), channel_id=1, source_target_pairs={{0,2},{3,1},{4,6},{7,5},{8,10},{11,9},{12,14},{15,13},{16,18},{19,... | collective-permute-start | bytes 1376264 | tf_op jit(solution)/shard_map/ppermute | solution.py:268
  26.7 1.6 %collective-permute-start.106 = (bf16[4,128,128]{2,1,0:T(8,128)(2,1)S(1)}, bf16[4,128,128]{2,1,0:T(8,128)(2,1)S(1)}, u32[]{:S(2)}, u32[]{:S(2)}) collective-permute-start(bf16[4,128,128]{2,1,0:T(8,128)(2,1)S(1)} %add.31), channel_id=1, source_target_pairs={{0,16},{4,20},{8,24},{12,28},{16,0},{20,4},{24,8},{28,12},{1,17},{... | collective-permute-start | bytes 393224 | tf_op jit(solution)/shard_map/ppermute | solution.py:268
  28.3 3.4 %collective-permute-done.106 = bf16[4,128,128]{2,1,0:T(8,128)(2,1)S(1)} collective-permute-done((bf16[4,128,128]{2,1,0:T(8,128)(2,1)S(1)}, bf16[4,128,128]{2,1,0:T(8,128)(2,1)S(1)}, u32[]{:S(2)}, u32[]{:S(2)}) %collective-permute-start.106) | collective-permute-done | bytes 131104 | tf_op jit(solution)/shard_map/ppermute | solution.py:268
  31.7 1.3 %collective-permute-start.107 = (bf16[4,128,128]{2,1,0:T(8,128)(2,1)S(1)}, bf16[4,128,128]{2,1,0:T(8,128)(2,1)S(1)}, u32[]{:S(2)}, u32[]{:S(2)}) collective-permute-start(bf16[4,128,128]{2,1,0:T(8,128)(2,1)S(1)} %add.32), channel_id=1, source_target_pairs={{0,1},{3,2},{4,5},{7,6},{8,9},{11,10},{12,13},{15,14},{16,17},{19,... | collective-permute-start | bytes 393224 | tf_op jit(solution)/shard_map/ppermute | solution.py:268
  34.4 8.6 %collective-permute-done.107 = bf16[4,128,128]{2,1,0:T(8,128)(2,1)S(1)} collective-permute-done((bf16[4,128,128]{2,1,0:T(8,128)(2,1)S(1)}, bf16[4,128,128]{2,1,0:T(8,128)(2,1)S(1)}, u32[]{:S(2)}, u32[]{:S(2)}) %collective-permute-start.107) | collective-permute-done | bytes 131104 | tf_op jit(solution)/shard_map/ppermute | solution.py:268
  42.9 5.4 %collective-permute-start.109 = (bf16[2,128,128]{2,1,0:T(8,128)(2,1)S(1)}, bf16[2,128,128]{2,1,0:T(8,128)(2,1)S(1)}, u32[]{:S(2)}, u32[]{:S(2)}) collective-permute-start(bf16[2,128,128]{2,1,0:T(8,128)(2,1)S(1)} %get-tuple-element.321), channel_id=1, source_target_pairs={{0,2},{3,1},{4,6},{7,5},{8,10},{11,9},{12,14},{15,13},{16,18},{19,... | collective-permute-start | bytes 196616 | tf_op jit(solution)/shard_map/ppermute | solution.py:268
  50.9 1.0 factor.1
  51.9 74.3 %conditional.1 = (f32[89,1,1,128,128]{4,3,2,1,0:T(8,128)}) conditional(s32[]{:T(128)} %bitcast.29, (bf16[512,256]{1,0:T(8,128)(2,1)S(1)}, bf16[14,128,128]{2,1,0:T(8,128)(2,1)}, bf16[14,128,128]{2,1,0:T(8,128)(2,1)}, bf16[14,128,128]{2,1,0:T(8,128)(2,1)}, bf16[14,128,128]{2,1,0:T(8,128)(2,1)}, ...), branch_computations={%region_1.2_spmd, %region_2.3_spmd, %region_3.4_spmd, %region_4.5_... | conditional | bytes 70911072 | solution.py:407
  51.9 2.7 %design.26.refs_0_ = bf16[11,128,128]{2,1,0:T(8,128)(2,1)} custom-call(s32[8,128]{1,0:T(8,128)S(1)} %get-tuple-element.195.listed, bf16[4,89,32,128]{3,2,1,0:T(8,128)(2,1)S(1)} %get-tuple-element.198.legendre, f32[4,128,128]{2,1,0:T(8,128)S(1)} %get-tuple-element.199.table), custom_call_target="tpu_custom_call" | custom-call | tf_op jit(solution)/shard_map/cond/branch_2_fun/design/pallas_call | solution.py:315
  54.6 4.9 %collective-permute-start.6 = (bf16[11,128,128]{2,1,0:T(8,128)(2,1)}, bf16[11,128,128]{2,1,0:T(8,128)(2,1)}, u32[]{:S(2)}, u32[]{:S(2)}) collective-permute-start(bf16[11,128,128]{2,1,0:T(8,128)(2,1)} %design.26.refs_0_), channel_id=1, source_target_pairs={{0,1},{3,2},{4,5},{7,6},{8,9},{11,10},{12,13},{15,14},{16,17},{19,... | collective-permute-start | bytes 1081352 | tf_op jit(solution)/shard_map/cond/branch_2_fun/ppermute | solution.py:268
  59.5 1.4 %collective-permute-start.7 = (bf16[11,128,128]{2,1,0:T(8,128)(2,1)}, bf16[11,128,128]{2,1,0:T(8,128)(2,1)}, u32[]{:S(2)}, u32[]{:S(2)}) collective-permute-start(bf16[11,128,128]{2,1,0:T(8,128)(2,1)} %design.26.refs_0_), channel_id=1, source_target_pairs={{1,2},{2,1},{5,6},{6,5},{9,10},{10,9},{13,14},{14,13},{17,18},{18,... | collective-permute-start | bytes 1081352 | tf_op jit(solution)/shard_map/cond/branch_2_fun/ppermute | solution.py:268
  60.9 3.3 %collective-permute-start.8 = (bf16[11,128,128]{2,1,0:T(8,128)(2,1)}, bf16[11,128,128]{2,1,0:T(8,128)(2,1)}, u32[]{:S(2)}, u32[]{:S(2)}) collective-permute-start(bf16[11,128,128]{2,1,0:T(8,128)(2,1)} %design.26.refs_0_), channel_id=1, source_target_pairs={{0,2},{3,1},{4,6},{7,5},{8,10},{11,9},{12,14},{15,13},{16,18},{19,... | collective-permute-start | bytes 1081352 | tf_op jit(solution)/shard_map/cond/branch_2_fun/ppermute | solution.py:268
  64.2 4.6 %product.37 = (f32[14,128,128]{2,1,0:T(8,128)}, f32[14,128,128]{2,1,0:T(8,128)}) custom-call(bf16[512,256]{1,0:T(8,128)(2,1)S(1)} %get-tuple-element.197.factor, bf16[14,128,128]{2,1,0:T(8,128)(2,1)} %get-tuple-element.205.refs_0_, bf16[14,128,128]{2,1,0:T(8,128)(2,1)} %get-tuple-element.206.refs_1_, bf16[14,128,128]{2,1,0:T(8,128)(2,1)} %get-tuple-element.207.refs_2_, ...), custom_call_target="tpu_custom_call" | custom-call | tf_op jit(solution)/shard_map/cond/branch_2_fun/product/pallas_call | solution.py:368
  68.8 1.3 %collective-permute-start.14 = (f32[14,128,128]{2,1,0:T(8,128)}, f32[14,128,128]{2,1,0:T(8,128)}, u32[]{:S(2)}, u32[]{:S(2)}) collective-permute-start(f32[14,128,128]{2,1,0:T(8,128)} %get-tuple-element.210), channel_id=1, source_target_pairs={{1,0},{2,3},{5,4},{6,7},{9,8},{10,11},{13,12},{14,15},{17,16},{18,... | collective-permute-start | bytes 2752520 | tf_op jit(solution)/shard_map/cond/branch_2_fun/ppermute | solution.py:268
  70.1 2.3 %design.27.refs_0_ = bf16[8,128,128]{2,1,0:T(8,128)(2,1)} custom-call(s32[8,128]{1,0:T(8,128)S(1)} %get-tuple-element.195.listed, bf16[4,89,32,128]{3,2,1,0:T(8,128)(2,1)S(1)} %get-tuple-element.198.legendre, f32[4,128,128]{2,1,0:T(8,128)S(1)} %get-tuple-element.199.table), custom_call_target="tpu_custom_call" | custom-call | tf_op jit(solution)/shard_map/cond/branch_2_fun/design/pallas_call | solution.py:315
  72.4 5.5 %collective-permute-start.10 = (bf16[8,128,128]{2,1,0:T(8,128)(2,1)}, bf16[8,128,128]{2,1,0:T(8,128)(2,1)S(1)}, u32[]{:S(2)}, u32[]{:S(2)}) collective-permute-start(bf16[8,128,128]{2,1,0:T(8,128)(2,1)} %design.27.refs_0_), channel_id=1, source_target_pairs={{0,1},{3,2},{4,5},{7,6},{8,9},{11,10},{12,13},{15,14},{16,17},{19,... | collective-permute-start | bytes 786440 | tf_op jit(solution)/shard_map/cond/branch_2_fun/ppermute | solution.py:268
  78.6 4.0 %collective-permute-start.12 = (bf16[8,128,128]{2,1,0:T(8,128)(2,1)}, bf16[8,128,128]{2,1,0:T(8,128)(2,1)S(1)}, u32[]{:S(2)}, u32[]{:S(2)}) collective-permute-start(bf16[8,128,128]{2,1,0:T(8,128)(2,1)} %design.27.refs_0_), channel_id=1, source_target_pairs={{0,2},{3,1},{4,6},{7,5},{8,10},{11,9},{12,14},{15,13},{16,18},{19,... | collective-permute-start | bytes 786440 | tf_op jit(solution)/shard_map/cond/branch_2_fun/ppermute | solution.py:268
  82.6 4.0 %product.35 = (f32[11,128,128]{2,1,0:T(8,128)}, f32[11,128,128]{2,1,0:T(8,128)}) custom-call(bf16[512,256]{1,0:T(8,128)(2,1)S(1)} %get-tuple-element.197.factor, bf16[11,128,128]{2,1,0:T(8,128)(2,1)} %design.26.refs_0_, bf16[11,128,128]{2,1,0:T(8,128)(2,1)} %collective-permute-done.6.refs_1_, bf16[11,128,128]{2,1,0:T(8,128)(2,1)} %collective-permute-done.7.refs_2_, ...), custom_call_target="tpu_custom_call" | custom-call | tf_op jit(solution)/shard_map/cond/branch_2_fun/product/pallas_call | solution.py:368
  86.6 1.3 %collective-permute-start.9 = (f32[11,128,128]{2,1,0:T(8,128)}, f32[11,128,128]{2,1,0:T(8,128)S(1)}, u32[]{:S(2)}, u32[]{:S(2)}) collective-permute-start(f32[11,128,128]{2,1,0:T(8,128)} %get-tuple-element.201), channel_id=1, source_target_pairs={{1,0},{2,3},{5,4},{6,7},{9,8},{10,11},{13,12},{14,15},{17,16},{18,... | collective-permute-start | bytes 2162696 | tf_op jit(solution)/shard_map/cond/branch_2_fun/ppermute | solution.py:268
  89.4 3.3 %product.36 = (f32[8,128,128]{2,1,0:T(8,128)}, f32[8,128,128]{2,1,0:T(8,128)}) custom-call(bf16[512,256]{1,0:T(8,128)(2,1)S(1)} %get-tuple-element.197.factor, bf16[8,128,128]{2,1,0:T(8,128)(2,1)} %design.27.refs_0_, bf16[8,128,128]{2,1,0:T(8,128)(2,1)} %copy-done.29, bf16[8,128,128]{2,1,0:T(8,128)(2,1)} %copy-done.32, bf16[8,128,128]{2,1,0:T(8,128)(2,1)} %copy-done.33), custom_call_target="tpu_custom_call" | custom-call | tf_op jit(solution)/shard_map/cond/branch_2_fun/product/pallas_call | solution.py:368
  92.8 1.3 %collective-permute-start.13 = (f32[8,128,128]{2,1,0:T(8,128)}, f32[8,128,128]{2,1,0:T(8,128)S(1)}, u32[]{:S(2)}, u32[]{:S(2)}) collective-permute-start(f32[8,128,128]{2,1,0:T(8,128)} %get-tuple-element.204), channel_id=1, source_target_pairs={{1,0},{2,3},{5,4},{6,7},{9,8},{10,11},{13,12},{14,15},{17,16},{18,... | collective-permute-start | bytes 1572872 | tf_op jit(solution)/shard_map/cond/branch_2_fun/ppermute | solution.py:268
  94.0 5.1 %branch_2_fun.1.refs_0_ = f32[89,128,128]{2,1,0:T(8,128)} custom-call(s32[8,128]{1,0:T(8,128)S(1)} %get-tuple-element.195.listed, f32[89,128,128]{2,1,0:T(8,128)} %get-tuple-element.202.resident), custom_call_target="tpu_custom_call" | custom-call | tf_op jit(solution)/shard_map/cond/branch_2_fun/pallas_call | solution.py:357
  99.2 3.9 %update.35.refs_0_ = f32[89,128,128]{2,1,0:T(8,128)} custom-call(s32[8,128]{1,0:T(8,128)S(1)} %get-tuple-element.195.listed, s32[1]{0:T(128)} %get-tuple-element.196.slab_start, f32[14,128,128]{2,1,0:T(8,128)} %get-tuple-element.209.own, f32[14,128,128]{2,1,0:T(8,128)} %collective-permute-done.14.extra, ...), custom_call_target="tpu_custom_call", output_to_operand_aliasing={{}: (5, {})} | custom-call | tf_op jit(solution)/shard_map/cond/branch_2_fun/update/pallas_call | solution.py:378
  103.1 14.1 %collective-permute-done.13.extra = f32[8,128,128]{2,1,0:T(8,128)S(1)} collective-permute-done((f32[8,128,128]{2,1,0:T(8,128)}, f32[8,128,128]{2,1,0:T(8,128)S(1)}, u32[]{:S(2)}, u32[]{:S(2)}) %collective-permute-start.13) | collective-permute-done | bytes 524320 | tf_op jit(solution)/shard_map/cond/branch_2_fun/ppermute | solution.py:268
  118.0 3.4 %update.36.refs_0_ = f32[89,128,128]{2,1,0:T(8,128)} custom-call(s32[8,128]{1,0:T(8,128)S(1)} %get-tuple-element.195.listed, s32[1]{0:T(128)} %get-tuple-element.196.slab_start, f32[8,128,128]{2,1,0:T(8,128)} %get-tuple-element.203.own, f32[8,128,128]{2,1,0:T(8,128)} %copy-done.21, ...), custom_call_target="tpu_custom_call", output_to_operand_aliasing={{}: (5, {})} | custom-call | tf_op jit(solution)/shard_map/cond/branch_2_fun/update/pallas_call | solution.py:378
  122.3 3.6 %update.37 = f32[89,128,128]{2,1,0:T(8,128)} custom-call(s32[8,128]{1,0:T(8,128)S(1)} %get-tuple-element.195.listed, s32[1]{0:T(128)} %get-tuple-element.196.slab_start, f32[11,128,128]{2,1,0:T(8,128)} %get-tuple-element.200.own, f32[11,128,128]{2,1,0:T(8,128)} %copy-done.16, ...), custom_call_target="tpu_custom_call", output_to_operand_aliasing={{}: (5, {})} | custom-call | tf_op jit(solution)/shard_map/cond/branch_2_fun/update/pallas_call | solution.py:378
  (46 shorter events, 13.6 us)
Async XLA Ops:
  0.0 13.7 %copy-start = (bf16[4,32,89,1,128]{4,1,3,2,0:T(8,128)(2,1)S(1)}, bf16[4,32,89,1,128]{4,1,3,2,0:T(8,128)(2,1)}, u32[]{:S(2)}) copy-start(bf16[4,32,89,1,128]{4,1,3,2,0:T(8,128)(2,1)} %param.16) | copy-start | bytes 8749060
  8.2 1.7 %collective-permute-start.104 = (bf16[4,128,128]{2,1,0:T(8,128)(2,1)}, bf16[4,128,128]{2,1,0:T(8,128)(2,1)S(1)}, u32[]{:S(2)}, u32[]{:S(2)}) collective-permute-start(bf16[4,128,128]{2,1,0:T(8,128)(2,1)} %get-tuple-element.317), channel_id=1, source_target_pairs={{0,4},{4,0},{8,12},{12,8},{16,20},{20,16},{24,28},{28,24},{1,5},{5... | collective-permute-start | bytes 393224 | tf_op jit(solution)/shard_map/ppermute | solution.py:268
  10.8 14.9 %collective-permute-start.105 = (bf16[4,128,128]{2,1,0:T(8,128)(2,1)S(1)}, bf16[4,128,128]{2,1,0:T(8,128)(2,1)}, u32[]{:S(2)}, u32[]{:S(2)}) collective-permute-start(bf16[4,128,128]{2,1,0:T(8,128)(2,1)S(1)} %add.30), channel_id=1, source_target_pairs={{0,8},{4,12},{8,0},{12,4},{16,24},{20,28},{24,16},{28,20},{1,9},{5... | collective-permute-start | bytes 393224 | tf_op jit(solution)/shard_map/ppermute | solution.py:268
  16.8 35.1 %collective-permute-start.110 = (bf16[14,128,128]{2,1,0:T(8,128)(2,1)}, bf16[14,128,128]{2,1,0:T(8,128)(2,1)}, u32[]{:S(2)}, u32[]{:S(2)}) collective-permute-start(bf16[14,128,128]{2,1,0:T(8,128)(2,1)} %design.49), channel_id=1, source_target_pairs={{0,1},{3,2},{4,5},{7,6},{8,9},{11,10},{12,13},{15,14},{16,17},{19,... | collective-permute-start | bytes 1376264 | tf_op jit(solution)/shard_map/ppermute | solution.py:268
  21.0 30.8 %collective-permute-start.111 = (bf16[14,128,128]{2,1,0:T(8,128)(2,1)}, bf16[14,128,128]{2,1,0:T(8,128)(2,1)}, u32[]{:S(2)}, u32[]{:S(2)}) collective-permute-start(bf16[14,128,128]{2,1,0:T(8,128)(2,1)} %design.49), channel_id=1, source_target_pairs={{1,2},{2,1},{5,6},{6,5},{9,10},{10,9},{13,14},{14,13},{17,18},{18,... | collective-permute-start | bytes 1376264 | tf_op jit(solution)/shard_map/ppermute | solution.py:268
  22.5 29.4 %collective-permute-start.112 = (bf16[14,128,128]{2,1,0:T(8,128)(2,1)}, bf16[14,128,128]{2,1,0:T(8,128)(2,1)}, u32[]{:S(2)}, u32[]{:S(2)}) collective-permute-start(bf16[14,128,128]{2,1,0:T(8,128)(2,1)} %design.49), channel_id=1, source_target_pairs={{0,2},{3,1},{4,6},{7,5},{8,10},{11,9},{12,14},{15,13},{16,18},{19,... | collective-permute-start | bytes 1376264 | tf_op jit(solution)/shard_map/ppermute | solution.py:268
  26.7 5.0 %collective-permute-start.106 = (bf16[4,128,128]{2,1,0:T(8,128)(2,1)S(1)}, bf16[4,128,128]{2,1,0:T(8,128)(2,1)S(1)}, u32[]{:S(2)}, u32[]{:S(2)}) collective-permute-start(bf16[4,128,128]{2,1,0:T(8,128)(2,1)S(1)} %add.31), channel_id=1, source_target_pairs={{0,16},{4,20},{8,24},{12,28},{16,0},{20,4},{24,8},{28,12},{1,17},{... | collective-permute-start | bytes 393224 | tf_op jit(solution)/shard_map/ppermute | solution.py:268
  31.7 11.2 %collective-permute-start.107 = (bf16[4,128,128]{2,1,0:T(8,128)(2,1)S(1)}, bf16[4,128,128]{2,1,0:T(8,128)(2,1)S(1)}, u32[]{:S(2)}, u32[]{:S(2)}) collective-permute-start(bf16[4,128,128]{2,1,0:T(8,128)(2,1)S(1)} %add.32), channel_id=1, source_target_pairs={{0,1},{3,2},{4,5},{7,6},{8,9},{11,10},{12,13},{15,14},{16,17},{19,... | collective-permute-start | bytes 393224 | tf_op jit(solution)/shard_map/ppermute | solution.py:268
  33.7 15.9 %collective-permute-start.108 = (bf16[2,128,128]{2,1,0:T(8,128)(2,1)S(1)}, bf16[2,128,128]{2,1,0:T(8,128)(2,1)S(1)}, u32[]{:S(2)}, u32[]{:S(2)}) collective-permute-start(bf16[2,128,128]{2,1,0:T(8,128)(2,1)S(1)} %get-tuple-element.321), channel_id=1, source_target_pairs={{1,2},{2,1},{5,6},{6,5},{9,10},{10,9},{13,14},{14,13},{17,18},{18,... | collective-permute-start | bytes 196616 | tf_op jit(solution)/shard_map/ppermute | solution.py:268
  42.9 7.3 %collective-permute-start.109 = (bf16[2,128,128]{2,1,0:T(8,128)(2,1)S(1)}, bf16[2,128,128]{2,1,0:T(8,128)(2,1)S(1)}, u32[]{:S(2)}, u32[]{:S(2)}) collective-permute-start(bf16[2,128,128]{2,1,0:T(8,128)(2,1)S(1)} %get-tuple-element.321), channel_id=1, source_target_pairs={{0,2},{3,1},{4,6},{7,5},{8,10},{11,9},{12,14},{15,13},{16,18},{19,... | collective-permute-start | bytes 196616 | tf_op jit(solution)/shard_map/ppermute | solution.py:268
  49.6 1.2 copy-start.54
  50.2 0.6 copy-start.55
  54.6 23.3 %collective-permute-start.6 = (bf16[11,128,128]{2,1,0:T(8,128)(2,1)}, bf16[11,128,128]{2,1,0:T(8,128)(2,1)}, u32[]{:S(2)}, u32[]{:S(2)}) collective-permute-start(bf16[11,128,128]{2,1,0:T(8,128)(2,1)} %design.26.refs_0_), channel_id=1, source_target_pairs={{0,1},{3,2},{4,5},{7,6},{8,9},{11,10},{12,13},{15,14},{16,17},{19,... | collective-permute-start | bytes 1081352 | tf_op jit(solution)/shard_map/cond/branch_2_fun/ppermute | solution.py:268
  59.5 19.1 %collective-permute-start.7 = (bf16[11,128,128]{2,1,0:T(8,128)(2,1)}, bf16[11,128,128]{2,1,0:T(8,128)(2,1)}, u32[]{:S(2)}, u32[]{:S(2)}) collective-permute-start(bf16[11,128,128]{2,1,0:T(8,128)(2,1)} %design.26.refs_0_), channel_id=1, source_target_pairs={{1,2},{2,1},{5,6},{6,5},{9,10},{10,9},{13,14},{14,13},{17,18},{18,... | collective-permute-start | bytes 1081352 | tf_op jit(solution)/shard_map/cond/branch_2_fun/ppermute | solution.py:268
  60.9 21.7 %collective-permute-start.8 = (bf16[11,128,128]{2,1,0:T(8,128)(2,1)}, bf16[11,128,128]{2,1,0:T(8,128)(2,1)}, u32[]{:S(2)}, u32[]{:S(2)}) collective-permute-start(bf16[11,128,128]{2,1,0:T(8,128)(2,1)} %design.26.refs_0_), channel_id=1, source_target_pairs={{0,2},{3,1},{4,6},{7,5},{8,10},{11,9},{12,14},{15,13},{16,18},{19,... | collective-permute-start | bytes 1081352 | tf_op jit(solution)/shard_map/cond/branch_2_fun/ppermute | solution.py:268
  68.8 30.4 %collective-permute-start.14 = (f32[14,128,128]{2,1,0:T(8,128)}, f32[14,128,128]{2,1,0:T(8,128)}, u32[]{:S(2)}, u32[]{:S(2)}) collective-permute-start(f32[14,128,128]{2,1,0:T(8,128)} %get-tuple-element.210), channel_id=1, source_target_pairs={{1,0},{2,3},{5,4},{6,7},{9,8},{10,11},{13,12},{14,15},{17,16},{18,... | collective-permute-start | bytes 2752520 | tf_op jit(solution)/shard_map/cond/branch_2_fun/ppermute | solution.py:268
  72.4 15.5 %collective-permute-start.10 = (bf16[8,128,128]{2,1,0:T(8,128)(2,1)}, bf16[8,128,128]{2,1,0:T(8,128)(2,1)S(1)}, u32[]{:S(2)}, u32[]{:S(2)}) collective-permute-start(bf16[8,128,128]{2,1,0:T(8,128)(2,1)} %design.27.refs_0_), channel_id=1, source_target_pairs={{0,1},{3,2},{4,5},{7,6},{8,9},{11,10},{12,13},{15,14},{16,17},{19,... | collective-permute-start | bytes 786440 | tf_op jit(solution)/shard_map/cond/branch_2_fun/ppermute | solution.py:268
  77.9 10.0 %collective-permute-start.11 = (bf16[8,128,128]{2,1,0:T(8,128)(2,1)}, bf16[8,128,128]{2,1,0:T(8,128)(2,1)S(1)}, u32[]{:S(2)}, u32[]{:S(2)}) collective-permute-start(bf16[8,128,128]{2,1,0:T(8,128)(2,1)} %design.27.refs_0_), channel_id=1, source_target_pairs={{1,2},{2,1},{5,6},{6,5},{9,10},{10,9},{13,14},{14,13},{17,18},{18,... | collective-permute-start | bytes 786440 | tf_op jit(solution)/shard_map/cond/branch_2_fun/ppermute | solution.py:268
  78.6 9.3 %collective-permute-start.12 = (bf16[8,128,128]{2,1,0:T(8,128)(2,1)}, bf16[8,128,128]{2,1,0:T(8,128)(2,1)S(1)}, u32[]{:S(2)}, u32[]{:S(2)}) collective-permute-start(bf16[8,128,128]{2,1,0:T(8,128)(2,1)} %design.27.refs_0_), channel_id=1, source_target_pairs={{0,2},{3,1},{4,6},{7,5},{8,10},{11,9},{12,14},{15,13},{16,18},{19,... | collective-permute-start | bytes 786440 | tf_op jit(solution)/shard_map/cond/branch_2_fun/ppermute | solution.py:268
  86.6 34.8 %collective-permute-start.9 = (f32[11,128,128]{2,1,0:T(8,128)}, f32[11,128,128]{2,1,0:T(8,128)S(1)}, u32[]{:S(2)}, u32[]{:S(2)}) collective-permute-start(f32[11,128,128]{2,1,0:T(8,128)} %get-tuple-element.201), channel_id=1, source_target_pairs={{1,0},{2,3},{5,4},{6,7},{9,8},{10,11},{13,12},{14,15},{17,16},{18,... | collective-permute-start | bytes 2162696 | tf_op jit(solution)/shard_map/cond/branch_2_fun/ppermute | solution.py:268
  87.9 0.7 copy-start.29
  87.9 0.8 copy-start.32
  88.7 0.7 copy-start.33
  92.8 24.5 %collective-permute-start.13 = (f32[8,128,128]{2,1,0:T(8,128)}, f32[8,128,128]{2,1,0:T(8,128)S(1)}, u32[]{:S(2)}, u32[]{:S(2)}) collective-permute-start(f32[8,128,128]{2,1,0:T(8,128)} %get-tuple-element.204), channel_id=1, source_target_pairs={{1,0},{2,3},{5,4},{6,7},{9,8},{10,11},{13,12},{14,15},{17,16},{18,... | collective-permute-start | bytes 1572872 | tf_op jit(solution)/shard_map/cond/branch_2_fun/ppermute | solution.py:268
  117.2 0.8 copy-start.21
  121.5 0.9 copy-start.16

commit v2 on v1

--- a/solution.py
+++ b/solution.py
@@ -26,23 +26,23 @@
 
 
 def first_counts(slot_count):
-    return max(2, (slot_count * 16) // 100), max(2, (slot_count * 9) // 100)
-
-
-def rest_counts(slot_count):
-    most = slot_count - first_counts(slot_count)[0]
-    counts = [count for count in (0,) + tuple(range(8, most, 11)) if count <= most - 6]
-    return counts + [most]
-
-
-def chunk_sizes(total, second):
-    if total <= second + 1:
-        return [total] if total else []
-    if total <= second + 12:
-        return [second, total - second]
-    left = total - second - 6
-    count = -(-left // 22)
-    return [second] + [left * (k + 1) // count - left * k // count for k in range(count)] + [6]
+    return max(2, (slot_count * 12) // 100), max(2, (slot_count * 14) // 100)
+
+
+def totals_of(slot_count):
+    first, second = first_counts(slot_count)
+    counts = [first] + list(range(first + second, slot_count - 5, 11))
+    return counts + [slot_count]
+
+
+def chunk_sizes(total, first, second):
+    sizes = [first, second][: 1 if total <= first else 2]
+    left = total - sum(sizes)
+    if left <= 12:
+        return sizes + [left] * (left > 0)
+    left -= 6
+    count = -(-left // 21)
+    return sizes + [left * (k + 1) // count - left * k // count for k in range(count)] + [6]
 
 
 def design_tile(tile, slot, legendre, table):
@@ -61,7 +61,7 @@
 
 
 def plan_kernel(
-    counts, first, row_count, slab_start, order, legendre, table, weight,
+    counts, row_count, slab_start, order, legendre, table, weight,
     listed, info, output,
 ):
     lanes = legendre.shape[3]
@@ -79,7 +79,7 @@
     most = jnp.max(jnp.sum(matches, axis=1))
     choice = jnp.int32(0)
     for below in counts[:-1]:
-        choice += jnp.where(most > first + below, 1, 0)
+        choice += jnp.where(most > below, 1, 0)
 
     mine = lax.rem(spot, row_count) == row
     own = jnp.where(needed & mine, 1.0, 0.0)
@@ -136,7 +136,8 @@
     spot = jnp.where(col >= half, 2 * half - 1 - col, col)
     for index, stream in enumerate(streams):
         here = pl.ds(index * rows, rows)
-        output[here, :lanes] = stream[spot]
+        kept = (spot > 0) | (index == 0)
+        output[here, :lanes] = jnp.where(kept, stream[spot], jnp.zeros_like(stream[0]))
         if 1 <= index <= inner:
             output[here, lanes:] = jnp.zeros_like(stream[0])
         else:
@@ -263,15 +264,17 @@
     middles = [mirrored([(half - 1 - t, half)]) for t in range(half)]
     outward = mirrored([(i, i - 1) for i in range(2, half)])
     last_hop = mirrored([(1, 0)])
+    filler = last_hop if half == 2 else []
 
     def shift(value, pairs, axis="col"):
         return lax.ppermute(value, axis, pairs)
 
-    def streams_of(whole_item, near, far):
+    def streams_of(whole_item, near, far, idle=False):
+        more = filler if idle else []
         ins = []
         for _ in range(inner):
-            ins.append(shift(ins[-1] if ins else whole_item, inward))
-        mids = [shift(far(whole_item), pairs) for pairs in middles]
+            ins.append(shift(ins[-1] if ins else whole_item, inward + more))
+        mids = [shift(far(whole_item), pairs + more * (t > 0)) for t, pairs in enumerate(middles)]
         froms = []
         for t in range(col_count - 2):
             piece = mids[t] if t < half else None
@@ -299,7 +302,7 @@
     values = legendre.transpose(0, 2, 3, 1, 4).reshape(block_count, slot_count, shard_rows, lanes)
     old = resident.reshape(slot_count, lanes, lanes)
     first, second = first_counts(slot_count)
-    counts = rest_counts(slot_count)
+    counts = totals_of(slot_count)
     tile_shape = (own_rows, lanes)
 
     def tiles_of(size):
@@ -321,7 +324,7 @@
         )(listed, values, table)
 
     listed, info, both = pl.pallas_call(
-        functools.partial(plan_kernel, counts, first, row_count),
+        functools.partial(plan_kernel, counts, row_count),
         out_shape=[
             jax.ShapeDtypeStruct((8, -(-slot_count // 128) * 128), jnp.int32),
             jax.ShapeDtypeStruct((1, 128), jnp.int32),
@@ -332,23 +335,14 @@
         name="plan",
     )(slab_start, tile_order, values, table, weights)
 
-    own_first = design(0, first, listed, values, table)
-    nears, froms = streams_of(own_first, same, same)
-    streams_first = nears + froms
-    bit = 1
-    while bit < row_count:
-        pairs = [(r, r ^ bit) for r in range(row_count)]
-        both = both + shift(both, pairs, "row")
-        bit *= 2
-    nears, froms = streams_of(both, lambda x: x[:half], lambda x: x[half:])
-    factors = nears + froms
-    factor = pl.pallas_call(
-        functools.partial(factor_kernel, inner, half),
-        out_shape=jax.ShapeDtypeStruct((len(factors) * own_rows, 2 * lanes), bf16),
-        in_specs=[vmem] * len(factors),
-        out_specs=vmem,
-        name="factor",
-    )(*factors)
+    def collect(factors):
+        return pl.pallas_call(
+            functools.partial(factor_kernel, inner, half),
+            out_shape=jax.ShapeDtypeStruct((len(factors) * own_rows, 2 * lanes), bf16),
+            in_specs=[vmem] * len(factors),
+            out_specs=vmem,
+            name="factor",
+        )(*factors)
 
     def copy_rest(offset, listed, old):
         size = slot_count - offset
@@ -386,15 +380,20 @@
         )(listed, slab_start, own, extra, old, *previous)
 
     def branch(total):
-        def run(factor, streams_first, listed, slab_start, old, values, table):
-            output = copy_rest(first + total, listed, old)
+        def run(both, listed, slab_start, old, values, table):
+            bit = 1
+            while bit < row_count:
+                pairs = [(r, r ^ bit) for r in range(row_count)]
+                both = both + shift(both, pairs, "row")
+                bit *= 2
+            nears, froms = streams_of(both, lambda x: x[:half], lambda x: x[half:], True)
+            factor = collect(nears + froms)
+            output = copy_rest(total, listed, old)
             waiting, offset = [], 0
-            for k, size in enumerate([first] + chunk_sizes(total, second)):
-                streams = streams_first
-                if k > 0:
-                    piece = design(offset, size, listed, values, table)
-                    nears, froms = streams_of(piece, same, same)
-                    streams = nears + froms
+            for k, size in enumerate(chunk_sizes(total, first, second)):
+                piece = design(offset, size, listed, values, table)
+                nears, froms = streams_of(piece, same, same, k == 0)
+                streams = nears + froms
                 own, end = multiply(factor, streams)
                 waiting.append((k, offset, own, shift(end, last_hop)))
                 offset += size
@@ -407,7 +406,7 @@
     output = lax.switch(
         info[0, 0],
         [branch(total) for total in counts],
-        factor, streams_first, listed, slab_start, old, values, table,
+        both, listed, slab_start, old, values, table,
     )
     return output.reshape(resident.shape)
 

time: 127 us -> 141 us (1.11)
  waiting for transfers between devices: 28 us -> 36.3 us
  Pallas kernels: 40.4 us -> 43.9 us
  starting transfers between devices: 44.8 us -> 47 us
  other arithmetic: 4.48 us -> 2.51 us
    ppermute x18, waiting for transfers between devices: 28 us -> 36.3 us  [shift(): return lax.ppermute(value, axis, pairs)]
    pallas_call x3, Pallas kernels: 8.06 us -> 10.8 us  [design(): pl.pallas_call(functools.partial(design_kernel, offset), out_shape=tiles_...]
    ppermute x18, starting transfers between devices: 44.8 us -> 47 us  [shift(): return lax.ppermute(value, axis, pairs)]
    add x3, other arithmetic: 1.94 us -> 0.12 us  [run(): both = both + shift(both, pairs, 'row')]
    cond x10 -> x18, local copies, waits for them, and re-layouts: 3.15 us -> 4.19 us
  transfers between devices with their start and end apart: 18 -> 18, of which waited for: 5 -> 3; matrix products, arithmetic and copies ran while one was open for 2% -> 2% of each run, Pallas kernels for 24% -> 27%
where the time goes in v2:
time: 141 us; the launch traced here: 140 us
  starting transfers between devices  47 us (33%)
  Pallas kernels  43.9 us (31%)
  waiting for transfers between devices  36.3 us (26%)
  local copies, waits for them, and re-layouts  7.91 us (6%)
  other arithmetic  2.51 us (2%)
  between operations  1.49 us (1%)
    ppermute x18, starting transfers between devices, shift(): return lax.ppermute(value, axis, pairs)  47 us
    ppermute x18, waiting for transfers between devices, shift(): return lax.ppermute(value, axis, pairs)  36.3 us
    pallas_call x3, Pallas kernels, multiply(): pl.pallas_call(product_kernel, out_shape=[product, product], in_specs=[vm...  12.3 us
    pallas_call x3, Pallas kernels, update(): pl.pallas_call(functools.partial(update_kernel, offset), in_specs=[smem]...  10.9 us
    pallas_call x3, Pallas kernels, design(): pl.pallas_call(functools.partial(design_kernel, offset), out_shape=tiles_...  10.8 us
    pallas_call x1, Pallas kernels, copy_rest(): pl.pallas_call(functools.partial(copy_kernel, offset), in_specs=[smem, an...  5.14 us
    cond x18, local copies, waits for them, and re-layouts  4.19 us
    pallas_call x1, Pallas kernels, per_device(): pl.pallas_call(functools.partial(plan_kernel, counts, row_count), out_sha...  3.12 us
  transfers between devices with their start and end apart: 18, of which 3 were waited for; matrix products, arithmetic and copies ran while one was open for 2% of the time, Pallas kernels for 27%

profile of v2, /device:TPU:0, one launch (start us, length us, event | category | flops | bytes accessed | tf_op | source)
XLA Modules:
  0.0 139.9 jit_solution(12064992707311659528)
XLA Ops:
  2.3 0.9 multiply_cosine_fusion.table
  4.7 3.1 %plan.1 = (s32[8,128]{1,0:T(8,128)S(1)}, s32[1,128]{1,0:T(1,128)}, bf16[4,128,128]{2,1,0:T(8,128)(2,1)S(1)}) custom-call(s32[1]{0:T(128)S(6)} %copy.99.slab_start, s32[712]{0:T(1024)} %order.1, bf16[4,89,32,128]{3,2,1,0:T(8,128)(2,1)} %bitcast.51, f32[4,128,128]{2,1,0:T(8,128)S(1)} %multiply_cosine_fusion.table, f32[128,128]{1,0:T(8,128)} %broadcast_in_dim.25.weight), custom_call_target="tpu_custom_call" | custom-call | tf_op jit(solution)/shard_map/plan/pallas_call | solution.py:326
  8.4 131.3 %conditional.1 = (f32[89,1,1,128,128]{4,3,2,1,0:T(8,128)}) conditional(s32[]{:T(128)} %bitcast.29, (bf16[4,128,128]{2,1,0:T(8,128)(2,1)S(1)}, s32[8,128]{1,0:T(8,128)S(1)}, bf16[4,89,32,128]{3,2,1,0:T(8,128)(2,1)}, f32[4,128,128]{2,1,0:T(8,128)S(1)}, f32[89,128,128]{2,1,0:T(8,128)}, /*index=5*/s32[1]{0:T(128)}) %tuple.80, ...), branch_computations={%region_1.2_spmd, %region_2.3_spmd, %region_3.4_spmd, %region_4.5_... | conditional | flops 196608 | bytes 92800520 | solution.py:406
  9.0 4.3 %design.36.refs_0_ = bf16[12,128,128]{2,1,0:T(8,128)(2,1)} custom-call(s32[8,128]{1,0:T(8,128)S(1)} %get-tuple-element.129.listed, bf16[4,89,32,128]{3,2,1,0:T(8,128)(2,1)} %get-tuple-element.132.legendre, f32[4,128,128]{2,1,0:T(8,128)S(1)} %get-tuple-element.133.table), custom_call_target="tpu_custom_call" | custom-call | tf_op jit(solution)/shard_map/cond/branch_2_fun/design/pallas_call | solution.py:318
  13.4 5.1 %collective-permute-start.34 = (bf16[12,128,128]{2,1,0:T(8,128)(2,1)}, bf16[12,128,128]{2,1,0:T(8,128)(2,1)}, u32[]{:S(2)}, u32[]{:S(2)}) collective-permute-start(bf16[12,128,128]{2,1,0:T(8,128)(2,1)} %design.36.refs_0_), channel_id=1, source_target_pairs={{0,1},{3,2},{4,5},{7,6},{8,9},{11,10},{12,13},{15,14},{16,17},{19,... | collective-permute-start | bytes 1179656 | tf_op jit(solution)/shard_map/cond/branch_2_fun/ppermute | solution.py:270
  18.5 3.9 %design.35.refs_0_ = bf16[11,128,128]{2,1,0:T(8,128)(2,1)} custom-call(s32[8,128]{1,0:T(8,128)S(1)} %get-tuple-element.129.listed, bf16[4,89,32,128]{3,2,1,0:T(8,128)(2,1)} %get-tuple-element.132.legendre, f32[4,128,128]{2,1,0:T(8,128)S(1)} %get-tuple-element.133.table), custom_call_target="tpu_custom_call" | custom-call | tf_op jit(solution)/shard_map/cond/branch_2_fun/design/pallas_call | solution.py:318
  22.4 1.3 collective-permute-start.30
  23.8 1.6 %collective-permute-start.25 = (bf16[4,128,128]{2,1,0:T(8,128)(2,1)S(1)}, bf16[4,128,128]{2,1,0:T(8,128)(2,1)S(1)}, u32[]{:S(2)}, u32[]{:S(2)}) collective-permute-start(bf16[4,128,128]{2,1,0:T(8,128)(2,1)S(1)} %add.71), channel_id=1, source_target_pairs={{0,8},{4,12},{8,0},{12,4},{16,24},{20,28},{24,16},{28,20},{1,9},{5... | collective-permute-start | bytes 393224 | tf_op jit(solution)/shard_map/cond/branch_2_fun/ppermute | solution.py:270
  25.3 1.4 %collective-permute-start.35 = (bf16[12,128,128]{2,1,0:T(8,128)(2,1)}, bf16[12,128,128]{2,1,0:T(8,128)(2,1)}, u32[]{:S(2)}, u32[]{:S(2)}) collective-permute-start(bf16[12,128,128]{2,1,0:T(8,128)(2,1)} %design.36.refs_0_), channel_id=1, source_target_pairs={{1,2},{2,1},{5,6},{6,5},{9,10},{10,9},{13,14},{14,13},{17,18},{18,... | collective-permute-start | bytes 1179656 | tf_op jit(solution)/shard_map/cond/branch_2_fun/ppermute | solution.py:270
  26.7 3.2 %collective-permute-start.36 = (bf16[12,128,128]{2,1,0:T(8,128)(2,1)}, bf16[12,128,128]{2,1,0:T(8,128)(2,1)}, u32[]{:S(2)}, u32[]{:S(2)}) collective-permute-start(bf16[12,128,128]{2,1,0:T(8,128)(2,1)} %design.36.refs_0_), channel_id=1, source_target_pairs={{0,2},{3,1},{4,6},{7,5},{8,10},{11,9},{12,14},{15,13},{16,18},{19,... | collective-permute-start | bytes 1179656 | tf_op jit(solution)/shard_map/cond/branch_2_fun/ppermute | solution.py:270
  30.0 1.6 %collective-permute-start.26 = (bf16[4,128,128]{2,1,0:T(8,128)(2,1)S(1)}, bf16[4,128,128]{2,1,0:T(8,128)(2,1)S(1)}, u32[]{:S(2)}, u32[]{:S(2)}) collective-permute-start(bf16[4,128,128]{2,1,0:T(8,128)(2,1)S(1)} %add.72), channel_id=1, source_target_pairs={{0,16},{4,20},{8,24},{12,28},{16,0},{20,4},{24,8},{28,12},{1,17},{... | collective-permute-start | bytes 393224 | tf_op jit(solution)/shard_map/cond/branch_2_fun/ppermute | solution.py:270
  31.6 3.5 %collective-permute-done.26 = bf16[4,128,128]{2,1,0:T(8,128)(2,1)S(1)} collective-permute-done((bf16[4,128,128]{2,1,0:T(8,128)(2,1)S(1)}, bf16[4,128,128]{2,1,0:T(8,128)(2,1)S(1)}, u32[]{:S(2)}, u32[]{:S(2)}) %collective-permute-start.26) | collective-permute-done | bytes 131104 | tf_op jit(solution)/shard_map/cond/branch_2_fun/ppermute | solution.py:270
  35.1 1.4 %collective-permute-start.31 = (bf16[11,128,128]{2,1,0:T(8,128)(2,1)}, bf16[11,128,128]{2,1,0:T(8,128)(2,1)}, u32[]{:S(2)}, u32[]{:S(2)}) collective-permute-start(bf16[11,128,128]{2,1,0:T(8,128)(2,1)} %design.35.refs_0_), channel_id=1, source_target_pairs={{1,2},{2,1},{5,6},{6,5},{9,10},{10,9},{13,14},{14,13},{17,18},{18,... | collective-permute-start | bytes 1081352 | tf_op jit(solution)/shard_map/cond/branch_2_fun/ppermute | solution.py:270
  36.6 4.7 %collective-permute-start.32 = (bf16[11,128,128]{2,1,0:T(8,128)(2,1)}, bf16[11,128,128]{2,1,0:T(8,128)(2,1)}, u32[]{:S(2)}, u32[]{:S(2)}) collective-permute-start(bf16[11,128,128]{2,1,0:T(8,128)(2,1)} %design.35.refs_0_), channel_id=1, source_target_pairs={{0,2},{3,1},{4,6},{7,5},{8,10},{11,9},{12,14},{15,13},{16,18},{19,... | collective-permute-start | bytes 1081352 | tf_op jit(solution)/shard_map/cond/branch_2_fun/ppermute | solution.py:270
  42.6 1.1 collective-permute-done.36.refs_3_
  43.7 13.2 %collective-permute-start.29 = (bf16[2,128,128]{2,1,0:T(8,128)(2,1)S(1)}, bf16[2,128,128]{2,1,0:T(8,128)(2,1)}, u32[]{:S(2)}, u32[]{:S(2)}) collective-permute-start(bf16[2,128,128]{2,1,0:T(8,128)(2,1)S(1)} %get-tuple-element.235), channel_id=1, source_target_pairs={{0,2},{3,1},{1,0},{2,3},{4,6},{7,5},{5,4},{6,7},{8,10},{11,9},{9,8... | collective-permute-start | bytes 196616 | tf_op jit(solution)/shard_map/cond/branch_2_fun/ppermute | solution.py:270
  56.9 2.5 %design.37.refs_0_ = bf16[10,128,128]{2,1,0:T(8,128)(2,1)} custom-call(s32[8,128]{1,0:T(8,128)S(1)} %get-tuple-element.129.listed, bf16[4,89,32,128]{3,2,1,0:T(8,128)(2,1)S(1)} %copy-done.1, f32[4,128,128]{2,1,0:T(8,128)S(1)} %get-tuple-element.133.table), custom_call_target="tpu_custom_call" | custom-call | tf_op jit(solution)/shard_map/cond/branch_2_fun/design/pallas_call | solution.py:318
  59.4 5.1 %collective-permute-start.38 = (bf16[10,128,128]{2,1,0:T(8,128)(2,1)}, bf16[10,128,128]{2,1,0:T(8,128)(2,1)S(1)}, u32[]{:S(2)}, u32[]{:S(2)}) collective-permute-start(bf16[10,128,128]{2,1,0:T(8,128)(2,1)} %design.37.refs_0_), channel_id=1, source_target_pairs={{0,1},{3,2},{1,0},{2,3},{4,5},{7,6},{5,4},{6,7},{8,9},{11,10},{9,8... | collective-permute-start | bytes 983048 | tf_op jit(solution)/shard_map/cond/branch_2_fun/ppermute | solution.py:270
  65.2 2.8 %collective-permute-start.40 = (bf16[10,128,128]{2,1,0:T(8,128)(2,1)}, bf16[10,128,128]{2,1,0:T(8,128)(2,1)S(1)}, u32[]{:S(2)}, u32[]{:S(2)}) collective-permute-start(bf16[10,128,128]{2,1,0:T(8,128)(2,1)} %design.37.refs_0_), channel_id=1, source_target_pairs={{0,2},{3,1},{1,0},{2,3},{4,6},{7,5},{5,4},{6,7},{8,10},{11,9},{9,8... | collective-permute-start | bytes 983048 | tf_op jit(solution)/shard_map/cond/branch_2_fun/ppermute | solution.py:270
  67.9 1.5 %slice.91.refs_1_ = bf16[2,128,128]{2,1,0:T(8,128)(2,1)} slice(bf16[4,128,128]{2,1,0:T(8,128)(2,1)} %collective-permute-done.27), slice={[0:2], [0:128], [0:128]} | slice | bytes 131072 | tf_op jit(solution)/shard_map/cond/branch_2_fun/slice | solution.py:389
  69.4 1.7 %factor.10 = bf16[512,256]{1,0:T(8,128)(2,1)} custom-call(bf16[2,128,128]{2,1,0:T(8,128)(2,1)} %get-tuple-element.236.refs_0_, bf16[2,128,128]{2,1,0:T(8,128)(2,1)} %slice.91.refs_1_, bf16[2,128,128]{2,1,0:T(8,128)(2,1)} %copy-done.73, bf16[2,128,128]{2,1,0:T(8,128)(2,1)} %collective-permute-done.29.refs_3_), custom_call_target="tpu_custom_call" | custom-call | tf_op jit(solution)/shard_map/cond/branch_2_fun/factor/pallas_call | solution.py:339
  71.1 4.3 %product.36 = (f32[12,128,128]{2,1,0:T(8,128)}, f32[12,128,128]{2,1,0:T(8,128)}) custom-call(bf16[512,256]{1,0:T(8,128)(2,1)} %factor.10, bf16[12,128,128]{2,1,0:T(8,128)(2,1)} %design.36.refs_0_, bf16[12,128,128]{2,1,0:T(8,128)(2,1)} %collective-permute-done.34.refs_1_, bf16[12,128,128]{2,1,0:T(8,128)(2,1)} %collective-permute-done.35.refs_2_, ...), custom_call_target="tpu_custom_call" | custom-call | tf_op jit(solution)/shard_map/cond/branch_2_fun/product/pallas_call | solution.py:362
  75.4 1.3 collective-permute-start.37
  76.7 4.1 %product.35 = (f32[11,128,128]{2,1,0:T(8,128)}, f32[11,128,128]{2,1,0:T(8,128)}) custom-call(bf16[512,256]{1,0:T(8,128)(2,1)} %factor.10, bf16[11,128,128]{2,1,0:T(8,128)(2,1)} %design.35.refs_0_, bf16[11,128,128]{2,1,0:T(8,128)(2,1)} %copy-done.39, bf16[11,128,128]{2,1,0:T(8,128)(2,1)} %collective-permute-done.31.refs_2_, ...), custom_call_target="tpu_custom_call" | custom-call | tf_op jit(solution)/shard_map/cond/branch_2_fun/product/pallas_call | solution.py:362
  80.8 1.3 collective-permute-start.33
  83.6 3.9 %product.37 = (f32[10,128,128]{2,1,0:T(8,128)}, f32[10,128,128]{2,1,0:T(8,128)}) custom-call(bf16[512,256]{1,0:T(8,128)(2,1)} %factor.10, bf16[10,128,128]{2,1,0:T(8,128)(2,1)} %design.37.refs_0_, bf16[10,128,128]{2,1,0:T(8,128)(2,1)} %copy-done.41, bf16[10,128,128]{2,1,0:T(8,128)(2,1)} %copy-done.44, bf16[10,128,128]{2,1,0:T(8,128)(2,1)} %copy-done.48), custom_call_target="tpu_custom_call" | custom-call | tf_op jit(solution)/shard_map/cond/branch_2_fun/product/pallas_call | solution.py:362
  87.5 1.3 collective-permute-start.41
  88.8 5.1 %branch_2_fun.1.refs_0_ = f32[89,128,128]{2,1,0:T(8,128)} custom-call(s32[8,128]{1,0:T(8,128)S(1)} %get-tuple-element.129.listed, f32[89,128,128]{2,1,0:T(8,128)} %get-tuple-element.136.resident), custom_call_target="tpu_custom_call" | custom-call | tf_op jit(solution)/shard_map/cond/branch_2_fun/pallas_call | solution.py:351
  93.9 31.7 %collective-permute-done.41.extra = f32[10,128,128]{2,1,0:T(8,128)S(1)} collective-permute-done((f32[10,128,128]{2,1,0:T(8,128)}, f32[10,128,128]{2,1,0:T(8,128)S(1)}, u32[]{:S(2)}, u32[]{:S(2)}) %collective-permute-start.41) | collective-permute-done | bytes 655392 | tf_op jit(solution)/shard_map/cond/branch_2_fun/ppermute | solution.py:270
  126.5 3.6 %update.35.refs_0_ = f32[89,128,128]{2,1,0:T(8,128)} custom-call(s32[8,128]{1,0:T(8,128)S(1)} %get-tuple-element.129.listed, s32[1]{0:T(128)} %get-tuple-element.130.slab_start, f32[10,128,128]{2,1,0:T(8,128)} %get-tuple-element.139.own, f32[10,128,128]{2,1,0:T(8,128)} %copy-done.26, ...), custom_call_target="tpu_custom_call", output_to_operand_aliasing={{}: (5, {})} | custom-call | tf_op jit(solution)/shard_map/cond/branch_2_fun/update/pallas_call | solution.py:372
  131.0 3.7 %update.36.refs_0_ = f32[89,128,128]{2,1,0:T(8,128)} custom-call(s32[8,128]{1,0:T(8,128)S(1)} %get-tuple-element.129.listed, s32[1]{0:T(128)} %get-tuple-element.130.slab_start, f32[12,128,128]{2,1,0:T(8,128)} %get-tuple-element.137.own, f32[12,128,128]{2,1,0:T(8,128)} %copy-done.15, ...), custom_call_target="tpu_custom_call", output_to_operand_aliasing={{}: (5, {})} | custom-call | tf_op jit(solution)/shard_map/cond/branch_2_fun/update/pallas_call | solution.py:372
  135.6 3.6 %update.37 = f32[89,128,128]{2,1,0:T(8,128)} custom-call(s32[8,128]{1,0:T(8,128)S(1)} %get-tuple-element.129.listed, s32[1]{0:T(128)} %get-tuple-element.130.slab_start, f32[11,128,128]{2,1,0:T(8,128)} %get-tuple-element.134.own, f32[11,128,128]{2,1,0:T(8,128)} %copy-done.20, ...), custom_call_target="tpu_custom_call", output_to_operand_aliasing={{}: (5, {})} | custom-call | tf_op jit(solution)/shard_map/cond/branch_2_fun/update/pallas_call | solution.py:372
  (48 shorter events, 10.0 us)
Async XLA Ops:
  8.5 48.4 %copy-start.1 = (bf16[4,89,32,128]{3,2,1,0:T(8,128)(2,1)S(1)}, bf16[4,89,32,128]{3,2,1,0:T(8,128)(2,1)}, u32[]{:S(2)}) copy-start(bf16[4,89,32,128]{3,2,1,0:T(8,128)(2,1)} %get-tuple-element.132.legendre) | copy-start | bytes 8749060 | tf_op jit(solution)/shard_map/cond
  8.5 15.2 %collective-permute-start.24 = (bf16[4,128,128]{2,1,0:T(8,128)(2,1)S(1)}, bf16[4,128,128]{2,1,0:T(8,128)(2,1)S(1)}, u32[]{:S(2)}, u32[]{:S(2)}) collective-permute-start(bf16[4,128,128]{2,1,0:T(8,128)(2,1)S(1)} %get-tuple-element.131), channel_id=1, source_target_pairs={{0,4},{4,0},{8,12},{12,8},{16,20},{20,16},{24,28},{28,24},{1,5},{5... | collective-permute-start | bytes 393224 | tf_op jit(solution)/shard_map/cond/branch_2_fun/ppermute | solution.py:270
  13.4 27.9 %collective-permute-start.34 = (bf16[12,128,128]{2,1,0:T(8,128)(2,1)}, bf16[12,128,128]{2,1,0:T(8,128)(2,1)}, u32[]{:S(2)}, u32[]{:S(2)}) collective-permute-start(bf16[12,128,128]{2,1,0:T(8,128)(2,1)} %design.36.refs_0_), channel_id=1, source_target_pairs={{0,1},{3,2},{4,5},{7,6},{8,9},{11,10},{12,13},{15,14},{16,17},{19,... | collective-permute-start | bytes 1179656 | tf_op jit(solution)/shard_map/cond/branch_2_fun/ppermute | solution.py:270
  22.4 14.2 %collective-permute-start.30 = (bf16[11,128,128]{2,1,0:T(8,128)(2,1)}, bf16[11,128,128]{2,1,0:T(8,128)(2,1)S(1)}, u32[]{:S(2)}, u32[]{:S(2)}) collective-permute-start(bf16[11,128,128]{2,1,0:T(8,128)(2,1)} %design.35.refs_0_), channel_id=1, source_target_pairs={{0,1},{3,2},{4,5},{7,6},{8,9},{11,10},{12,13},{15,14},{16,17},{19,... | collective-permute-start | bytes 1081352 | tf_op jit(solution)/shard_map/cond/branch_2_fun/ppermute | solution.py:270
  23.8 6.2 %collective-permute-start.25 = (bf16[4,128,128]{2,1,0:T(8,128)(2,1)S(1)}, bf16[4,128,128]{2,1,0:T(8,128)(2,1)S(1)}, u32[]{:S(2)}, u32[]{:S(2)}) collective-permute-start(bf16[4,128,128]{2,1,0:T(8,128)(2,1)S(1)} %add.71), channel_id=1, source_target_pairs={{0,8},{4,12},{8,0},{12,4},{16,24},{20,28},{24,16},{28,20},{1,9},{5... | collective-permute-start | bytes 393224 | tf_op jit(solution)/shard_map/cond/branch_2_fun/ppermute | solution.py:270
  25.3 16.6 %collective-permute-start.35 = (bf16[12,128,128]{2,1,0:T(8,128)(2,1)}, bf16[12,128,128]{2,1,0:T(8,128)(2,1)}, u32[]{:S(2)}, u32[]{:S(2)}) collective-permute-start(bf16[12,128,128]{2,1,0:T(8,128)(2,1)} %design.36.refs_0_), channel_id=1, source_target_pairs={{1,2},{2,1},{5,6},{6,5},{9,10},{10,9},{13,14},{14,13},{17,18},{18,... | collective-permute-start | bytes 1179656 | tf_op jit(solution)/shard_map/cond/branch_2_fun/ppermute | solution.py:270
  26.7 17.0 %collective-permute-start.36 = (bf16[12,128,128]{2,1,0:T(8,128)(2,1)}, bf16[12,128,128]{2,1,0:T(8,128)(2,1)}, u32[]{:S(2)}, u32[]{:S(2)}) collective-permute-start(bf16[12,128,128]{2,1,0:T(8,128)(2,1)} %design.36.refs_0_), channel_id=1, source_target_pairs={{0,2},{3,1},{4,6},{7,5},{8,10},{11,9},{12,14},{15,13},{16,18},{19,... | collective-permute-start | bytes 1179656 | tf_op jit(solution)/shard_map/cond/branch_2_fun/ppermute | solution.py:270
  30.0 5.1 %collective-permute-start.26 = (bf16[4,128,128]{2,1,0:T(8,128)(2,1)S(1)}, bf16[4,128,128]{2,1,0:T(8,128)(2,1)S(1)}, u32[]{:S(2)}, u32[]{:S(2)}) collective-permute-start(bf16[4,128,128]{2,1,0:T(8,128)(2,1)S(1)} %add.72), channel_id=1, source_target_pairs={{0,16},{4,20},{8,24},{12,28},{16,0},{20,4},{24,8},{28,12},{1,17},{... | collective-permute-start | bytes 393224 | tf_op jit(solution)/shard_map/cond/branch_2_fun/ppermute | solution.py:270
  35.1 40.3 %collective-permute-start.31 = (bf16[11,128,128]{2,1,0:T(8,128)(2,1)}, bf16[11,128,128]{2,1,0:T(8,128)(2,1)}, u32[]{:S(2)}, u32[]{:S(2)}) collective-permute-start(bf16[11,128,128]{2,1,0:T(8,128)(2,1)} %design.35.refs_0_), channel_id=1, source_target_pairs={{1,2},{2,1},{5,6},{6,5},{9,10},{10,9},{13,14},{14,13},{17,18},{18,... | collective-permute-start | bytes 1081352 | tf_op jit(solution)/shard_map/cond/branch_2_fun/ppermute | solution.py:270
  36.6 5.4 %copy-start.39 = (bf16[11,128,128]{2,1,0:T(8,128)(2,1)}, bf16[11,128,128]{2,1,0:T(8,128)(2,1)S(1)}, u32[]{:S(2)}) copy-start(bf16[11,128,128]{2,1,0:T(8,128)(2,1)S(1)} %collective-permute-done.30.refs_1_) | copy-start | bytes 1081348 | tf_op jit(solution)/shard_map/cond
  36.6 40.1 %collective-permute-start.32 = (bf16[11,128,128]{2,1,0:T(8,128)(2,1)}, bf16[11,128,128]{2,1,0:T(8,128)(2,1)}, u32[]{:S(2)}, u32[]{:S(2)}) collective-permute-start(bf16[11,128,128]{2,1,0:T(8,128)(2,1)} %design.35.refs_0_), channel_id=1, source_target_pairs={{0,2},{3,1},{4,6},{7,5},{8,10},{11,9},{12,14},{15,13},{16,18},{19,... | collective-permute-start | bytes 1081352 | tf_op jit(solution)/shard_map/cond/branch_2_fun/ppermute | solution.py:270
  41.3 23.9 %collective-permute-start.27 = (bf16[4,128,128]{2,1,0:T(8,128)(2,1)S(1)}, bf16[4,128,128]{2,1,0:T(8,128)(2,1)}, u32[]{:S(2)}, u32[]{:S(2)}) collective-permute-start(bf16[4,128,128]{2,1,0:T(8,128)(2,1)S(1)} %add.73), channel_id=1, source_target_pairs={{0,1},{3,2},{1,0},{2,3},{4,5},{7,6},{5,4},{6,7},{8,9},{11,10},{9,8... | collective-permute-start | bytes 393224 | tf_op jit(solution)/shard_map/cond/branch_2_fun/ppermute | solution.py:270
  41.9 17.5 %collective-permute-start.28 = (bf16[2,128,128]{2,1,0:T(8,128)(2,1)S(1)}, bf16[2,128,128]{2,1,0:T(8,128)(2,1)S(1)}, u32[]{:S(2)}, u32[]{:S(2)}) collective-permute-start(bf16[2,128,128]{2,1,0:T(8,128)(2,1)S(1)} %get-tuple-element.235), channel_id=1, source_target_pairs={{1,2},{2,1},{5,6},{6,5},{9,10},{10,9},{13,14},{14,13},{17,18},{18,... | collective-permute-start | bytes 196616 | tf_op jit(solution)/shard_map/cond/branch_2_fun/ppermute | solution.py:270
  43.7 20.8 %collective-permute-start.29 = (bf16[2,128,128]{2,1,0:T(8,128)(2,1)S(1)}, bf16[2,128,128]{2,1,0:T(8,128)(2,1)}, u32[]{:S(2)}, u32[]{:S(2)}) collective-permute-start(bf16[2,128,128]{2,1,0:T(8,128)(2,1)S(1)} %get-tuple-element.235), channel_id=1, source_target_pairs={{0,2},{3,1},{1,0},{2,3},{4,6},{7,5},{5,4},{6,7},{8,10},{11,9},{9,8... | collective-permute-start | bytes 196616 | tf_op jit(solution)/shard_map/cond/branch_2_fun/ppermute | solution.py:270
  59.4 10.0 %copy-start.73 = (bf16[2,128,128]{2,1,0:T(8,128)(2,1)}, bf16[2,128,128]{2,1,0:T(8,128)(2,1)S(1)}, u32[]{:S(2)}) copy-start(bf16[2,128,128]{2,1,0:T(8,128)(2,1)S(1)} %collective-permute-done.28.refs_2_) | copy-start | bytes 196612 | tf_op jit(solution)/shard_map/cond
  59.4 22.6 %collective-permute-start.38 = (bf16[10,128,128]{2,1,0:T(8,128)(2,1)}, bf16[10,128,128]{2,1,0:T(8,128)(2,1)S(1)}, u32[]{:S(2)}, u32[]{:S(2)}) collective-permute-start(bf16[10,128,128]{2,1,0:T(8,128)(2,1)} %design.37.refs_0_), channel_id=1, source_target_pairs={{0,1},{3,2},{1,0},{2,3},{4,5},{7,6},{5,4},{6,7},{8,9},{11,10},{9,8... | collective-permute-start | bytes 983048 | tf_op jit(solution)/shard_map/cond/branch_2_fun/ppermute | solution.py:270
  64.5 17.6 %collective-permute-start.39 = (bf16[10,128,128]{2,1,0:T(8,128)(2,1)}, bf16[10,128,128]{2,1,0:T(8,128)(2,1)S(1)}, u32[]{:S(2)}, u32[]{:S(2)}) collective-permute-start(bf16[10,128,128]{2,1,0:T(8,128)(2,1)} %design.37.refs_0_), channel_id=1, source_target_pairs={{1,2},{2,1},{5,6},{6,5},{9,10},{10,9},{13,14},{14,13},{17,18},{18,... | collective-permute-start | bytes 983048 | tf_op jit(solution)/shard_map/cond/branch_2_fun/ppermute | solution.py:270
  65.2 16.9 %collective-permute-start.40 = (bf16[10,128,128]{2,1,0:T(8,128)(2,1)}, bf16[10,128,128]{2,1,0:T(8,128)(2,1)S(1)}, u32[]{:S(2)}, u32[]{:S(2)}) collective-permute-start(bf16[10,128,128]{2,1,0:T(8,128)(2,1)} %design.37.refs_0_), channel_id=1, source_target_pairs={{0,2},{3,1},{1,0},{2,3},{4,6},{7,5},{5,4},{6,7},{8,10},{11,9},{9,8... | collective-permute-start | bytes 983048 | tf_op jit(solution)/shard_map/cond/branch_2_fun/ppermute | solution.py:270
  75.4 54.7 %collective-permute-start.37 = (f32[12,128,128]{2,1,0:T(8,128)}, f32[12,128,128]{2,1,0:T(8,128)S(1)}, u32[]{:S(2)}, u32[]{:S(2)}) collective-permute-start(f32[12,128,128]{2,1,0:T(8,128)} %get-tuple-element.138), channel_id=1, source_target_pairs={{1,0},{2,3},{5,4},{6,7},{9,8},{10,11},{13,12},{14,15},{17,16},{18,... | collective-permute-start | bytes 2359304 | tf_op jit(solution)/shard_map/cond/branch_2_fun/ppermute | solution.py:270
  80.8 54.0 %collective-permute-start.33 = (f32[11,128,128]{2,1,0:T(8,128)}, f32[11,128,128]{2,1,0:T(8,128)S(1)}, u32[]{:S(2)}, u32[]{:S(2)}) collective-permute-start(f32[11,128,128]{2,1,0:T(8,128)} %get-tuple-element.135), channel_id=1, source_target_pairs={{1,0},{2,3},{5,4},{6,7},{9,8},{10,11},{13,12},{14,15},{17,16},{18,... | collective-permute-start | bytes 2162696 | tf_op jit(solution)/shard_map/cond/branch_2_fun/ppermute | solution.py:270
  82.1 0.7 copy-start.41
  82.1 0.8 copy-start.44
  82.9 0.7 copy-start.48
  87.5 38.1 %collective-permute-start.41 = (f32[10,128,128]{2,1,0:T(8,128)}, f32[10,128,128]{2,1,0:T(8,128)S(1)}, u32[]{:S(2)}, u32[]{:S(2)}) collective-permute-start(f32[10,128,128]{2,1,0:T(8,128)} %get-tuple-element.140), channel_id=1, source_target_pairs={{1,0},{2,3},{5,4},{6,7},{9,8},{10,11},{13,12},{14,15},{17,16},{18,... | collective-permute-start | bytes 1966088 | tf_op jit(solution)/shard_map/cond/branch_2_fun/ppermute | solution.py:270
  125.6 0.9 copy-start.26
  130.1 0.9 copy-start.15
  134.7 0.9 copy-start.20

commit v3 on v2

--- a/solution.py
+++ b/solution.py
@@ -18,31 +18,18 @@
     return pl.BlockSpec(memory_space=space)
 
 
-def lookup_weights(obs_weight, span_weight, span_of):
-    group_count = span_weight.shape[0]
-    matches = span_of[:, None] == jnp.arange(group_count, dtype=jnp.int32)[None, :]
-    factor = jnp.sum(jnp.where(matches, span_weight[None, :], 0.0), axis=1)
-    return obs_weight * factor * (0.25 / math.sqrt(obs_weight.shape[0]))
-
-
-def first_counts(slot_count):
-    return max(2, (slot_count * 12) // 100), max(2, (slot_count * 14) // 100)
-
-
 def totals_of(slot_count):
-    first, second = first_counts(slot_count)
-    counts = [first] + list(range(first + second, slot_count - 5, 11))
-    return counts + [slot_count]
-
-
-def chunk_sizes(total, first, second):
-    sizes = [first, second][: 1 if total <= first else 2]
-    left = total - sum(sizes)
-    if left <= 12:
-        return sizes + [left] * (left > 0)
-    left -= 6
-    count = -(-left // 21)
-    return sizes + [left * (k + 1) // count - left * k // count for k in range(count)] + [6]
+    counts = [9, 19, 29] + list(range(40, slot_count - 4, 12))
+    return [count for count in counts if count < slot_count] + [slot_count]
+
+
+def chunk_sizes(total):
+    count = max(1, -(-(total - 2) // 13))
+    less = max(1, (total - 4 * (count // 2)) // count)
+    sizes = [less + 4 * (k % 2) if count > 1 else total for k in range(count)]
+    for k in (list(range(1, count, 2)) + list(range(0, count, 2)))[: total - sum(sizes)]:
+        sizes[k] += 1
+    return sizes
 
 
 def design_tile(tile, slot, legendre, table):
@@ -61,7 +48,7 @@
 
 
 def plan_kernel(
-    counts, row_count, slab_start, order, legendre, table, weight,
+    counts, row_count, slab_start, span_weight, order, obs_weight, span_of, legendre, table,
     listed, info, output,
 ):
     lanes = legendre.shape[3]
@@ -108,13 +95,30 @@
     col_count = output.shape[0]
     half = col_count // 2
     is_right = col >= half
+    observations = obs_weight.shape[0]
+    blocks, _, shard_rows, _ = legendre.shape
+    span = span_of[...].reshape(1, observations)
+    factor = jnp.zeros(span.shape, jnp.float32)
+    for group in range(span_weight.shape[0]):
+        factor += jnp.where(span == group, span_weight[group], 0.0)
+    weights = obs_weight[...].reshape(1, observations) * factor
+    weights *= 0.25 / math.sqrt(observations)
+    shape = (blocks * shard_rows, observations)
+    mine = lax.broadcasted_iota(jnp.int32, shape, 0)
+    mine = mine // shard_rows * (shard_rows * col_count) + lax.rem(mine, shard_rows)
+    mine = mine + col * shard_rows == lax.broadcasted_iota(jnp.int32, shape, 1)
+    weight = lax.dot_general(
+        jnp.where(mine, 1.0, 0.0), jnp.broadcast_to(weights, (lanes, observations)),
+        (((1,), (1,)), ((), ())),
+        precision=lax.Precision.HIGHEST, preferred_element_type=jnp.float32,
+    )
     for place in range(col_count):
         near_left = place if place < half else col_count - 1 - (place - half)
         near_right = col_count - 1 - near_left
         tile = start + jnp.where(is_right, near_right, near_left)
         position = jnp.sum(jnp.where(tiles == tile, spot, 0))
         column = design_tile(tile, position // row_count, legendre, table)
-        column = weight[...] * column.astype(jnp.float32)
+        column = weight * column.astype(jnp.float32)
         column = jnp.where(lax.rem(position, row_count) == row, column, 0.0)
         output[place] = column.astype(jnp.bfloat16)
 
@@ -150,10 +154,12 @@
     )
 
 
-def product_kernel(factor, *refs):
-    streams, own, end = refs[:-2], refs[-2], refs[-1]
+def product_kernel(count, factor, *refs):
+    streams, following, (own, *ends) = refs[:count], refs[count:-3], refs[-3:]
     lanes = own.shape[1]
     size = own.shape[0]
+    col = lax.axis_index("col")
+    is_end = (col == 0) | (col == lax.axis_size("col") - 1)
 
     def piece(first, width):
         both = lax.dot_general(
@@ -162,7 +168,10 @@
         )
         for k in range(width):
             own[first + k] = both[k * lanes : (k + 1) * lanes, :lanes]
-            end[first + k] = both[k * lanes : (k + 1) * lanes, lanes:]
+            end = both[k * lanes : (k + 1) * lanes, lanes:]
+            high = end.astype(jnp.bfloat16)
+            ends[0][first + k] = high
+            ends[1][first + k] = (end - high.astype(jnp.float32)).astype(jnp.bfloat16)
 
     def step(index, carry):
         piece(2 * index, 2)
@@ -171,6 +180,11 @@
     lax.fori_loop(0, size // 2, step, 0)
     if size % 2:
         piece(size - 1, 1)
+    for later in following:
+        @pl.when(is_end)
+        def _(later=later):
+            ends[0][: later.shape[0]] = later[...]
+            ends[1][: later.shape[0]] = later[...]
 
 
 def copy_kernel(offset, listed, resident, output, held, ins, outs):
@@ -199,14 +213,19 @@
 
 
 def update_kernel(
-    offset, listed, slab_start, own, extra, resident, *refs,
+    offset, listed, slab_start, own, high, low, resident, *refs,
 ):
-    output, own_held, extra_held, old, new, ins, outs, more = refs[-8:]
+    output, own_held, high_held, low_held, old, new, ins, outs, more = refs[-9:]
     size = old.shape[0]
     lanes = old.shape[1]
-    column = slab_start[0] + lax.axis_index("col")
-    own_copy = pltpu.make_async_copy(own, own_held, more.at[0])
-    extra_copy = pltpu.make_async_copy(extra, extra_held, more.at[1])
+    col = lax.axis_index("col")
+    column = slab_start[0] + col
+    is_end = (col == 0) | (col == lax.axis_size("col") - 1)
+    copies = [
+        pltpu.make_async_copy(own, own_held, more.at[0]),
+        pltpu.make_async_copy(high.at[pl.ds(0, size)], high_held, more.at[1]),
+        pltpu.make_async_copy(low.at[pl.ds(0, size)], low_held, more.at[2]),
+    ]
 
     def fetch(index):
         return pltpu.make_async_copy(
@@ -218,22 +237,23 @@
             new.at[index], output.at[listed[0, offset + index]], outs.at[index]
         )
 
-    own_copy.start()
-    extra_copy.start()
+    for copy in copies:
+        copy.start()
 
     @pl.loop(0, size)
     def _(index):
         fetch(index).start()
 
-    own_copy.wait()
-    extra_copy.wait()
+    for copy in copies:
+        copy.wait()
 
     @pl.loop(0, size)
     def _(index):
         fetch(index).wait()
         tile = listed[1, offset + index]
         keep = (tile >= column) & (tile * lanes < UNK)
-        change = own_held[index] + extra_held[index]
+        extra = high_held[index].astype(jnp.float32) + low_held[index].astype(jnp.float32)
+        change = own_held[index] + jnp.where(is_end, extra, 0.0)
         new[index] = old[index] + jnp.where(keep, change, 0.0)
         store(index).start()
 
@@ -283,7 +303,7 @@
                 moved = shift(moved, outward)
                 piece = moved if piece is None else piece + moved
             froms.append(piece)
-        return [near(item) for item in [whole_item] + ins], froms
+        return [whole_item] + ins, froms
 
     def same(item):
         return item
@@ -292,8 +312,6 @@
         values = values.reshape(block_count, block_rows)
         return lax.dynamic_slice_in_dim(values, col_index * shard_rows, shard_rows, 1)
 
-    weights = own_part(lookup_weights(obs_weight, span_weight, span_of))
-    weights = jnp.broadcast_to(weights.reshape(own_rows, 1), (own_rows, lanes))
     pages = PERIOD // lanes + 2
     lane_orders = jnp.arange(pages * lanes, dtype=jnp.int32) % PERIOD
     lane_orders = lane_orders.astype(jnp.float32).reshape(pages, 1, lanes)
@@ -301,7 +319,6 @@
 
     values = legendre.transpose(0, 2, 3, 1, 4).reshape(block_count, slot_count, shard_rows, lanes)
     old = resident.reshape(slot_count, lanes, lanes)
-    first, second = first_counts(slot_count)
     counts = totals_of(slot_count)
     tile_shape = (own_rows, lanes)
 
@@ -330,10 +347,10 @@
             jax.ShapeDtypeStruct((1, 128), jnp.int32),
             tiles_of(col_count),
         ],
-        in_specs=[smem] + [vmem] * 4,
+        in_specs=[smem] * 2 + [vmem] * 5,
         out_specs=[vmem] * 3,
         name="plan",
-    )(slab_start, tile_order, values, table, weights)
+    )(slab_start, span_weight, tile_order, obs_weight, span_of, values, table)
 
     def collect(factors):
         return pl.pallas_call(
@@ -357,29 +374,40 @@
         )(listed, old)
         return [output]
 
-    def multiply(factor, streams):
-        product = jax.ShapeDtypeStruct((streams[0].shape[0], lanes, lanes), jnp.float32)
+    def multiply(factor, streams, size, following):
+        width = max([size] + [item.shape[0] for item in following])
         return pl.pallas_call(
-            product_kernel,
-            out_shape=[product, product],
-            in_specs=[vmem] * (1 + len(streams)),
-            out_specs=[vmem] * 2,
+            functools.partial(product_kernel, len(streams)),
+            out_shape=[
+                jax.ShapeDtypeStruct((size, lanes, lanes), jnp.float32),
+                jax.ShapeDtypeStruct((width, lanes, lanes), bf16),
+                jax.ShapeDtypeStruct((width, lanes, lanes), bf16),
+            ],
+            in_specs=[vmem] * (1 + len(streams) + len(following)),
+            out_specs=[vmem] * 3,
             name="product",
-        )(factor, *streams)
-
-    def update(offset, listed, slab_start, own, extra, old, previous):
+        )(factor, *streams, *following)
+
+    def update(offset, listed, slab_start, own, high, low, old, previous):
         size = own.shape[0]
+        part = pltpu.VMEM((size, lanes, lanes), bf16)
         return pl.pallas_call(
             functools.partial(update_kernel, offset),
-            in_specs=[smem] * 2 + [anywhere] * (3 + len(previous)),
+            in_specs=[smem] * 2 + [anywhere] * (4 + len(previous)),
             out_specs=anywhere,
             out_shape=jax.ShapeDtypeStruct(old.shape, old.dtype),
-            scratch_shapes=[held(size)] * 4 + [sems(size), sems(size), sems(2)],
-            input_output_aliases={5: 0} if previous else {},
+            scratch_shapes=[
+                held(size), part, part, held(size), held(size),
+                sems(size), sems(size), sems(3),
+            ],
+            input_output_aliases={6: 0} if previous else {},
             name="update",
-        )(listed, slab_start, own, extra, old, *previous)
+        )(listed, slab_start, own, high, low, old, *previous)
 
     def branch(total):
+        sizes = chunk_sizes(total)
+        riding = half == 2 and own_rows == lanes
+
         def run(both, listed, slab_start, old, values, table):
             bit = 1
             while bit < row_count:
@@ -388,17 +416,29 @@
                 bit *= 2
             nears, froms = streams_of(both, lambda x: x[:half], lambda x: x[half:], True)
             factor = collect(nears + froms)
+            offsets = [sum(sizes[:k]) for k in range(len(sizes))]
+            designs = [
+                design(offset, size, listed, values, table)
+                for offset, size in zip(offsets, sizes)
+            ]
+            done = []
+            for k, size in enumerate(sizes):
+                if k < 2 or not riding:
+                    nears, froms = streams_of(designs[k], same, same, k == 0)
+                    streams = nears + froms
+                else:
+                    passed = shift(designs[k], middles[0])
+                    near_end, far_end = done[k - 2][1:]
+                    streams = [designs[k], near_end, passed, far_end]
+                following = designs[k + 2 : k + 3] if riding else []
+                own, high, low = multiply(factor, streams, size, following)
+                more = [inward, middles[1]] if riding else [[], []]
+                high = shift(high, last_hop + more[0])
+                low = shift(low, last_hop + more[1])
+                done.append((own, high, low))
             output = copy_rest(total, listed, old)
-            waiting, offset = [], 0
-            for k, size in enumerate(chunk_sizes(total, first, second)):
-                piece = design(offset, size, listed, values, table)
-                nears, froms = streams_of(piece, same, same, k == 0)
-                streams = nears + froms
-                own, end = multiply(factor, streams)
-                waiting.append((k, offset, own, shift(end, last_hop)))
-                offset += size
-            for k, offset, own, extra in waiting:
-                output = [update(offset, listed, slab_start, own, extra, old, output)]
+            for k, (own, high, low) in enumerate(done):
+                output = [update(offsets[k], listed, slab_start, own, high, low, old, output)]
             return output[0]
 
         return run

time: 141 us -> 119 us (0.84)
  waiting for transfers between devices: 36.3 us -> 13.4 us
  starting transfers between devices: 47 us -> 55 us
  local copies, waits for them, and re-layouts: 7.91 us -> 3.78 us
  Pallas kernels: 43.9 us -> 41.4 us
    ppermute x18 -> x19, waiting for transfers between devices: 36.3 us -> 13.4 us  [shift(): return lax.ppermute(value, axis, pairs)]
    ppermute x18 -> x19, starting transfers between devices: 47 us -> 55 us  [shift(): return lax.ppermute(value, axis, pairs)]
    pallas_call x3, Pallas kernels: 10.8 us -> 8.78 us  [design(): pl.pallas_call(functools.partial(design_kernel, offset), out_shape=tiles_...]
    cond x18 -> x26, local copies, waits for them, and re-layouts: 4.19 us -> 2.26 us
    add x3, other arithmetic: 0.12 us -> 1.95 us  [run(): both = both + shift(both, pairs, 'row')]
    slice x1 -> x0, local copies, waits for them, and re-layouts: 1.45 us -> none  [run(): x[:half]]
  transfers between devices with their start and end apart: 18 -> 19, of which waited for: 3 -> 6; matrix products, arithmetic and copies ran while one was open for 2% -> 2% of each run, Pallas kernels for 27% -> 29%
where the time goes in v3:
time: 119 us; the launch traced here: 118 us
  starting transfers between devices  55 us (46%)
  Pallas kernels  41.4 us (35%)
  waiting for transfers between devices  13.4 us (11%)
  local copies, waits for them, and re-layouts  3.78 us (3%)
  other arithmetic  2.87 us (2%)
  between operations  1.33 us (1%)
    ppermute x19, starting transfers between devices, shift(): return lax.ppermute(value, axis, pairs)  55 us
    ppermute x19, waiting for transfers between devices, shift(): return lax.ppermute(value, axis, pairs)  13.4 us
    pallas_call x3, Pallas kernels, multiply(): pl.pallas_call(functools.partial(product_kernel, len(streams)), out_shape...  11.6 us
    pallas_call x3, Pallas kernels, update(): pl.pallas_call(functools.partial(update_kernel, offset), in_specs=[smem]...  10.6 us
    pallas_call x3, Pallas kernels, design(): pl.pallas_call(functools.partial(design_kernel, offset), out_shape=tiles_...  8.78 us
    pallas_call x1, Pallas kernels, copy_rest(): pl.pallas_call(functools.partial(copy_kernel, offset), in_specs=[smem, an...  5.48 us
    pallas_call x1, Pallas kernels, per_device(): pl.pallas_call(functools.partial(plan_kernel, counts, row_count), out_sha...  3.2 us
  transfers between devices with their start and end apart: 19, of which 6 were waited for; matrix products, arithmetic and copies ran while one was open for 2% of the time, Pallas kernels for 29%

profile of v3, /device:TPU:0, one launch (start us, length us, event | category | flops | bytes accessed | tf_op | source)
XLA Modules:
  0.0 118.5 jit_solution(5939903370603032115)
XLA Ops:
  2.4 3.2 %plan.1 = (s32[8,128]{1,0:T(8,128)S(1)}, s32[1,128]{1,0:T(1,128)}, bf16[4,128,128]{2,1,0:T(8,128)(2,1)S(1)}) custom-call(s32[1]{0:T(128)S(6)} %copy.95.slab_start, f32[8]{0:T(128)} %span_weight.1, s32[712]{0:T(1024)} %order.1, f32[512]{0:T(512)} %obs_weight.1, s32[512]{0:T(512)} %span_of.1, bf16[4,89,32,128]{3,2,1,0:T(8,128)(2,1)} %bitcast.50, ...), custom_call_target="tpu_custom_call" | custom-call | tf_op jit(solution)/shard_map/plan/pallas_call | solution.py:343
  6.3 111.5 %conditional.1 = (f32[89,1,1,128,128]{4,3,2,1,0:T(8,128)}) conditional(s32[]{:T(128)} %bitcast.28, (bf16[4,128,128]{2,1,0:T(8,128)(2,1)S(1)}, s32[8,128]{1,0:T(8,128)S(1)}, bf16[4,89,32,128]{3,2,1,0:T(8,128)(2,1)}, f32[4,128,128]{2,1,0:T(8,128)S(1)}, f32[89,128,128]{2,1,0:T(8,128)}, /*index=5*/s32[1]{0:T(128)}) %tuple.71, ...), branch_computations={%region_0.1_spmd, %region_1.2_spmd, %region_2.3_spmd, %region_3.4_... | conditional | flops 196608 | bytes 69862928 | solution.py:446
  6.9 1.0 collective-permute-done.27
  7.9 2.9 %collective-permute-start.28 = (bf16[4,128,128]{2,1,0:T(8,128)(2,1)S(1)}, bf16[4,128,128]{2,1,0:T(8,128)(2,1)S(1)}, u32[]{:S(2)}, u32[]{:S(2)}) collective-permute-start(bf16[4,128,128]{2,1,0:T(8,128)(2,1)S(1)} %add.70), channel_id=1, source_target_pairs={{0,8},{4,12},{8,0},{12,4},{16,24},{20,28},{24,16},{28,20},{1,9},{5... | collective-permute-start | bytes 393224 | tf_op jit(solution)/shard_map/cond/branch_2_fun/ppermute | solution.py:290
  10.8 3.5 %design.35.refs_0_ = bf16[8,128,128]{2,1,0:T(8,128)(2,1)} custom-call(s32[8,128]{1,0:T(8,128)S(1)} %get-tuple-element.132.listed, bf16[4,89,32,128]{3,2,1,0:T(8,128)(2,1)} %get-tuple-element.135.legendre, f32[4,128,128]{2,1,0:T(8,128)S(1)} %get-tuple-element.136.table), custom_call_target="tpu_custom_call" | custom-call | tf_op jit(solution)/shard_map/cond/branch_2_fun/design/pallas_call | solution.py:335
  14.4 1.6 %collective-permute-start.33 = (bf16[8,128,128]{2,1,0:T(8,128)(2,1)}, bf16[8,128,128]{2,1,0:T(8,128)(2,1)}, u32[]{:S(2)}, u32[]{:S(2)}) collective-permute-start(bf16[8,128,128]{2,1,0:T(8,128)(2,1)} %design.35.refs_0_), channel_id=1, source_target_pairs={{0,1},{3,2},{1,0},{2,3},{4,5},{7,6},{5,4},{6,7},{8,9},{11,10},{9,8... | collective-permute-start | bytes 786440 | tf_op jit(solution)/shard_map/cond/branch_2_fun/ppermute | solution.py:290
  15.9 1.0 add.71
  16.9 1.6 %collective-permute-start.29 = (bf16[4,128,128]{2,1,0:T(8,128)(2,1)S(1)}, bf16[4,128,128]{2,1,0:T(8,128)(2,1)}, u32[]{:S(2)}, u32[]{:S(2)}) collective-permute-start(bf16[4,128,128]{2,1,0:T(8,128)(2,1)S(1)} %add.71), channel_id=1, source_target_pairs={{0,16},{4,20},{8,24},{12,28},{16,0},{20,4},{24,8},{28,12},{1,17},{... | collective-permute-start | bytes 393224 | tf_op jit(solution)/shard_map/cond/branch_2_fun/ppermute | solution.py:290
  18.5 3.0 %design.36.refs_0_ = bf16[13,128,128]{2,1,0:T(8,128)(2,1)} custom-call(s32[8,128]{1,0:T(8,128)S(1)} %get-tuple-element.132.listed, bf16[4,89,32,128]{3,2,1,0:T(8,128)(2,1)S(1)} %copy-done.3, f32[4,128,128]{2,1,0:T(8,128)S(1)} %get-tuple-element.136.table), custom_call_target="tpu_custom_call" | custom-call | tf_op jit(solution)/shard_map/cond/branch_2_fun/design/pallas_call | solution.py:335
  21.4 3.2 %collective-permute-start.41 = (bf16[13,128,128]{2,1,0:T(8,128)(2,1)}, bf16[13,128,128]{2,1,0:T(8,128)(2,1)}, u32[]{:S(2)}, u32[]{:S(2)}) collective-permute-start(bf16[13,128,128]{2,1,0:T(8,128)(2,1)} %design.36.refs_0_), channel_id=1, source_target_pairs={{0,1},{3,2},{4,5},{7,6},{8,9},{11,10},{12,13},{15,14},{16,17},{19,... | collective-permute-start | bytes 1277960 | tf_op jit(solution)/shard_map/cond/branch_2_fun/ppermute | solution.py:290
  26.4 5.4 %collective-permute-start.32 = (bf16[2,128,128]{2,1,0:T(8,128)(2,1)S(1)}, bf16[2,128,128]{2,1,0:T(8,128)(2,1)S(1)}, u32[]{:S(2)}, u32[]{:S(2)}) collective-permute-start(bf16[2,128,128]{2,1,0:T(8,128)(2,1)S(1)} %slice.38), channel_id=1, source_target_pairs={{0,2},{3,1},{1,0},{2,3},{4,6},{7,5},{5,4},{6,7},{8,10},{11,9},{9,8... | collective-permute-start | bytes 196616 | tf_op jit(solution)/shard_map/cond/branch_2_fun/ppermute | solution.py:290
  31.7 1.4 %collective-permute-start.42 = (bf16[13,128,128]{2,1,0:T(8,128)(2,1)}, bf16[13,128,128]{2,1,0:T(8,128)(2,1)}, u32[]{:S(2)}, u32[]{:S(2)}) collective-permute-start(bf16[13,128,128]{2,1,0:T(8,128)(2,1)} %design.36.refs_0_), channel_id=1, source_target_pairs={{1,2},{2,1},{5,6},{6,5},{9,10},{10,9},{13,14},{14,13},{17,18},{18,... | collective-permute-start | bytes 1277960 | tf_op jit(solution)/shard_map/cond/branch_2_fun/ppermute | solution.py:290
  33.2 6.1 %collective-permute-start.43 = (bf16[13,128,128]{2,1,0:T(8,128)(2,1)}, bf16[13,128,128]{2,1,0:T(8,128)(2,1)}, u32[]{:S(2)}, u32[]{:S(2)}) collective-permute-start(bf16[13,128,128]{2,1,0:T(8,128)(2,1)} %design.36.refs_0_), channel_id=1, source_target_pairs={{0,2},{3,1},{4,6},{7,5},{8,10},{11,9},{12,14},{15,13},{16,18},{19,... | collective-permute-start | bytes 1277960 | tf_op jit(solution)/shard_map/cond/branch_2_fun/ppermute | solution.py:290
  39.3 1.4 %collective-permute-start.34 = (bf16[8,128,128]{2,1,0:T(8,128)(2,1)}, bf16[8,128,128]{2,1,0:T(8,128)(2,1)}, u32[]{:S(2)}, u32[]{:S(2)}) collective-permute-start(bf16[8,128,128]{2,1,0:T(8,128)(2,1)} %design.35.refs_0_), channel_id=1, source_target_pairs={{1,2},{2,1},{5,6},{6,5},{9,10},{10,9},{13,14},{14,13},{17,18},{18,... | collective-permute-start | bytes 786440 | tf_op jit(solution)/shard_map/cond/branch_2_fun/ppermute | solution.py:290
  40.7 5.9 %collective-permute-start.35 = (bf16[8,128,128]{2,1,0:T(8,128)(2,1)}, bf16[8,128,128]{2,1,0:T(8,128)(2,1)}, u32[]{:S(2)}, u32[]{:S(2)}) collective-permute-start(bf16[8,128,128]{2,1,0:T(8,128)(2,1)} %design.35.refs_0_), channel_id=1, source_target_pairs={{0,2},{3,1},{1,0},{2,3},{4,6},{7,5},{5,4},{6,7},{8,10},{11,9},{9,8... | collective-permute-start | bytes 786440 | tf_op jit(solution)/shard_map/cond/branch_2_fun/ppermute | solution.py:290
  46.6 2.3 %design.34.refs_4_.refs_0_ = bf16[8,128,128]{2,1,0:T(8,128)(2,1)} custom-call(s32[8,128]{1,0:T(8,128)S(1)} %get-tuple-element.132.listed, bf16[4,89,32,128]{3,2,1,0:T(8,128)(2,1)S(1)} %copy-done.3, f32[4,128,128]{2,1,0:T(8,128)S(1)} %get-tuple-element.136.table), custom_call_target="tpu_custom_call" | custom-call | tf_op jit(solution)/shard_map/cond/branch_2_fun/design/pallas_call | solution.py:335
  48.9 1.8 %factor.10 = bf16[512,256]{1,0:T(8,128)(2,1)} custom-call(bf16[4,128,128]{2,1,0:T(8,128)(2,1)} %copy-done.23, bf16[4,128,128]{2,1,0:T(8,128)(2,1)} %copy-done.72, bf16[2,128,128]{2,1,0:T(8,128)(2,1)} %copy-done.83, bf16[2,128,128]{2,1,0:T(8,128)(2,1)} %copy-done.85), custom_call_target="tpu_custom_call" | custom-call | tf_op jit(solution)/shard_map/cond/branch_2_fun/factor/pallas_call | solution.py:356
  51.6 3.6 %product.34 = (f32[8,128,128]{2,1,0:T(8,128)}, bf16[8,128,128]{2,1,0:T(8,128)(2,1)}, bf16[8,128,128]{2,1,0:T(8,128)(2,1)}) custom-call(bf16[512,256]{1,0:T(8,128)(2,1)} %factor.10, bf16[8,128,128]{2,1,0:T(8,128)(2,1)} %design.35.refs_0_, bf16[8,128,128]{2,1,0:T(8,128)(2,1)} %collective-permute-done.33.refs_1_, ...), custom_call_target="tpu_custom_call" | custom-call | tf_op jit(solution)/shard_map/cond/branch_2_fun/product/pallas_call | solution.py:379
  55.2 17.7 %collective-permute-start.36 = (bf16[8,128,128]{2,1,0:T(8,128)(2,1)}, bf16[8,128,128]{2,1,0:T(8,128)(2,1)S(1)}, u32[]{:S(2)}, u32[]{:S(2)}) collective-permute-start(bf16[8,128,128]{2,1,0:T(8,128)(2,1)} %get-tuple-element.137), channel_id=1, source_target_pairs={{1,0},{2,3},{0,1},{3,2},{5,4},{6,7},{4,5},{7,6},{9,8},{10,11},{8,9... | collective-permute-start | bytes 786440 | tf_op jit(solution)/shard_map/cond/branch_2_fun/ppermute | solution.py:290
  73.4 4.7 %product.36 = (f32[13,128,128]{2,1,0:T(8,128)}, bf16[13,128,128]{2,1,0:T(8,128)(2,1)}, bf16[13,128,128]{2,1,0:T(8,128)(2,1)}) custom-call(bf16[512,256]{1,0:T(8,128)(2,1)} %factor.10, bf16[13,128,128]{2,1,0:T(8,128)(2,1)} %design.36.refs_0_, bf16[13,128,128]{2,1,0:T(8,128)(2,1)} %collective-permute-done.41.refs_1_, ...), custom_call_target="tpu_custom_call" | custom-call | tf_op jit(solution)/shard_map/cond/branch_2_fun/product/pallas_call | solution.py:379
  78.1 1.5 %collective-permute-start.44 = (bf16[13,128,128]{2,1,0:T(8,128)(2,1)}, bf16[13,128,128]{2,1,0:T(8,128)(2,1)S(1)}, u32[]{:S(2)}, u32[]{:S(2)}) collective-permute-start(bf16[13,128,128]{2,1,0:T(8,128)(2,1)} %get-tuple-element.144), channel_id=1, source_target_pairs={{1,0},{2,3},{0,1},{3,2},{5,4},{6,7},{4,5},{7,6},{9,8},{10,11},{8,9... | collective-permute-start | bytes 1277960 | tf_op jit(solution)/shard_map/cond/branch_2_fun/ppermute | solution.py:290
  79.6 1.0 collective-permute-start.45
  80.5 5.3 %collective-permute-done.38.refs_3_.low = bf16[8,128,128]{2,1,0:T(8,128)(2,1)S(1)} collective-permute-done((bf16[8,128,128]{2,1,0:T(8,128)(2,1)}, bf16[8,128,128]{2,1,0:T(8,128)(2,1)S(1)}, u32[]{:S(2)}, u32[]{:S(2)}) %collective-permute-start.38) | collective-permute-done | bytes 262176 | tf_op jit(solution)/shard_map/cond/branch_2_fun/ppermute | solution.py:290
  86.6 3.4 %product.35 = (f32[8,128,128]{2,1,0:T(8,128)}, bf16[8,128,128]{2,1,0:T(8,128)(2,1)}, bf16[8,128,128]{2,1,0:T(8,128)(2,1)}) custom-call(bf16[512,256]{1,0:T(8,128)(2,1)} %factor.10, bf16[8,128,128]{2,1,0:T(8,128)(2,1)} %design.34.refs_4_.refs_0_, bf16[8,128,128]{2,1,0:T(8,128)(2,1)} %copy-done.19, bf16[8,128,128]{2,1,0:T(8,128)(2,1)} %copy-done.66, ...), custom_call_target="tpu_custom_call" | custom-call | tf_op jit(solution)/shard_map/cond/branch_2_fun/product/pallas_call | solution.py:379
  90.0 2.5 %collective-permute-start.39 = (bf16[8,128,128]{2,1,0:T(8,128)(2,1)}, bf16[8,128,128]{2,1,0:T(8,128)(2,1)S(1)}, u32[]{:S(2)}, u32[]{:S(2)}) collective-permute-start(bf16[8,128,128]{2,1,0:T(8,128)(2,1)} %get-tuple-element.140), channel_id=1, source_target_pairs={{1,0},{2,3},{0,1},{3,2},{5,4},{6,7},{4,5},{7,6},{9,8},{10,11},{8,9... | collective-permute-start | bytes 786440 | tf_op jit(solution)/shard_map/cond/branch_2_fun/ppermute | solution.py:290
  92.9 5.5 %branch_2_fun.1.refs_0_ = f32[89,128,128]{2,1,0:T(8,128)} custom-call(s32[8,128]{1,0:T(8,128)S(1)} %get-tuple-element.132.listed, f32[89,128,128]{2,1,0:T(8,128)} %get-tuple-element.142.resident), custom_call_target="tpu_custom_call" | custom-call | tf_op jit(solution)/shard_map/cond/branch_2_fun/pallas_call | solution.py:368
  98.4 3.4 %update.34.refs_0_ = f32[89,128,128]{2,1,0:T(8,128)} custom-call(s32[8,128]{1,0:T(8,128)S(1)} %get-tuple-element.132.listed, s32[1]{0:T(128)} %get-tuple-element.133.slab_start, f32[8,128,128]{2,1,0:T(8,128)} %get-tuple-element.146.own, bf16[8,128,128]{2,1,0:T(8,128)(2,1)} %copy-done.19, ...), custom_call_target="tpu_custom_call", output_to_operand_aliasing={{}: (6, {})} | custom-call | tf_op jit(solution)/shard_map/cond/branch_2_fun/update/pallas_call | solution.py:394
  101.8 2.3 %collective-permute-done.45.low = bf16[13,128,128]{2,1,0:T(8,128)(2,1)S(1)} collective-permute-done((bf16[13,128,128]{2,1,0:T(8,128)(2,1)}, bf16[13,128,128]{2,1,0:T(8,128)(2,1)S(1)}, u32[]{:S(2)}, u32[]{:S(2)}) %collective-permute-start.45) | collective-permute-done | bytes 426016 | tf_op jit(solution)/shard_map/cond/branch_2_fun/ppermute | solution.py:290
  104.9 3.8 %update.35.refs_0_ = f32[89,128,128]{2,1,0:T(8,128)} custom-call(s32[8,128]{1,0:T(8,128)S(1)} %get-tuple-element.132.listed, s32[1]{0:T(128)} %get-tuple-element.133.slab_start, f32[13,128,128]{2,1,0:T(8,128)} %get-tuple-element.143.own, bf16[13,128,128]{2,1,0:T(8,128)(2,1)} %copy-done.40, ...), custom_call_target="tpu_custom_call", output_to_operand_aliasing={{}: (6, {})} | custom-call | tf_op jit(solution)/shard_map/cond/branch_2_fun/update/pallas_call | solution.py:394
  108.7 1.0 collective-permute-done.39.high
  109.7 3.5 %collective-permute-done.40.low = bf16[8,128,128]{2,1,0:T(8,128)(2,1)S(1)} collective-permute-done((bf16[8,128,128]{2,1,0:T(8,128)(2,1)}, bf16[8,128,128]{2,1,0:T(8,128)(2,1)S(1)}, u32[]{:S(2)}, u32[]{:S(2)}) %collective-permute-start.40) | collective-permute-done | bytes 262176 | tf_op jit(solution)/shard_map/cond/branch_2_fun/ppermute | solution.py:290
  113.9 3.4 %update.36 = f32[89,128,128]{2,1,0:T(8,128)} custom-call(s32[8,128]{1,0:T(8,128)S(1)} %get-tuple-element.132.listed, s32[1]{0:T(128)} %get-tuple-element.133.slab_start, f32[8,128,128]{2,1,0:T(8,128)} %get-tuple-element.139.own, bf16[8,128,128]{2,1,0:T(8,128)(2,1)} %copy-done.64, bf16[8,128,128]{2,1,0:T(8,128)(2,1)} %copy-done.65, ...), custom_call_target="tpu_custom_call", output_to_operand_aliasing={{}: (6, {})} | custom-call | tf_op jit(solution)/shard_map/cond/branch_2_fun/update/pallas_call | solution.py:394
  (57 shorter events, 9.0 us)
Async XLA Ops:
  6.3 12.2 %copy-start.3 = (bf16[4,89,32,128]{3,2,1,0:T(8,128)(2,1)S(1)}, bf16[4,89,32,128]{3,2,1,0:T(8,128)(2,1)}, u32[]{:S(2)}) copy-start(bf16[4,89,32,128]{3,2,1,0:T(8,128)(2,1)} %get-tuple-element.135.legendre) | copy-start | bytes 8749060 | tf_op jit(solution)/shard_map/cond
  6.3 1.5 %collective-permute-start.27 = (bf16[4,128,128]{2,1,0:T(8,128)(2,1)S(1)}, bf16[4,128,128]{2,1,0:T(8,128)(2,1)S(1)}, u32[]{:S(2)}, u32[]{:S(2)}) collective-permute-start(bf16[4,128,128]{2,1,0:T(8,128)(2,1)S(1)} %get-tuple-element.134), channel_id=1, source_target_pairs={{0,4},{4,0},{8,12},{12,8},{16,20},{20,16},{24,28},{28,24},{1,5},{5... | collective-permute-start | bytes 393224 | tf_op jit(solution)/shard_map/cond/branch_2_fun/ppermute | solution.py:290
  7.9 8.0 %copy-start.31 = (bf16[4,128,128]{2,1,0:T(8,128)(2,1)}, bf16[4,128,128]{2,1,0:T(8,128)(2,1)S(1)}, u32[]{:S(2)}) copy-start(bf16[4,128,128]{2,1,0:T(8,128)(2,1)S(1)} %add.70) | copy-start | bytes 393220 | tf_op jit(solution)/shard_map/cond
  7.9 8.0 %collective-permute-start.28 = (bf16[4,128,128]{2,1,0:T(8,128)(2,1)S(1)}, bf16[4,128,128]{2,1,0:T(8,128)(2,1)S(1)}, u32[]{:S(2)}, u32[]{:S(2)}) collective-permute-start(bf16[4,128,128]{2,1,0:T(8,128)(2,1)S(1)} %add.70), channel_id=1, source_target_pairs={{0,8},{4,12},{8,0},{12,4},{16,24},{20,28},{24,16},{28,20},{1,9},{5... | collective-permute-start | bytes 393224 | tf_op jit(solution)/shard_map/cond/branch_2_fun/ppermute | solution.py:290
  14.4 17.4 %collective-permute-start.33 = (bf16[8,128,128]{2,1,0:T(8,128)(2,1)}, bf16[8,128,128]{2,1,0:T(8,128)(2,1)}, u32[]{:S(2)}, u32[]{:S(2)}) collective-permute-start(bf16[8,128,128]{2,1,0:T(8,128)(2,1)} %design.35.refs_0_), channel_id=1, source_target_pairs={{0,1},{3,2},{1,0},{2,3},{4,5},{7,6},{5,4},{6,7},{8,9},{11,10},{9,8... | collective-permute-start | bytes 786440 | tf_op jit(solution)/shard_map/cond/branch_2_fun/ppermute | solution.py:290
  16.9 7.7 %collective-permute-start.29 = (bf16[4,128,128]{2,1,0:T(8,128)(2,1)S(1)}, bf16[4,128,128]{2,1,0:T(8,128)(2,1)}, u32[]{:S(2)}, u32[]{:S(2)}) collective-permute-start(bf16[4,128,128]{2,1,0:T(8,128)(2,1)S(1)} %add.71), channel_id=1, source_target_pairs={{0,16},{4,20},{8,24},{12,28},{16,0},{20,4},{24,8},{28,12},{1,17},{... | collective-permute-start | bytes 393224 | tf_op jit(solution)/shard_map/cond/branch_2_fun/ppermute | solution.py:290
  21.4 51.4 %collective-permute-start.41 = (bf16[13,128,128]{2,1,0:T(8,128)(2,1)}, bf16[13,128,128]{2,1,0:T(8,128)(2,1)}, u32[]{:S(2)}, u32[]{:S(2)}) collective-permute-start(bf16[13,128,128]{2,1,0:T(8,128)(2,1)} %design.36.refs_0_), channel_id=1, source_target_pairs={{0,1},{3,2},{4,5},{7,6},{8,9},{11,10},{12,13},{15,14},{16,17},{19,... | collective-permute-start | bytes 1277960 | tf_op jit(solution)/shard_map/cond/branch_2_fun/ppermute | solution.py:290
  25.6 23.3 %copy-start.23 = (bf16[4,128,128]{2,1,0:T(8,128)(2,1)}, bf16[4,128,128]{2,1,0:T(8,128)(2,1)S(1)}, u32[]{:S(2)}) copy-start(bf16[4,128,128]{2,1,0:T(8,128)(2,1)S(1)} %add.72.refs_0_) | copy-start | bytes 393220 | tf_op jit(solution)/shard_map/cond
  25.6 15.1 %collective-permute-start.30 = (bf16[4,128,128]{2,1,0:T(8,128)(2,1)S(1)}, bf16[4,128,128]{2,1,0:T(8,128)(2,1)S(1)}, u32[]{:S(2)}, u32[]{:S(2)}) collective-permute-start(bf16[4,128,128]{2,1,0:T(8,128)(2,1)S(1)} %add.72.refs_0_), channel_id=1, source_target_pairs={{0,1},{3,2},{1,0},{2,3},{4,5},{7,6},{5,4},{6,7},{8,9},{11,10},{9,8... | collective-permute-start | bytes 393224 | tf_op jit(solution)/shard_map/cond/branch_2_fun/ppermute | solution.py:290
  25.7 7.5 %collective-permute-start.31 = (bf16[2,128,128]{2,1,0:T(8,128)(2,1)S(1)}, bf16[2,128,128]{2,1,0:T(8,128)(2,1)S(1)}, u32[]{:S(2)}, u32[]{:S(2)}) collective-permute-start(bf16[2,128,128]{2,1,0:T(8,128)(2,1)S(1)} %slice.38), channel_id=1, source_target_pairs={{1,2},{2,1},{5,6},{6,5},{9,10},{10,9},{13,14},{14,13},{17,18},{18,... | collective-permute-start | bytes 196616 | tf_op jit(solution)/shard_map/cond/branch_2_fun/ppermute | solution.py:290
  26.4 12.9 %collective-permute-start.32 = (bf16[2,128,128]{2,1,0:T(8,128)(2,1)S(1)}, bf16[2,128,128]{2,1,0:T(8,128)(2,1)S(1)}, u32[]{:S(2)}, u32[]{:S(2)}) collective-permute-start(bf16[2,128,128]{2,1,0:T(8,128)(2,1)S(1)} %slice.38), channel_id=1, source_target_pairs={{0,2},{3,1},{1,0},{2,3},{4,6},{7,5},{5,4},{6,7},{8,10},{11,9},{9,8... | collective-permute-start | bytes 196616 | tf_op jit(solution)/shard_map/cond/branch_2_fun/ppermute | solution.py:290
  31.7 41.7 %collective-permute-start.42 = (bf16[13,128,128]{2,1,0:T(8,128)(2,1)}, bf16[13,128,128]{2,1,0:T(8,128)(2,1)}, u32[]{:S(2)}, u32[]{:S(2)}) collective-permute-start(bf16[13,128,128]{2,1,0:T(8,128)(2,1)} %design.36.refs_0_), channel_id=1, source_target_pairs={{1,2},{2,1},{5,6},{6,5},{9,10},{10,9},{13,14},{14,13},{17,18},{18,... | collective-permute-start | bytes 1277960 | tf_op jit(solution)/shard_map/cond/branch_2_fun/ppermute | solution.py:290
  33.2 15.7 %copy-start.83 = (bf16[2,128,128]{2,1,0:T(8,128)(2,1)}, bf16[2,128,128]{2,1,0:T(8,128)(2,1)S(1)}, u32[]{:S(2)}) copy-start(bf16[2,128,128]{2,1,0:T(8,128)(2,1)S(1)} %collective-permute-done.31.refs_2_) | copy-start | bytes 196612 | tf_op jit(solution)/shard_map/cond
  33.2 40.2 %collective-permute-start.43 = (bf16[13,128,128]{2,1,0:T(8,128)(2,1)}, bf16[13,128,128]{2,1,0:T(8,128)(2,1)}, u32[]{:S(2)}, u32[]{:S(2)}) collective-permute-start(bf16[13,128,128]{2,1,0:T(8,128)(2,1)} %design.36.refs_0_), channel_id=1, source_target_pairs={{0,2},{3,1},{4,6},{7,5},{8,10},{11,9},{12,14},{15,13},{16,18},{19,... | collective-permute-start | bytes 1277960 | tf_op jit(solution)/shard_map/cond/branch_2_fun/ppermute | solution.py:290
  39.3 1.4 %copy-start.85 = (bf16[2,128,128]{2,1,0:T(8,128)(2,1)}, bf16[2,128,128]{2,1,0:T(8,128)(2,1)S(1)}, u32[]{:S(2)}) copy-start(bf16[2,128,128]{2,1,0:T(8,128)(2,1)S(1)} %collective-permute-done.32.refs_3_) | copy-start | bytes 196612 | tf_op jit(solution)/shard_map/cond
  39.3 11.4 %collective-permute-start.34 = (bf16[8,128,128]{2,1,0:T(8,128)(2,1)}, bf16[8,128,128]{2,1,0:T(8,128)(2,1)}, u32[]{:S(2)}, u32[]{:S(2)}) collective-permute-start(bf16[8,128,128]{2,1,0:T(8,128)(2,1)} %design.35.refs_0_), channel_id=1, source_target_pairs={{1,2},{2,1},{5,6},{6,5},{9,10},{10,9},{13,14},{14,13},{17,18},{18,... | collective-permute-start | bytes 786440 | tf_op jit(solution)/shard_map/cond/branch_2_fun/ppermute | solution.py:290
  40.6 8.2 %copy-start.72 = (bf16[4,128,128]{2,1,0:T(8,128)(2,1)}, bf16[4,128,128]{2,1,0:T(8,128)(2,1)S(1)}, u32[]{:S(2)}) copy-start(bf16[4,128,128]{2,1,0:T(8,128)(2,1)S(1)} %collective-permute-done.30.refs_1_) | copy-start | bytes 393220 | tf_op jit(solution)/shard_map/cond
  40.7 11.0 %collective-permute-start.35 = (bf16[8,128,128]{2,1,0:T(8,128)(2,1)}, bf16[8,128,128]{2,1,0:T(8,128)(2,1)}, u32[]{:S(2)}, u32[]{:S(2)}) collective-permute-start(bf16[8,128,128]{2,1,0:T(8,128)(2,1)} %design.35.refs_0_), channel_id=1, source_target_pairs={{0,2},{3,1},{1,0},{2,3},{4,6},{7,5},{5,4},{6,7},{8,10},{11,9},{9,8... | collective-permute-start | bytes 786440 | tf_op jit(solution)/shard_map/cond/branch_2_fun/ppermute | solution.py:290
  50.7 29.9 %collective-permute-start.37 = (bf16[8,128,128]{2,1,0:T(8,128)(2,1)}, bf16[8,128,128]{2,1,0:T(8,128)(2,1)S(1)}, u32[]{:S(2)}, u32[]{:S(2)}) collective-permute-start(bf16[8,128,128]{2,1,0:T(8,128)(2,1)} %design.34.refs_4_.refs_0_), channel_id=1, source_target_pairs={{1,2},{2,1},{5,6},{6,5},{9,10},{10,9},{13,14},{14,13},{17,18},{18,... | collective-permute-start | bytes 786440 | tf_op jit(solution)/shard_map/cond/branch_2_fun/ppermute | solution.py:290
  55.2 25.3 %collective-permute-start.36 = (bf16[8,128,128]{2,1,0:T(8,128)(2,1)}, bf16[8,128,128]{2,1,0:T(8,128)(2,1)S(1)}, u32[]{:S(2)}, u32[]{:S(2)}) collective-permute-start(bf16[8,128,128]{2,1,0:T(8,128)(2,1)} %get-tuple-element.137), channel_id=1, source_target_pairs={{1,0},{2,3},{0,1},{3,2},{5,4},{6,7},{4,5},{7,6},{9,8},{10,11},{8,9... | collective-permute-start | bytes 786440 | tf_op jit(solution)/shard_map/cond/branch_2_fun/ppermute | solution.py:290
  72.9 13.0 %collective-permute-start.38 = (bf16[8,128,128]{2,1,0:T(8,128)(2,1)}, bf16[8,128,128]{2,1,0:T(8,128)(2,1)S(1)}, u32[]{:S(2)}, u32[]{:S(2)}) collective-permute-start(bf16[8,128,128]{2,1,0:T(8,128)(2,1)} %get-tuple-element.138), channel_id=1, source_target_pairs={{1,0},{2,3},{0,2},{3,1},{5,4},{6,7},{4,6},{7,5},{9,8},{10,11},{8,1... | collective-permute-start | bytes 786440 | tf_op jit(solution)/shard_map/cond/branch_2_fun/ppermute | solution.py:290
  78.1 23.7 %collective-permute-start.44 = (bf16[13,128,128]{2,1,0:T(8,128)(2,1)}, bf16[13,128,128]{2,1,0:T(8,128)(2,1)S(1)}, u32[]{:S(2)}, u32[]{:S(2)}) collective-permute-start(bf16[13,128,128]{2,1,0:T(8,128)(2,1)} %get-tuple-element.144), channel_id=1, source_target_pairs={{1,0},{2,3},{0,1},{3,2},{5,4},{6,7},{4,5},{7,6},{9,8},{10,11},{8,9... | collective-permute-start | bytes 1277960 | tf_op jit(solution)/shard_map/cond/branch_2_fun/ppermute | solution.py:290
  79.6 24.5 %collective-permute-start.45 = (bf16[13,128,128]{2,1,0:T(8,128)(2,1)}, bf16[13,128,128]{2,1,0:T(8,128)(2,1)S(1)}, u32[]{:S(2)}, u32[]{:S(2)}) collective-permute-start(bf16[13,128,128]{2,1,0:T(8,128)(2,1)} %get-tuple-element.145), channel_id=1, source_target_pairs={{1,0},{2,3},{0,2},{3,1},{5,4},{6,7},{4,6},{7,5},{9,8},{10,11},{8,1... | collective-permute-start | bytes 1277960 | tf_op jit(solution)/shard_map/cond/branch_2_fun/ppermute | solution.py:290
  80.5 5.3 %copy-start.66 = (bf16[8,128,128]{2,1,0:T(8,128)(2,1)}, bf16[8,128,128]{2,1,0:T(8,128)(2,1)S(1)}, u32[]{:S(2)}) copy-start(bf16[8,128,128]{2,1,0:T(8,128)(2,1)S(1)} %collective-permute-done.37.refs_2_) | copy-start | bytes 786436 | tf_op jit(solution)/shard_map/cond
  80.5 5.3 %copy-start.19 = (bf16[8,128,128]{2,1,0:T(8,128)(2,1)}, bf16[8,128,128]{2,1,0:T(8,128)(2,1)S(1)}, u32[]{:S(2)}) copy-start(bf16[8,128,128]{2,1,0:T(8,128)(2,1)S(1)} %collective-permute-done.36.refs_1_.high) | copy-start | bytes 786436 | tf_op jit(solution)/shard_map/cond
  85.9 0.7 copy-start.20
  90.0 19.7 %collective-permute-start.39 = (bf16[8,128,128]{2,1,0:T(8,128)(2,1)}, bf16[8,128,128]{2,1,0:T(8,128)(2,1)S(1)}, u32[]{:S(2)}, u32[]{:S(2)}) collective-permute-start(bf16[8,128,128]{2,1,0:T(8,128)(2,1)} %get-tuple-element.140), channel_id=1, source_target_pairs={{1,0},{2,3},{0,1},{3,2},{5,4},{6,7},{4,5},{7,6},{9,8},{10,11},{8,9... | collective-permute-start | bytes 786440 | tf_op jit(solution)/shard_map/cond/branch_2_fun/ppermute | solution.py:290
  92.5 20.7 %collective-permute-start.40 = (bf16[8,128,128]{2,1,0:T(8,128)(2,1)}, bf16[8,128,128]{2,1,0:T(8,128)(2,1)S(1)}, u32[]{:S(2)}, u32[]{:S(2)}) collective-permute-start(bf16[8,128,128]{2,1,0:T(8,128)(2,1)} %get-tuple-element.141), channel_id=1, source_target_pairs={{1,0},{2,3},{0,2},{3,1},{5,4},{6,7},{4,6},{7,5},{9,8},{10,11},{8,1... | collective-permute-start | bytes 786440 | tf_op jit(solution)/shard_map/cond/branch_2_fun/ppermute | solution.py:290
  101.8 2.3 %copy-start.40 = (bf16[13,128,128]{2,1,0:T(8,128)(2,1)}, bf16[13,128,128]{2,1,0:T(8,128)(2,1)S(1)}, u32[]{:S(2)}) copy-start(bf16[13,128,128]{2,1,0:T(8,128)(2,1)S(1)} %collective-permute-done.44.high) | copy-start | bytes 1277956 | tf_op jit(solution)/shard_map/cond
  104.1 0.8 copy-start.41
  109.7 3.5 %copy-start.64 = (bf16[8,128,128]{2,1,0:T(8,128)(2,1)}, bf16[8,128,128]{2,1,0:T(8,128)(2,1)S(1)}, u32[]{:S(2)}) copy-start(bf16[8,128,128]{2,1,0:T(8,128)(2,1)S(1)} %collective-permute-done.39.high) | copy-start | bytes 786436 | tf_op jit(solution)/shard_map/cond
  113.2 0.7 copy-start.65
  (2 other events, 1.4 us)

commit v4 on v3

--- a/solution.py
+++ b/solution.py
@@ -19,14 +19,14 @@
 
 
 def totals_of(slot_count):
-    counts = [9, 19, 29] + list(range(40, slot_count - 4, 12))
+    counts = range(9, slot_count - 6, 16)
     return [count for count in counts if count < slot_count] + [slot_count]
 
 
 def chunk_sizes(total):
-    count = max(1, -(-(total - 2) // 13))
-    less = max(1, (total - 4 * (count // 2)) // count)
-    sizes = [less + 4 * (k % 2) if count > 1 else total for k in range(count)]
+    count = total // 15 + 2 if total > 12 else 1
+    less = max(1, (total - 1 * (count // 2)) // count)
+    sizes = [less + 1 * (k % 2) if count > 1 else total for k in range(count)]
     for k in (list(range(1, count, 2)) + list(range(0, count, 2)))[: total - sum(sizes)]:
         sizes[k] += 1
     return sizes

time: 119 us -> 126 us (1.059)
  starting transfers between devices: 55 us -> 39.5 us
  waiting for transfers between devices: 13.4 us -> 26.9 us
  Pallas kernels: 41.4 us -> 51.9 us
  other arithmetic: 2.87 us -> 1.04 us
    ppermute x19 -> x22, starting transfers between devices: 55 us -> 39.5 us  [shift(): return lax.ppermute(value, axis, pairs)]
    ppermute x19 -> x22, waiting for transfers between devices: 13.4 us -> 26.9 us  [shift(): return lax.ppermute(value, axis, pairs)]
    pallas_call x3 -> x4, Pallas kernels: 11.6 us -> 16.3 us  [multiply(): pl.pallas_call(functools.partial(product_kernel, len(streams)), out_shape...]
    pallas_call x3 -> x4, Pallas kernels: 10.6 us -> 14.3 us  [update(): pl.pallas_call(functools.partial(update_kernel, offset), in_specs=[smem]...]
    pallas_call x3 -> x4, Pallas kernels: 8.78 us -> 11.9 us  [design(): pl.pallas_call(functools.partial(design_kernel, offset), out_shape=tiles_...]
    add x3, other arithmetic: 1.95 us -> 0.11 us  [run(): both = both + shift(both, pairs, 'row')]
  transfers between devices with their start and end apart: 19 -> 22, of which waited for: 6 -> 8; matrix products, arithmetic and copies ran while one was open for 2% -> 1% of each run, Pallas kernels for 29% -> 36%
where the time goes in v4:
time: 126 us
  Pallas kernels  51.9 us (41%)
  starting transfers between devices  39.5 us (31%)
  waiting for transfers between devices  26.9 us (21%)
  local copies, waits for them, and re-layouts  4.42 us (4%)
  between operations  1.33 us (1%)
    ppermute x22, starting transfers between devices, shift(): return lax.ppermute(value, axis, pairs)  39.5 us
    ppermute x22, waiting for transfers between devices, shift(): return lax.ppermute(value, axis, pairs)  26.9 us
    pallas_call x4, Pallas kernels, multiply(): pl.pallas_call(functools.partial(product_kernel, len(streams)), out_shape...  16.3 us
    pallas_call x4, Pallas kernels, update(): pl.pallas_call(functools.partial(update_kernel, offset), in_specs=[smem]...  14.3 us
    pallas_call x4, Pallas kernels, design(): pl.pallas_call(functools.partial(design_kernel, offset), out_shape=tiles_...  11.9 us
    pallas_call x1, Pallas kernels, copy_rest(): pl.pallas_call(functools.partial(copy_kernel, offset), in_specs=[smem, an...  4.44 us
    pallas_call x1, Pallas kernels, per_device(): pl.pallas_call(functools.partial(plan_kernel, counts, row_count), out_sha...  3.2 us
  transfers between devices with their start and end apart: 22, of which 8 were waited for; matrix products, arithmetic and copies ran while one was open for 1% of the time, Pallas kernels for 36%

profile of v4, /device:TPU:0, one launch (start us, length us, event | category | flops | bytes accessed | tf_op | source)
XLA Modules:
  0.0 125.7 jit_solution(6361061752518467338)
XLA Ops:
  2.4 3.2 %plan.1 = (s32[8,128]{1,0:T(8,128)S(1)}, s32[1,128]{1,0:T(1,128)}, bf16[4,128,128]{2,1,0:T(8,128)(2,1)S(1)}) custom-call(s32[1]{0:T(128)S(6)} %copy.79.slab_start, f32[8]{0:T(128)} %span_weight.1, s32[712]{0:T(1024)} %order.1, f32[512]{0:T(512)} %obs_weight.1, s32[512]{0:T(512)} %span_of.1, bf16[4,89,32,128]{3,2,1,0:T(8,128)(2,1)} %bitcast.40, ...), custom_call_target="tpu_custom_call" | custom-call | tf_op jit(solution)/shard_map/plan/pallas_call | solution.py:343
  6.3 118.7 %conditional.1 = (f32[89,1,1,128,128]{4,3,2,1,0:T(8,128)}) conditional(s32[]{:T(128)} %bitcast.22, (bf16[4,128,128]{2,1,0:T(8,128)(2,1)S(1)}, s32[8,128]{1,0:T(8,128)S(1)}, bf16[4,89,32,128]{3,2,1,0:T(8,128)(2,1)}, f32[4,128,128]{2,1,0:T(8,128)S(1)}, f32[89,128,128]{2,1,0:T(8,128)}, /*index=5*/s32[1]{0:T(128)}) %tuple.55, ...), branch_computations={%region_0.1_spmd, %region_1.2_spmd, %region_2.3_spmd, %region_3.4_... | conditional | flops 196608 | bytes 70518320 | solution.py:446
  6.9 4.2 %design.31.refs_0_ = bf16[11,128,128]{2,1,0:T(8,128)(2,1)} custom-call(s32[8,128]{1,0:T(8,128)S(1)} %get-tuple-element.109.listed, bf16[4,89,32,128]{3,2,1,0:T(8,128)(2,1)} %get-tuple-element.112.legendre, f32[4,128,128]{2,1,0:T(8,128)S(1)} %get-tuple-element.113.table), custom_call_target="tpu_custom_call" | custom-call | tf_op jit(solution)/shard_map/cond/branch_2_fun/design/pallas_call | solution.py:335
  11.1 5.1 %collective-permute-start.36 = (bf16[11,128,128]{2,1,0:T(8,128)(2,1)}, bf16[11,128,128]{2,1,0:T(8,128)(2,1)}, u32[]{:S(2)}, u32[]{:S(2)}) collective-permute-start(bf16[11,128,128]{2,1,0:T(8,128)(2,1)} %design.31.refs_0_), channel_id=1, source_target_pairs={{0,1},{3,2},{4,5},{7,6},{8,9},{11,10},{12,13},{15,14},{16,17},{19,... | collective-permute-start | bytes 1081352 | tf_op jit(solution)/shard_map/cond/branch_2_fun/ppermute | solution.py:290
  17.6 1.6 %collective-permute-start.31 = (bf16[4,128,128]{2,1,0:T(8,128)(2,1)S(1)}, bf16[4,128,128]{2,1,0:T(8,128)(2,1)S(1)}, u32[]{:S(2)}, u32[]{:S(2)}) collective-permute-start(bf16[4,128,128]{2,1,0:T(8,128)(2,1)S(1)} %add.58), channel_id=1, source_target_pairs={{0,8},{4,12},{8,0},{12,4},{16,24},{20,28},{24,16},{28,20},{1,9},{5... | collective-permute-start | bytes 393224 | tf_op jit(solution)/shard_map/cond/branch_2_fun/ppermute | solution.py:290
  19.2 4.1 %collective-permute-done.31 = bf16[4,128,128]{2,1,0:T(8,128)(2,1)S(1)} collective-permute-done((bf16[4,128,128]{2,1,0:T(8,128)(2,1)S(1)}, bf16[4,128,128]{2,1,0:T(8,128)(2,1)S(1)}, u32[]{:S(2)}, u32[]{:S(2)}) %collective-permute-start.31) | collective-permute-done | bytes 131104 | tf_op jit(solution)/shard_map/cond/branch_2_fun/ppermute | solution.py:290
  23.3 1.6 %collective-permute-start.32 = (bf16[4,128,128]{2,1,0:T(8,128)(2,1)S(1)}, bf16[4,128,128]{2,1,0:T(8,128)(2,1)S(1)}, u32[]{:S(2)}, u32[]{:S(2)}) collective-permute-start(bf16[4,128,128]{2,1,0:T(8,128)(2,1)S(1)} %add.59), channel_id=1, source_target_pairs={{0,16},{4,20},{8,24},{12,28},{16,0},{20,4},{24,8},{28,12},{1,17},{... | collective-permute-start | bytes 393224 | tf_op jit(solution)/shard_map/cond/branch_2_fun/ppermute | solution.py:290
  24.9 3.4 %collective-permute-done.32 = bf16[4,128,128]{2,1,0:T(8,128)(2,1)S(1)} collective-permute-done((bf16[4,128,128]{2,1,0:T(8,128)(2,1)S(1)}, bf16[4,128,128]{2,1,0:T(8,128)(2,1)S(1)}, u32[]{:S(2)}, u32[]{:S(2)}) %collective-permute-start.32) | collective-permute-done | bytes 131104 | tf_op jit(solution)/shard_map/cond/branch_2_fun/ppermute | solution.py:290
  29.2 4.9 %collective-permute-start.38 = (bf16[11,128,128]{2,1,0:T(8,128)(2,1)}, bf16[11,128,128]{2,1,0:T(8,128)(2,1)}, u32[]{:S(2)}, u32[]{:S(2)}) collective-permute-start(bf16[11,128,128]{2,1,0:T(8,128)(2,1)} %design.31.refs_0_), channel_id=1, source_target_pairs={{0,2},{3,1},{4,6},{7,5},{8,10},{11,9},{12,14},{15,13},{16,18},{19,... | collective-permute-start | bytes 1081352 | tf_op jit(solution)/shard_map/cond/branch_2_fun/ppermute | solution.py:290
  34.1 2.6 %design.33.refs_0_ = bf16[10,128,128]{2,1,0:T(8,128)(2,1)} custom-call(s32[8,128]{1,0:T(8,128)S(1)} %get-tuple-element.109.listed, bf16[4,89,32,128]{3,2,1,0:T(8,128)(2,1)S(1)} %copy-done.3, f32[4,128,128]{2,1,0:T(8,128)S(1)} %get-tuple-element.113.table), custom_call_target="tpu_custom_call" | custom-call | tf_op jit(solution)/shard_map/cond/branch_2_fun/design/pallas_call | solution.py:335
  38.0 4.8 %collective-permute-start.35 = (bf16[2,128,128]{2,1,0:T(8,128)(2,1)}, bf16[2,128,128]{2,1,0:T(8,128)(2,1)}, u32[]{:S(2)}, u32[]{:S(2)}) collective-permute-start(bf16[2,128,128]{2,1,0:T(8,128)(2,1)} %slice.30), channel_id=1, source_target_pairs={{0,2},{3,1},{1,0},{2,3},{4,6},{7,5},{5,4},{6,7},{8,10},{11,9},{9,8... | collective-permute-start | bytes 196616 | tf_op jit(solution)/shard_map/cond/branch_2_fun/ppermute | solution.py:290
  42.8 2.7 %design.30.refs_4_.refs_0_ = bf16[11,128,128]{2,1,0:T(8,128)(2,1)} custom-call(s32[8,128]{1,0:T(8,128)S(1)} %get-tuple-element.109.listed, bf16[4,89,32,128]{3,2,1,0:T(8,128)(2,1)S(1)} %copy-done.3, f32[4,128,128]{2,1,0:T(8,128)S(1)} %get-tuple-element.113.table), custom_call_target="tpu_custom_call" | custom-call | tf_op jit(solution)/shard_map/cond/branch_2_fun/design/pallas_call | solution.py:335
  45.5 1.4 %collective-permute-start.45 = (bf16[10,128,128]{2,1,0:T(8,128)(2,1)}, bf16[10,128,128]{2,1,0:T(8,128)(2,1)}, u32[]{:S(2)}, u32[]{:S(2)}) collective-permute-start(bf16[10,128,128]{2,1,0:T(8,128)(2,1)} %design.33.refs_0_), channel_id=1, source_target_pairs={{1,2},{2,1},{5,6},{6,5},{9,10},{10,9},{13,14},{14,13},{17,18},{18,... | collective-permute-start | bytes 983048 | tf_op jit(solution)/shard_map/cond/branch_2_fun/ppermute | solution.py:290
  48.0 3.5 %collective-permute-start.46 = (bf16[10,128,128]{2,1,0:T(8,128)(2,1)}, bf16[10,128,128]{2,1,0:T(8,128)(2,1)}, u32[]{:S(2)}, u32[]{:S(2)}) collective-permute-start(bf16[10,128,128]{2,1,0:T(8,128)(2,1)} %design.33.refs_0_), channel_id=1, source_target_pairs={{0,2},{3,1},{1,0},{2,3},{4,6},{7,5},{5,4},{6,7},{8,10},{11,9},{9,8... | collective-permute-start | bytes 983048 | tf_op jit(solution)/shard_map/cond/branch_2_fun/ppermute | solution.py:290
  51.5 1.4 %collective-permute-start.40 = (bf16[11,128,128]{2,1,0:T(8,128)(2,1)}, bf16[11,128,128]{2,1,0:T(8,128)(2,1)}, u32[]{:S(2)}, u32[]{:S(2)}) collective-permute-start(bf16[11,128,128]{2,1,0:T(8,128)(2,1)} %design.30.refs_4_.refs_0_), channel_id=1, source_target_pairs={{1,2},{2,1},{5,6},{6,5},{9,10},{10,9},{13,14},{14,13},{17,18},{18,... | collective-permute-start | bytes 1081352 | tf_op jit(solution)/shard_map/cond/branch_2_fun/ppermute | solution.py:290
  52.8 1.7 %factor.8 = bf16[512,256]{1,0:T(8,128)(2,1)} custom-call(bf16[4,128,128]{2,1,0:T(8,128)(2,1)} %copy-done.17, bf16[4,128,128]{2,1,0:T(8,128)(2,1)} %copy-done.55, bf16[2,128,128]{2,1,0:T(8,128)(2,1)} %copy-done.64, bf16[2,128,128]{2,1,0:T(8,128)(2,1)} %collective-permute-done.35.refs_3_), custom_call_target="tpu_custom_call" | custom-call | tf_op jit(solution)/shard_map/cond/branch_2_fun/factor/pallas_call | solution.py:356
  54.6 4.4 %product.30 = (f32[11,128,128]{2,1,0:T(8,128)}, bf16[11,128,128]{2,1,0:T(8,128)(2,1)}, bf16[11,128,128]{2,1,0:T(8,128)(2,1)}) custom-call(bf16[512,256]{1,0:T(8,128)(2,1)} %factor.8, bf16[11,128,128]{2,1,0:T(8,128)(2,1)} %design.31.refs_0_, bf16[11,128,128]{2,1,0:T(8,128)(2,1)} %collective-permute-done.36.refs_1_, ...), custom_call_target="tpu_custom_call" | custom-call | tf_op jit(solution)/shard_map/cond/branch_2_fun/product/pallas_call | solution.py:379
  61.3 2.4 %design.32.refs_4_.refs_0_ = bf16[9,128,128]{2,1,0:T(8,128)(2,1)} custom-call(s32[8,128]{1,0:T(8,128)S(1)} %get-tuple-element.109.listed, bf16[4,89,32,128]{3,2,1,0:T(8,128)(2,1)S(1)} %copy-done.3, f32[4,128,128]{2,1,0:T(8,128)S(1)} %get-tuple-element.113.table), custom_call_target="tpu_custom_call" | custom-call | tf_op jit(solution)/shard_map/cond/branch_2_fun/design/pallas_call | solution.py:335
  63.7 4.0 %product.32 = (f32[10,128,128]{2,1,0:T(8,128)}, bf16[10,128,128]{2,1,0:T(8,128)(2,1)}, bf16[10,128,128]{2,1,0:T(8,128)(2,1)}) custom-call(bf16[512,256]{1,0:T(8,128)(2,1)} %factor.8, bf16[10,128,128]{2,1,0:T(8,128)(2,1)} %design.33.refs_0_, bf16[10,128,128]{2,1,0:T(8,128)(2,1)} %collective-permute-done.44.refs_1_, ...), custom_call_target="tpu_custom_call" | custom-call | tf_op jit(solution)/shard_map/cond/branch_2_fun/product/pallas_call | solution.py:379
  67.8 3.6 %collective-permute-start.47 = (bf16[10,128,128]{2,1,0:T(8,128)(2,1)}, bf16[10,128,128]{2,1,0:T(8,128)(2,1)S(1)}, u32[]{:S(2)}, u32[]{:S(2)}) collective-permute-start(bf16[10,128,128]{2,1,0:T(8,128)(2,1)} %get-tuple-element.120), channel_id=1, source_target_pairs={{1,0},{2,3},{0,1},{3,2},{5,4},{6,7},{4,5},{7,6},{9,8},{10,11},{8,9... | collective-permute-start | bytes 983048 | tf_op jit(solution)/shard_map/cond/branch_2_fun/ppermute | solution.py:290
  72.8 5.5 %collective-permute-done.41.refs_3_.low = bf16[11,128,128]{2,1,0:T(8,128)(2,1)} collective-permute-done((bf16[11,128,128]{2,1,0:T(8,128)(2,1)}, bf16[11,128,128]{2,1,0:T(8,128)(2,1)}, u32[]{:S(2)}, u32[]{:S(2)}) %collective-permute-start.41) | collective-permute-done | bytes 360480 | tf_op jit(solution)/shard_map/cond/branch_2_fun/ppermute | solution.py:290
  78.3 4.1 %product.31 = (f32[11,128,128]{2,1,0:T(8,128)}, bf16[11,128,128]{2,1,0:T(8,128)(2,1)}, bf16[11,128,128]{2,1,0:T(8,128)(2,1)}) custom-call(bf16[512,256]{1,0:T(8,128)(2,1)} %factor.8, bf16[11,128,128]{2,1,0:T(8,128)(2,1)} %design.30.refs_4_.refs_0_, bf16[11,128,128]{2,1,0:T(8,128)(2,1)} %collective-permute-done.39.refs_1_.high, ...), custom_call_target="tpu_custom_call" | custom-call | tf_op jit(solution)/shard_map/cond/branch_2_fun/product/pallas_call | solution.py:379
  82.5 1.4 %collective-permute-start.42 = (bf16[11,128,128]{2,1,0:T(8,128)(2,1)}, bf16[11,128,128]{2,1,0:T(8,128)(2,1)S(1)}, u32[]{:S(2)}, u32[]{:S(2)}) collective-permute-start(bf16[11,128,128]{2,1,0:T(8,128)(2,1)} %get-tuple-element.117), channel_id=1, source_target_pairs={{1,0},{2,3},{0,1},{3,2},{5,4},{6,7},{4,5},{7,6},{9,8},{10,11},{8,9... | collective-permute-start | bytes 1081352 | tf_op jit(solution)/shard_map/cond/branch_2_fun/ppermute | solution.py:290
  85.3 7.0 %collective-permute-done.49.refs_3_.low = bf16[10,128,128]{2,1,0:T(8,128)(2,1)S(1)} collective-permute-done((bf16[10,128,128]{2,1,0:T(8,128)(2,1)}, bf16[10,128,128]{2,1,0:T(8,128)(2,1)S(1)}, u32[]{:S(2)}, u32[]{:S(2)}) %collective-permute-start.49) | collective-permute-done | bytes 327712 | tf_op jit(solution)/shard_map/cond/branch_2_fun/ppermute | solution.py:290
  93.0 3.7 %product.33 = (f32[9,128,128]{2,1,0:T(8,128)}, bf16[9,128,128]{2,1,0:T(8,128)(2,1)}, bf16[9,128,128]{2,1,0:T(8,128)(2,1)}) custom-call(bf16[512,256]{1,0:T(8,128)(2,1)} %factor.8, bf16[9,128,128]{2,1,0:T(8,128)(2,1)} %design.32.refs_4_.refs_0_, bf16[10,128,128]{2,1,0:T(8,128)(2,1)} %copy-done.13, bf16[9,128,128]{2,1,0:T(8,128)(2,1)} %copy-done.45, ...), custom_call_target="tpu_custom_call" | custom-call | tf_op jit(solution)/shard_map/cond/branch_2_fun/product/pallas_call | solution.py:379
  99.0 4.4 %branch_2_fun.1.refs_0_ = f32[89,128,128]{2,1,0:T(8,128)} custom-call(s32[8,128]{1,0:T(8,128)S(1)} %get-tuple-element.109.listed, f32[89,128,128]{2,1,0:T(8,128)} %get-tuple-element.119.resident), custom_call_target="tpu_custom_call" | custom-call | tf_op jit(solution)/shard_map/cond/branch_2_fun/pallas_call | solution.py:368
  103.5 3.6 %update.30.refs_0_ = f32[89,128,128]{2,1,0:T(8,128)} custom-call(s32[8,128]{1,0:T(8,128)S(1)} %get-tuple-element.109.listed, s32[1]{0:T(128)} %get-tuple-element.110.slab_start, f32[10,128,128]{2,1,0:T(8,128)} %get-tuple-element.126.own, bf16[10,128,128]{2,1,0:T(8,128)(2,1)} %copy-done.13, ...), custom_call_target="tpu_custom_call", output_to_operand_aliasing={{}: (6, {})} | custom-call | tf_op jit(solution)/shard_map/cond/branch_2_fun/update/pallas_call | solution.py:394
  107.0 3.6 %update.31.refs_0_ = f32[89,128,128]{2,1,0:T(8,128)} custom-call(s32[8,128]{1,0:T(8,128)S(1)} %get-tuple-element.109.listed, s32[1]{0:T(128)} %get-tuple-element.110.slab_start, f32[11,128,128]{2,1,0:T(8,128)} %get-tuple-element.125.own, bf16[11,128,128]{2,1,0:T(8,128)(2,1)} %collective-permute-done.39.refs_1_.high, ...), custom_call_target="tpu_custom_call", output_to_operand_aliasing={{}: (6, {})} | custom-call | tf_op jit(solution)/shard_map/cond/branch_2_fun/update/pallas_call | solution.py:394
  110.7 2.0 %collective-permute-done.50.high = bf16[9,128,128]{2,1,0:T(8,128)(2,1)S(1)} collective-permute-done((bf16[9,128,128]{2,1,0:T(8,128)(2,1)}, bf16[9,128,128]{2,1,0:T(8,128)(2,1)S(1)}, u32[]{:S(2)}, u32[]{:S(2)}) %collective-permute-start.50) | collective-permute-done | bytes 294944 | tf_op jit(solution)/shard_map/cond/branch_2_fun/ppermute | solution.py:290
  112.7 3.2 %collective-permute-done.51.low = bf16[9,128,128]{2,1,0:T(8,128)(2,1)S(1)} collective-permute-done((bf16[9,128,128]{2,1,0:T(8,128)(2,1)}, bf16[9,128,128]{2,1,0:T(8,128)(2,1)S(1)}, u32[]{:S(2)}, u32[]{:S(2)}) %collective-permute-start.51) | collective-permute-done | bytes 294944 | tf_op jit(solution)/shard_map/cond/branch_2_fun/ppermute | solution.py:290
  116.6 3.5 %update.32.refs_0_ = f32[89,128,128]{2,1,0:T(8,128)} custom-call(s32[8,128]{1,0:T(8,128)S(1)} %get-tuple-element.109.listed, s32[1]{0:T(128)} %get-tuple-element.110.slab_start, f32[9,128,128]{2,1,0:T(8,128)} %get-tuple-element.122.own, bf16[9,128,128]{2,1,0:T(8,128)(2,1)} %copy-done.48, ...), custom_call_target="tpu_custom_call", output_to_operand_aliasing={{}: (6, {})} | custom-call | tf_op jit(solution)/shard_map/cond/branch_2_fun/update/pallas_call | solution.py:394
  120.9 3.6 %update.33 = f32[89,128,128]{2,1,0:T(8,128)} custom-call(s32[8,128]{1,0:T(8,128)S(1)} %get-tuple-element.109.listed, s32[1]{0:T(128)} %get-tuple-element.110.slab_start, f32[11,128,128]{2,1,0:T(8,128)} %get-tuple-element.116.own, bf16[11,128,128]{2,1,0:T(8,128)(2,1)} %copy-done.36, bf16[11,128,128]{2,1,0:T(8,128)(2,1)} %copy-done.37, ...), custom_call_target="tpu_custom_call", output_to_operand_aliasing={{}: (6, {})} | custom-call | tf_op jit(solution)/shard_map/cond/branch_2_fun/update/pallas_call | solution.py:394
  (62 shorter events, 17.4 us)
Async XLA Ops:
  6.3 27.8 %copy-start.3 = (bf16[4,89,32,128]{3,2,1,0:T(8,128)(2,1)S(1)}, bf16[4,89,32,128]{3,2,1,0:T(8,128)(2,1)}, u32[]{:S(2)}) copy-start(bf16[4,89,32,128]{3,2,1,0:T(8,128)(2,1)} %get-tuple-element.112.legendre) | copy-start | bytes 8749060 | tf_op jit(solution)/shard_map/cond
  6.3 11.2 %collective-permute-start.30 = (bf16[4,128,128]{2,1,0:T(8,128)(2,1)S(1)}, bf16[4,128,128]{2,1,0:T(8,128)(2,1)S(1)}, u32[]{:S(2)}, u32[]{:S(2)}) collective-permute-start(bf16[4,128,128]{2,1,0:T(8,128)(2,1)S(1)} %get-tuple-element.111), channel_id=1, source_target_pairs={{0,4},{4,0},{8,12},{12,8},{16,20},{20,16},{24,28},{28,24},{1,5},{5... | collective-permute-start | bytes 393224 | tf_op jit(solution)/shard_map/cond/branch_2_fun/ppermute | solution.py:290
  11.1 26.2 %collective-permute-start.36 = (bf16[11,128,128]{2,1,0:T(8,128)(2,1)}, bf16[11,128,128]{2,1,0:T(8,128)(2,1)}, u32[]{:S(2)}, u32[]{:S(2)}) collective-permute-start(bf16[11,128,128]{2,1,0:T(8,128)(2,1)} %design.31.refs_0_), channel_id=1, source_target_pairs={{0,1},{3,2},{4,5},{7,6},{8,9},{11,10},{12,13},{15,14},{16,17},{19,... | collective-permute-start | bytes 1081352 | tf_op jit(solution)/shard_map/cond/branch_2_fun/ppermute | solution.py:290
  16.2 21.8 %collective-permute-start.37 = (bf16[11,128,128]{2,1,0:T(8,128)(2,1)}, bf16[11,128,128]{2,1,0:T(8,128)(2,1)}, u32[]{:S(2)}, u32[]{:S(2)}) collective-permute-start(bf16[11,128,128]{2,1,0:T(8,128)(2,1)} %design.31.refs_0_), channel_id=1, source_target_pairs={{1,2},{2,1},{5,6},{6,5},{9,10},{10,9},{13,14},{14,13},{17,18},{18,... | collective-permute-start | bytes 1081352 | tf_op jit(solution)/shard_map/cond/branch_2_fun/ppermute | solution.py:290
  17.6 5.7 %collective-permute-start.31 = (bf16[4,128,128]{2,1,0:T(8,128)(2,1)S(1)}, bf16[4,128,128]{2,1,0:T(8,128)(2,1)S(1)}, u32[]{:S(2)}, u32[]{:S(2)}) collective-permute-start(bf16[4,128,128]{2,1,0:T(8,128)(2,1)S(1)} %add.58), channel_id=1, source_target_pairs={{0,8},{4,12},{8,0},{12,4},{16,24},{20,28},{24,16},{28,20},{1,9},{5... | collective-permute-start | bytes 393224 | tf_op jit(solution)/shard_map/cond/branch_2_fun/ppermute | solution.py:290
  23.3 5.0 %collective-permute-start.32 = (bf16[4,128,128]{2,1,0:T(8,128)(2,1)S(1)}, bf16[4,128,128]{2,1,0:T(8,128)(2,1)S(1)}, u32[]{:S(2)}, u32[]{:S(2)}) collective-permute-start(bf16[4,128,128]{2,1,0:T(8,128)(2,1)S(1)} %add.59), channel_id=1, source_target_pairs={{0,16},{4,20},{8,24},{12,28},{16,0},{20,4},{24,8},{28,12},{1,17},{... | collective-permute-start | bytes 393224 | tf_op jit(solution)/shard_map/cond/branch_2_fun/ppermute | solution.py:290
  28.4 24.4 %copy-start.17 = (bf16[4,128,128]{2,1,0:T(8,128)(2,1)}, bf16[4,128,128]{2,1,0:T(8,128)(2,1)S(1)}, u32[]{:S(2)}) copy-start(bf16[4,128,128]{2,1,0:T(8,128)(2,1)S(1)} %add.60.refs_0_) | copy-start | bytes 393220 | tf_op jit(solution)/shard_map/cond
  28.4 23.0 %collective-permute-start.33 = (bf16[4,128,128]{2,1,0:T(8,128)(2,1)S(1)}, bf16[4,128,128]{2,1,0:T(8,128)(2,1)S(1)}, u32[]{:S(2)}, u32[]{:S(2)}) collective-permute-start(bf16[4,128,128]{2,1,0:T(8,128)(2,1)S(1)} %add.60.refs_0_), channel_id=1, source_target_pairs={{0,1},{3,2},{1,0},{2,3},{4,5},{7,6},{5,4},{6,7},{8,9},{11,10},{9,8... | collective-permute-start | bytes 393224 | tf_op jit(solution)/shard_map/cond/branch_2_fun/ppermute | solution.py:290
  29.2 25.4 %collective-permute-start.38 = (bf16[11,128,128]{2,1,0:T(8,128)(2,1)}, bf16[11,128,128]{2,1,0:T(8,128)(2,1)}, u32[]{:S(2)}, u32[]{:S(2)}) collective-permute-start(bf16[11,128,128]{2,1,0:T(8,128)(2,1)} %design.31.refs_0_), channel_id=1, source_target_pairs={{0,2},{3,1},{4,6},{7,5},{8,10},{11,9},{12,14},{15,13},{16,18},{19,... | collective-permute-start | bytes 1081352 | tf_op jit(solution)/shard_map/cond/branch_2_fun/ppermute | solution.py:290
  36.7 23.4 %collective-permute-start.44 = (bf16[10,128,128]{2,1,0:T(8,128)(2,1)}, bf16[10,128,128]{2,1,0:T(8,128)(2,1)}, u32[]{:S(2)}, u32[]{:S(2)}) collective-permute-start(bf16[10,128,128]{2,1,0:T(8,128)(2,1)} %design.33.refs_0_), channel_id=1, source_target_pairs={{0,1},{3,2},{1,0},{2,3},{4,5},{7,6},{5,4},{6,7},{8,9},{11,10},{9,8... | collective-permute-start | bytes 983048 | tf_op jit(solution)/shard_map/cond/branch_2_fun/ppermute | solution.py:290
  37.3 8.1 %collective-permute-start.34 = (bf16[2,128,128]{2,1,0:T(8,128)(2,1)}, bf16[2,128,128]{2,1,0:T(8,128)(2,1)S(1)}, u32[]{:S(2)}, u32[]{:S(2)}) collective-permute-start(bf16[2,128,128]{2,1,0:T(8,128)(2,1)} %slice.30), channel_id=1, source_target_pairs={{1,2},{2,1},{5,6},{6,5},{9,10},{10,9},{13,14},{14,13},{17,18},{18,... | collective-permute-start | bytes 196616 | tf_op jit(solution)/shard_map/cond/branch_2_fun/ppermute | solution.py:290
  38.0 10.0 %collective-permute-start.35 = (bf16[2,128,128]{2,1,0:T(8,128)(2,1)}, bf16[2,128,128]{2,1,0:T(8,128)(2,1)}, u32[]{:S(2)}, u32[]{:S(2)}) collective-permute-start(bf16[2,128,128]{2,1,0:T(8,128)(2,1)} %slice.30), channel_id=1, source_target_pairs={{0,2},{3,1},{1,0},{2,3},{4,6},{7,5},{5,4},{6,7},{8,10},{11,9},{9,8... | collective-permute-start | bytes 196616 | tf_op jit(solution)/shard_map/cond/branch_2_fun/ppermute | solution.py:290
  45.5 7.4 %copy-start.64 = (bf16[2,128,128]{2,1,0:T(8,128)(2,1)}, bf16[2,128,128]{2,1,0:T(8,128)(2,1)S(1)}, u32[]{:S(2)}) copy-start(bf16[2,128,128]{2,1,0:T(8,128)(2,1)S(1)} %collective-permute-done.34.refs_2_) | copy-start | bytes 196612 | tf_op jit(solution)/shard_map/cond
  45.5 18.2 %collective-permute-start.45 = (bf16[10,128,128]{2,1,0:T(8,128)(2,1)}, bf16[10,128,128]{2,1,0:T(8,128)(2,1)}, u32[]{:S(2)}, u32[]{:S(2)}) collective-permute-start(bf16[10,128,128]{2,1,0:T(8,128)(2,1)} %design.33.refs_0_), channel_id=1, source_target_pairs={{1,2},{2,1},{5,6},{6,5},{9,10},{10,9},{13,14},{14,13},{17,18},{18,... | collective-permute-start | bytes 983048 | tf_op jit(solution)/shard_map/cond/branch_2_fun/ppermute | solution.py:290
  48.0 15.7 %collective-permute-start.46 = (bf16[10,128,128]{2,1,0:T(8,128)(2,1)}, bf16[10,128,128]{2,1,0:T(8,128)(2,1)}, u32[]{:S(2)}, u32[]{:S(2)}) collective-permute-start(bf16[10,128,128]{2,1,0:T(8,128)(2,1)} %design.33.refs_0_), channel_id=1, source_target_pairs={{0,2},{3,1},{1,0},{2,3},{4,6},{7,5},{5,4},{6,7},{8,10},{11,9},{9,8... | collective-permute-start | bytes 983048 | tf_op jit(solution)/shard_map/cond/branch_2_fun/ppermute | solution.py:290
  51.5 1.4 %copy-start.55 = (bf16[4,128,128]{2,1,0:T(8,128)(2,1)}, bf16[4,128,128]{2,1,0:T(8,128)(2,1)S(1)}, u32[]{:S(2)}) copy-start(bf16[4,128,128]{2,1,0:T(8,128)(2,1)S(1)} %collective-permute-done.33.refs_1_) | copy-start | bytes 393220 | tf_op jit(solution)/shard_map/cond
  51.5 20.7 %collective-permute-start.40 = (bf16[11,128,128]{2,1,0:T(8,128)(2,1)}, bf16[11,128,128]{2,1,0:T(8,128)(2,1)}, u32[]{:S(2)}, u32[]{:S(2)}) collective-permute-start(bf16[11,128,128]{2,1,0:T(8,128)(2,1)} %design.30.refs_4_.refs_0_), channel_id=1, source_target_pairs={{1,2},{2,1},{5,6},{6,5},{9,10},{10,9},{13,14},{14,13},{17,18},{18,... | collective-permute-start | bytes 1081352 | tf_op jit(solution)/shard_map/cond/branch_2_fun/ppermute | solution.py:290
  59.0 13.8 %collective-permute-start.39 = (bf16[11,128,128]{2,1,0:T(8,128)(2,1)}, bf16[11,128,128]{2,1,0:T(8,128)(2,1)}, u32[]{:S(2)}, u32[]{:S(2)}) collective-permute-start(bf16[11,128,128]{2,1,0:T(8,128)(2,1)} %get-tuple-element.114), channel_id=1, source_target_pairs={{1,0},{2,3},{0,1},{3,2},{5,4},{6,7},{4,5},{7,6},{9,8},{10,11},{8,9... | collective-permute-start | bytes 1081352 | tf_op jit(solution)/shard_map/cond/branch_2_fun/ppermute | solution.py:290
  60.1 18.3 %collective-permute-start.41 = (bf16[11,128,128]{2,1,0:T(8,128)(2,1)}, bf16[11,128,128]{2,1,0:T(8,128)(2,1)}, u32[]{:S(2)}, u32[]{:S(2)}) collective-permute-start(bf16[11,128,128]{2,1,0:T(8,128)(2,1)} %get-tuple-element.115), channel_id=1, source_target_pairs={{1,0},{2,3},{0,2},{3,1},{5,4},{6,7},{4,6},{7,5},{9,8},{10,11},{8,1... | collective-permute-start | bytes 1081352 | tf_op jit(solution)/shard_map/cond/branch_2_fun/ppermute | solution.py:290
  67.8 17.5 %collective-permute-start.47 = (bf16[10,128,128]{2,1,0:T(8,128)(2,1)}, bf16[10,128,128]{2,1,0:T(8,128)(2,1)S(1)}, u32[]{:S(2)}, u32[]{:S(2)}) collective-permute-start(bf16[10,128,128]{2,1,0:T(8,128)(2,1)} %get-tuple-element.120), channel_id=1, source_target_pairs={{1,0},{2,3},{0,1},{3,2},{5,4},{6,7},{4,5},{7,6},{9,8},{10,11},{8,9... | collective-permute-start | bytes 983048 | tf_op jit(solution)/shard_map/cond/branch_2_fun/ppermute | solution.py:290
  71.3 20.9 %collective-permute-start.49 = (bf16[10,128,128]{2,1,0:T(8,128)(2,1)}, bf16[10,128,128]{2,1,0:T(8,128)(2,1)S(1)}, u32[]{:S(2)}, u32[]{:S(2)}) collective-permute-start(bf16[10,128,128]{2,1,0:T(8,128)(2,1)} %get-tuple-element.121), channel_id=1, source_target_pairs={{1,0},{2,3},{0,2},{3,1},{5,4},{6,7},{4,6},{7,5},{9,8},{10,11},{8,1... | collective-permute-start | bytes 983048 | tf_op jit(solution)/shard_map/cond/branch_2_fun/ppermute | solution.py:290
  72.1 12.6 %collective-permute-start.48 = (bf16[9,128,128]{2,1,0:T(8,128)(2,1)}, bf16[9,128,128]{2,1,0:T(8,128)(2,1)S(1)}, u32[]{:S(2)}, u32[]{:S(2)}) collective-permute-start(bf16[9,128,128]{2,1,0:T(8,128)(2,1)} %design.32.refs_4_.refs_0_), channel_id=1, source_target_pairs={{1,2},{2,1},{5,6},{6,5},{9,10},{10,9},{13,14},{14,13},{17,18},{18,... | collective-permute-start | bytes 884744 | tf_op jit(solution)/shard_map/cond/branch_2_fun/ppermute | solution.py:290
  82.5 37.6 %collective-permute-start.42 = (bf16[11,128,128]{2,1,0:T(8,128)(2,1)}, bf16[11,128,128]{2,1,0:T(8,128)(2,1)S(1)}, u32[]{:S(2)}, u32[]{:S(2)}) collective-permute-start(bf16[11,128,128]{2,1,0:T(8,128)(2,1)} %get-tuple-element.117), channel_id=1, source_target_pairs={{1,0},{2,3},{0,1},{3,2},{5,4},{6,7},{4,5},{7,6},{9,8},{10,11},{8,9... | collective-permute-start | bytes 1081352 | tf_op jit(solution)/shard_map/cond/branch_2_fun/ppermute | solution.py:290
  83.9 36.2 %collective-permute-start.43 = (bf16[11,128,128]{2,1,0:T(8,128)(2,1)}, bf16[11,128,128]{2,1,0:T(8,128)(2,1)S(1)}, u32[]{:S(2)}, u32[]{:S(2)}) collective-permute-start(bf16[11,128,128]{2,1,0:T(8,128)(2,1)} %get-tuple-element.118), channel_id=1, source_target_pairs={{1,0},{2,3},{0,2},{3,1},{5,4},{6,7},{4,6},{7,5},{9,8},{10,11},{8,1... | collective-permute-start | bytes 1081352 | tf_op jit(solution)/shard_map/cond/branch_2_fun/ppermute | solution.py:290
  84.8 7.5 %copy-start.45 = (bf16[9,128,128]{2,1,0:T(8,128)(2,1)}, bf16[9,128,128]{2,1,0:T(8,128)(2,1)S(1)}, u32[]{:S(2)}) copy-start(bf16[9,128,128]{2,1,0:T(8,128)(2,1)S(1)} %collective-permute-done.48.refs_2_) | copy-start | bytes 884740 | tf_op jit(solution)/shard_map/cond
  85.2 7.0 %copy-start.13 = (bf16[10,128,128]{2,1,0:T(8,128)(2,1)}, bf16[10,128,128]{2,1,0:T(8,128)(2,1)S(1)}, u32[]{:S(2)}) copy-start(bf16[10,128,128]{2,1,0:T(8,128)(2,1)S(1)} %collective-permute-done.47.refs_1_.high) | copy-start | bytes 983044 | tf_op jit(solution)/shard_map/cond
  92.3 0.7 copy-start.14
  96.7 16.0 %collective-permute-start.50 = (bf16[9,128,128]{2,1,0:T(8,128)(2,1)}, bf16[9,128,128]{2,1,0:T(8,128)(2,1)S(1)}, u32[]{:S(2)}, u32[]{:S(2)}) collective-permute-start(bf16[9,128,128]{2,1,0:T(8,128)(2,1)} %get-tuple-element.123), channel_id=1, source_target_pairs={{1,0},{2,3},{0,1},{3,2},{5,4},{6,7},{4,5},{7,6},{9,8},{10,11},{8,9... | collective-permute-start | bytes 884744 | tf_op jit(solution)/shard_map/cond/branch_2_fun/ppermute | solution.py:290
  98.1 17.8 %collective-permute-start.51 = (bf16[9,128,128]{2,1,0:T(8,128)(2,1)}, bf16[9,128,128]{2,1,0:T(8,128)(2,1)S(1)}, u32[]{:S(2)}, u32[]{:S(2)}) collective-permute-start(bf16[9,128,128]{2,1,0:T(8,128)(2,1)} %get-tuple-element.124), channel_id=1, source_target_pairs={{1,0},{2,3},{0,2},{3,1},{5,4},{6,7},{4,6},{7,5},{9,8},{10,11},{8,1... | collective-permute-start | bytes 884744 | tf_op jit(solution)/shard_map/cond/branch_2_fun/ppermute | solution.py:290
  112.7 3.2 %copy-start.48 = (bf16[9,128,128]{2,1,0:T(8,128)(2,1)}, bf16[9,128,128]{2,1,0:T(8,128)(2,1)S(1)}, u32[]{:S(2)}) copy-start(bf16[9,128,128]{2,1,0:T(8,128)(2,1)S(1)} %collective-permute-done.50.high) | copy-start | bytes 884740 | tf_op jit(solution)/shard_map/cond
  120.1 0.7 copy-start.36
  120.1 0.8 copy-start.37
  (3 other events, 2.1 us)

commit v5 on v4

--- a/solution.py
+++ b/solution.py
@@ -123,14 +123,16 @@
         output[place] = column.astype(jnp.bfloat16)
 
 
-def design_kernel(offset, listed, legendre, table, output):
-    def step(index, carry):
-        output[index] = design_tile(
-            listed[1, offset + index], listed[0, offset + index], legendre, table
-        )
-        return carry
-
-    lax.fori_loop(0, output.shape[0], step, 0)
+def design_kernel(offset, listed, legendre, table, *outputs):
+    for output in outputs:
+        def step(index, carry, output=output, offset=offset):
+            output[index] = design_tile(
+                listed[1, offset + index], listed[0, offset + index], legendre, table
+            )
+            return carry
+
+        lax.fori_loop(0, output.shape[0], step, 0)
+        offset += output.shape[0]
 
 
 def factor_kernel(inner, half, *refs):
@@ -331,12 +333,12 @@
     def sems(size):
         return pltpu.SemaphoreType.DMA((size,))
 
-    def design(offset, size, listed, values, table):
+    def design(offset, parts, listed, values, table):
         return pl.pallas_call(
             functools.partial(design_kernel, offset),
-            out_shape=tiles_of(size),
+            out_shape=[tiles_of(size) for size in parts],
             in_specs=[smem] + [vmem] * 2,
-            out_specs=vmem,
+            out_specs=[vmem] * len(parts),
             name="design",
         )(listed, values, table)
 
@@ -417,10 +419,11 @@
             nears, froms = streams_of(both, lambda x: x[:half], lambda x: x[half:], True)
             factor = collect(nears + froms)
             offsets = [sum(sizes[:k]) for k in range(len(sizes))]
-            designs = [
-                design(offset, size, listed, values, table)
-                for offset, size in zip(offsets, sizes)
-            ]
+            designs = []
+            while len(designs) < len(sizes):
+                k = len(designs)
+                parts = sizes[k : k + (2 if k == 1 else 1)]
+                designs += design(offsets[k], parts, listed, values, table)
             done = []
             for k, size in enumerate(sizes):
                 if k < 2 or not riding:

time: 126 us -> 130 us (1.032)
  waiting for transfers between devices: 26.9 us -> 32.5 us
  starting transfers between devices: 39.5 us -> 38 us
    ppermute x22, waiting for transfers between devices: 26.9 us -> 32.5 us  [shift(): return lax.ppermute(value, axis, pairs)]
    ppermute x22, starting transfers between devices: 39.5 us -> 38 us  [shift(): return lax.ppermute(value, axis, pairs)]
    pallas_call x4 -> x3, Pallas kernels: 11.9 us -> 10.6 us  [design(): pl.pallas_call(functools.partial(design_kernel, offset), out_shape=[tiles...]
    cond x22 -> x28, local copies, waits for them, and re-layouts: 2.29 us -> 3.05 us
  transfers between devices with their start and end apart: 22 -> 22, of which waited for: 8 -> 8; matrix products, arithmetic and copies ran while one was open for 1% -> 0% of each run, Pallas kernels for 36% -> 34%
where the time goes in v5:
time: 130 us; the launch traced here: 129 us
  Pallas kernels  50.6 us (39%)
  starting transfers between devices  38 us (29%)
  waiting for transfers between devices  32.5 us (25%)
  local copies, waits for them, and re-layouts  4.57 us (4%)
  between operations  1.33 us (1%)
    ppermute x22, starting transfers between devices, shift(): return lax.ppermute(value, axis, pairs)  38 us
    ppermute x22, waiting for transfers between devices, shift(): return lax.ppermute(value, axis, pairs)  32.5 us
    pallas_call x4, Pallas kernels, multiply(): pl.pallas_call(functools.partial(product_kernel, len(streams)), out_shape...  16.3 us
    pallas_call x4, Pallas kernels, update(): pl.pallas_call(functools.partial(update_kernel, offset), in_specs=[smem]...  14.3 us
    pallas_call x3, Pallas kernels, design(): pl.pallas_call(functools.partial(design_kernel, offset), out_shape=[tiles...  10.6 us
    pallas_call x1, Pallas kernels, copy_rest(): pl.pallas_call(functools.partial(copy_kernel, offset), in_specs=[smem, an...  4.44 us
    pallas_call x1, Pallas kernels, per_device(): pl.pallas_call(functools.partial(plan_kernel, counts, row_count), out_sha...  3.2 us
    cond x28, local copies, waits for them, and re-layouts  3.05 us
  transfers between devices with their start and end apart: 22, of which 8 were waited for; matrix products, arithmetic and copies ran while one was open for 0% of the time, Pallas kernels for 34%

profile of v5, /device:TPU:0, one launch (start us, length us, event | category | flops | bytes accessed | tf_op | source)
XLA Modules:
  0.0 128.8 jit_solution(5164124670926221856)
XLA Ops:
  2.4 3.2 %plan.1 = (s32[8,128]{1,0:T(8,128)S(1)}, s32[1,128]{1,0:T(1,128)}, bf16[4,128,128]{2,1,0:T(8,128)(2,1)S(1)}) custom-call(s32[1]{0:T(128)S(6)} %copy.79.slab_start, f32[8]{0:T(128)} %span_weight.1, s32[712]{0:T(1024)} %order.1, f32[512]{0:T(512)} %obs_weight.1, s32[512]{0:T(512)} %span_of.1, bf16[4,89,32,128]{3,2,1,0:T(8,128)(2,1)} %bitcast.40, ...), custom_call_target="tpu_custom_call" | custom-call | tf_op jit(solution)/shard_map/plan/pallas_call | solution.py:345
  6.3 121.8 %conditional.1 = (f32[89,1,1,128,128]{4,3,2,1,0:T(8,128)}) conditional(s32[]{:T(128)} %bitcast.22, (bf16[4,128,128]{2,1,0:T(8,128)(2,1)S(1)}, s32[8,128]{1,0:T(8,128)S(1)}, bf16[4,89,32,128]{3,2,1,0:T(8,128)(2,1)}, f32[4,128,128]{2,1,0:T(8,128)S(1)}, f32[89,128,128]{2,1,0:T(8,128)}, /*index=5*/s32[1]{0:T(128)}) %tuple.55, ...), branch_computations={%region_0.1_spmd, %region_1.2_spmd, %region_2.3_spmd, %region_3.4_... | conditional | flops 196608 | bytes 70518320 | solution.py:449
  6.9 5.3 %design.25 = (bf16[11,128,128]{2,1,0:T(8,128)(2,1)}, bf16[9,128,128]{2,1,0:T(8,128)(2,1)}) custom-call(s32[8,128]{1,0:T(8,128)S(1)} %get-tuple-element.111.listed, bf16[4,89,32,128]{3,2,1,0:T(8,128)(2,1)} %get-tuple-element.114.legendre, f32[4,128,128]{2,1,0:T(8,128)S(1)} %get-tuple-element.115.table), custom_call_target="tpu_custom_call" | custom-call | tf_op jit(solution)/shard_map/cond/branch_2_fun/design/pallas_call | solution.py:337
  12.2 5.1 %collective-permute-start.36 = (bf16[11,128,128]{2,1,0:T(8,128)(2,1)}, bf16[11,128,128]{2,1,0:T(8,128)(2,1)}, u32[]{:S(2)}, u32[]{:S(2)}) collective-permute-start(bf16[11,128,128]{2,1,0:T(8,128)(2,1)} %get-tuple-element.116.refs_0_), channel_id=1, source_target_pairs={{0,1},{3,2},{4,5},{7,6},{8,9},{11,10},{12,13},{15,14},{16,17},{19,... | collective-permute-start | bytes 1081352 | tf_op jit(solution)/shard_map/cond/branch_2_fun/ppermute | solution.py:292
  20.3 4.1 %collective-permute-done.31 = bf16[4,128,128]{2,1,0:T(8,128)(2,1)S(1)} collective-permute-done((bf16[4,128,128]{2,1,0:T(8,128)(2,1)S(1)}, bf16[4,128,128]{2,1,0:T(8,128)(2,1)S(1)}, u32[]{:S(2)}, u32[]{:S(2)}) %collective-permute-start.31) | collective-permute-done | bytes 131104 | tf_op jit(solution)/shard_map/cond/branch_2_fun/ppermute | solution.py:292
  24.4 1.6 %collective-permute-start.32 = (bf16[4,128,128]{2,1,0:T(8,128)(2,1)S(1)}, bf16[4,128,128]{2,1,0:T(8,128)(2,1)S(1)}, u32[]{:S(2)}, u32[]{:S(2)}) collective-permute-start(bf16[4,128,128]{2,1,0:T(8,128)(2,1)S(1)} %add.59), channel_id=1, source_target_pairs={{0,16},{4,20},{8,24},{12,28},{16,0},{20,4},{24,8},{28,12},{1,17},{... | collective-permute-start | bytes 393224 | tf_op jit(solution)/shard_map/cond/branch_2_fun/ppermute | solution.py:292
  26.0 3.4 %collective-permute-done.32 = bf16[4,128,128]{2,1,0:T(8,128)(2,1)S(1)} collective-permute-done((bf16[4,128,128]{2,1,0:T(8,128)(2,1)S(1)}, bf16[4,128,128]{2,1,0:T(8,128)(2,1)S(1)}, u32[]{:S(2)}, u32[]{:S(2)}) %collective-permute-start.32) | collective-permute-done | bytes 131104 | tf_op jit(solution)/shard_map/cond/branch_2_fun/ppermute | solution.py:292
  30.3 4.9 %collective-permute-start.38 = (bf16[11,128,128]{2,1,0:T(8,128)(2,1)}, bf16[11,128,128]{2,1,0:T(8,128)(2,1)}, u32[]{:S(2)}, u32[]{:S(2)}) collective-permute-start(bf16[11,128,128]{2,1,0:T(8,128)(2,1)} %get-tuple-element.116.refs_0_), channel_id=1, source_target_pairs={{0,2},{3,1},{4,6},{7,5},{8,10},{11,9},{12,14},{15,13},{16,18},{19,... | collective-permute-start | bytes 1081352 | tf_op jit(solution)/shard_map/cond/branch_2_fun/ppermute | solution.py:292
  35.2 2.6 %design.26.refs_0_ = bf16[10,128,128]{2,1,0:T(8,128)(2,1)} custom-call(s32[8,128]{1,0:T(8,128)S(1)} %get-tuple-element.111.listed, bf16[4,89,32,128]{3,2,1,0:T(8,128)(2,1)S(1)} %copy-done.3, f32[4,128,128]{2,1,0:T(8,128)S(1)} %get-tuple-element.115.table), custom_call_target="tpu_custom_call" | custom-call | tf_op jit(solution)/shard_map/cond/branch_2_fun/design/pallas_call | solution.py:337
  38.5 4.8 %collective-permute-start.35 = (bf16[2,128,128]{2,1,0:T(8,128)(2,1)S(1)}, bf16[2,128,128]{2,1,0:T(8,128)(2,1)}, u32[]{:S(2)}, u32[]{:S(2)}) collective-permute-start(bf16[2,128,128]{2,1,0:T(8,128)(2,1)S(1)} %slice.30), channel_id=1, source_target_pairs={{0,2},{3,1},{1,0},{2,3},{4,6},{7,5},{5,4},{6,7},{8,10},{11,9},{9,8... | collective-permute-start | bytes 196616 | tf_op jit(solution)/shard_map/cond/branch_2_fun/ppermute | solution.py:292
  44.7 4.3 %collective-permute-done.35.refs_3_ = bf16[2,128,128]{2,1,0:T(8,128)(2,1)} collective-permute-done((bf16[2,128,128]{2,1,0:T(8,128)(2,1)S(1)}, bf16[2,128,128]{2,1,0:T(8,128)(2,1)}, u32[]{:S(2)}, u32[]{:S(2)}) %collective-permute-start.35) | collective-permute-done | bytes 65568 | tf_op jit(solution)/shard_map/cond/branch_2_fun/ppermute | solution.py:292
  49.0 3.6 %collective-permute-start.46 = (bf16[10,128,128]{2,1,0:T(8,128)(2,1)}, bf16[10,128,128]{2,1,0:T(8,128)(2,1)}, u32[]{:S(2)}, u32[]{:S(2)}) collective-permute-start(bf16[10,128,128]{2,1,0:T(8,128)(2,1)} %design.26.refs_0_), channel_id=1, source_target_pairs={{0,2},{3,1},{1,0},{2,3},{4,6},{7,5},{5,4},{6,7},{8,10},{11,9},{9,8... | collective-permute-start | bytes 983048 | tf_op jit(solution)/shard_map/cond/branch_2_fun/ppermute | solution.py:292
  52.5 2.7 %design.24.refs_4_.refs_0_ = bf16[11,128,128]{2,1,0:T(8,128)(2,1)} custom-call(s32[8,128]{1,0:T(8,128)S(1)} %get-tuple-element.111.listed, bf16[4,89,32,128]{3,2,1,0:T(8,128)(2,1)S(1)} %copy-done.3, f32[4,128,128]{2,1,0:T(8,128)S(1)} %get-tuple-element.115.table), custom_call_target="tpu_custom_call" | custom-call | tf_op jit(solution)/shard_map/cond/branch_2_fun/design/pallas_call | solution.py:337
  55.9 1.7 %factor.8 = bf16[512,256]{1,0:T(8,128)(2,1)} custom-call(bf16[4,128,128]{2,1,0:T(8,128)(2,1)} %copy-done.19, bf16[4,128,128]{2,1,0:T(8,128)(2,1)} %copy-done.62, bf16[2,128,128]{2,1,0:T(8,128)(2,1)} %copy-done.71, bf16[2,128,128]{2,1,0:T(8,128)(2,1)} %collective-permute-done.35.refs_3_), custom_call_target="tpu_custom_call" | custom-call | tf_op jit(solution)/shard_map/cond/branch_2_fun/factor/pallas_call | solution.py:358
  57.7 4.3 %product.30 = (f32[11,128,128]{2,1,0:T(8,128)}, bf16[11,128,128]{2,1,0:T(8,128)(2,1)}, bf16[11,128,128]{2,1,0:T(8,128)(2,1)}) custom-call(bf16[512,256]{1,0:T(8,128)(2,1)} %factor.8, bf16[11,128,128]{2,1,0:T(8,128)(2,1)} %get-tuple-element.116.refs_0_, bf16[11,128,128]{2,1,0:T(8,128)(2,1)} %collective-permute-done.36.refs_1_, ...), custom_call_target="tpu_custom_call" | custom-call | tf_op jit(solution)/shard_map/cond/branch_2_fun/product/pallas_call | solution.py:381
  62.0 1.7 %collective-permute-start.39 = (bf16[11,128,128]{2,1,0:T(8,128)(2,1)}, bf16[11,128,128]{2,1,0:T(8,128)(2,1)S(1)}, u32[]{:S(2)}, u32[]{:S(2)}) collective-permute-start(bf16[11,128,128]{2,1,0:T(8,128)(2,1)} %get-tuple-element.117), channel_id=1, source_target_pairs={{1,0},{2,3},{0,1},{3,2},{5,4},{6,7},{4,5},{7,6},{9,8},{10,11},{8,9... | collective-permute-start | bytes 1081352 | tf_op jit(solution)/shard_map/cond/branch_2_fun/ppermute | solution.py:292
  64.3 4.1 %product.32 = (f32[10,128,128]{2,1,0:T(8,128)}, bf16[10,128,128]{2,1,0:T(8,128)(2,1)}, bf16[10,128,128]{2,1,0:T(8,128)(2,1)}) custom-call(bf16[512,256]{1,0:T(8,128)(2,1)} %factor.8, bf16[10,128,128]{2,1,0:T(8,128)(2,1)} %design.26.refs_0_, bf16[10,128,128]{2,1,0:T(8,128)(2,1)} %collective-permute-done.44.refs_1_, ...), custom_call_target="tpu_custom_call" | custom-call | tf_op jit(solution)/shard_map/cond/branch_2_fun/product/pallas_call | solution.py:381
  68.4 1.7 %collective-permute-start.47 = (bf16[10,128,128]{2,1,0:T(8,128)(2,1)}, bf16[10,128,128]{2,1,0:T(8,128)(2,1)S(1)}, u32[]{:S(2)}, u32[]{:S(2)}) collective-permute-start(bf16[10,128,128]{2,1,0:T(8,128)(2,1)} %get-tuple-element.124), channel_id=1, source_target_pairs={{1,0},{2,3},{0,1},{3,2},{5,4},{6,7},{4,5},{7,6},{9,8},{10,11},{8,9... | collective-permute-start | bytes 983048 | tf_op jit(solution)/shard_map/cond/branch_2_fun/ppermute | solution.py:292
  71.7 1.8 %collective-permute-done.39.refs_1_.high = bf16[11,128,128]{2,1,0:T(8,128)(2,1)S(1)} collective-permute-done((bf16[11,128,128]{2,1,0:T(8,128)(2,1)}, bf16[11,128,128]{2,1,0:T(8,128)(2,1)S(1)}, u32[]{:S(2)}, u32[]{:S(2)}) %collective-permute-start.39) | collective-permute-done | bytes 360480 | tf_op jit(solution)/shard_map/cond/branch_2_fun/ppermute | solution.py:292
  73.5 7.7 %collective-permute-done.41.refs_3_.low = bf16[11,128,128]{2,1,0:T(8,128)(2,1)S(1)} collective-permute-done((bf16[11,128,128]{2,1,0:T(8,128)(2,1)}, bf16[11,128,128]{2,1,0:T(8,128)(2,1)S(1)}, u32[]{:S(2)}, u32[]{:S(2)}) %collective-permute-start.41) | collective-permute-done | bytes 360480 | tf_op jit(solution)/shard_map/cond/branch_2_fun/ppermute | solution.py:292
  82.0 4.2 %product.31 = (f32[11,128,128]{2,1,0:T(8,128)}, bf16[11,128,128]{2,1,0:T(8,128)(2,1)}, bf16[11,128,128]{2,1,0:T(8,128)(2,1)}) custom-call(bf16[512,256]{1,0:T(8,128)(2,1)} %factor.8, bf16[11,128,128]{2,1,0:T(8,128)(2,1)} %design.24.refs_4_.refs_0_, bf16[11,128,128]{2,1,0:T(8,128)(2,1)} %copy-done.9, bf16[11,128,128]{2,1,0:T(8,128)(2,1)} %copy-done.35, ...), custom_call_target="tpu_custom_call" | custom-call | tf_op jit(solution)/shard_map/cond/branch_2_fun/product/pallas_call | solution.py:381
  86.2 2.1 %collective-permute-start.42 = (bf16[11,128,128]{2,1,0:T(8,128)(2,1)}, bf16[11,128,128]{2,1,0:T(8,128)(2,1)S(1)}, u32[]{:S(2)}, u32[]{:S(2)}) collective-permute-start(bf16[11,128,128]{2,1,0:T(8,128)(2,1)} %get-tuple-element.120), channel_id=1, source_target_pairs={{1,0},{2,3},{0,1},{3,2},{5,4},{6,7},{4,5},{7,6},{9,8},{10,11},{8,9... | collective-permute-start | bytes 1081352 | tf_op jit(solution)/shard_map/cond/branch_2_fun/ppermute | solution.py:292
  88.9 6.4 %collective-permute-done.49.refs_3_.low = bf16[10,128,128]{2,1,0:T(8,128)(2,1)S(1)} collective-permute-done((bf16[10,128,128]{2,1,0:T(8,128)(2,1)}, bf16[10,128,128]{2,1,0:T(8,128)(2,1)S(1)}, u32[]{:S(2)}, u32[]{:S(2)}) %collective-permute-start.49) | collective-permute-done | bytes 327712 | tf_op jit(solution)/shard_map/cond/branch_2_fun/ppermute | solution.py:292
  96.0 3.8 %product.33 = (f32[9,128,128]{2,1,0:T(8,128)}, bf16[9,128,128]{2,1,0:T(8,128)(2,1)}, bf16[9,128,128]{2,1,0:T(8,128)(2,1)}) custom-call(bf16[512,256]{1,0:T(8,128)(2,1)} %factor.8, bf16[9,128,128]{2,1,0:T(8,128)(2,1)} %get-tuple-element.123.refs_4_.refs_0_, bf16[10,128,128]{2,1,0:T(8,128)(2,1)} %copy-done.15, bf16[9,128,128]{2,1,0:T(8,128)(2,1)} %copy-done.50, ...), custom_call_target="tpu_custom_call" | custom-call | tf_op jit(solution)/shard_map/cond/branch_2_fun/product/pallas_call | solution.py:381
  99.8 2.0 %collective-permute-start.50 = (bf16[9,128,128]{2,1,0:T(8,128)(2,1)}, bf16[9,128,128]{2,1,0:T(8,128)(2,1)S(1)}, u32[]{:S(2)}, u32[]{:S(2)}) collective-permute-start(bf16[9,128,128]{2,1,0:T(8,128)(2,1)} %get-tuple-element.127), channel_id=1, source_target_pairs={{1,0},{2,3},{0,1},{3,2},{5,4},{6,7},{4,5},{7,6},{9,8},{10,11},{8,9... | collective-permute-start | bytes 884744 | tf_op jit(solution)/shard_map/cond/branch_2_fun/ppermute | solution.py:292
  102.5 4.4 %branch_2_fun.1.refs_0_ = f32[89,128,128]{2,1,0:T(8,128)} custom-call(s32[8,128]{1,0:T(8,128)S(1)} %get-tuple-element.111.listed, f32[89,128,128]{2,1,0:T(8,128)} %get-tuple-element.122.resident), custom_call_target="tpu_custom_call" | custom-call | tf_op jit(solution)/shard_map/cond/branch_2_fun/pallas_call | solution.py:370
  106.9 3.6 %update.30.refs_0_ = f32[89,128,128]{2,1,0:T(8,128)} custom-call(s32[8,128]{1,0:T(8,128)S(1)} %get-tuple-element.111.listed, s32[1]{0:T(128)} %get-tuple-element.112.slab_start, f32[10,128,128]{2,1,0:T(8,128)} %get-tuple-element.130.own, bf16[10,128,128]{2,1,0:T(8,128)(2,1)} %copy-done.15, ...), custom_call_target="tpu_custom_call", output_to_operand_aliasing={{}: (6, {})} | custom-call | tf_op jit(solution)/shard_map/cond/branch_2_fun/update/pallas_call | solution.py:396
  110.5 3.6 %update.31.refs_0_ = f32[89,128,128]{2,1,0:T(8,128)} custom-call(s32[8,128]{1,0:T(8,128)S(1)} %get-tuple-element.111.listed, s32[1]{0:T(128)} %get-tuple-element.112.slab_start, f32[11,128,128]{2,1,0:T(8,128)} %get-tuple-element.129.own, bf16[11,128,128]{2,1,0:T(8,128)(2,1)} %copy-done.9, ...), custom_call_target="tpu_custom_call", output_to_operand_aliasing={{}: (6, {})} | custom-call | tf_op jit(solution)/shard_map/cond/branch_2_fun/update/pallas_call | solution.py:396
  114.1 1.6 %collective-permute-done.50.high = bf16[9,128,128]{2,1,0:T(8,128)(2,1)S(1)} collective-permute-done((bf16[9,128,128]{2,1,0:T(8,128)(2,1)}, bf16[9,128,128]{2,1,0:T(8,128)(2,1)S(1)}, u32[]{:S(2)}, u32[]{:S(2)}) %collective-permute-start.50) | collective-permute-done | bytes 294944 | tf_op jit(solution)/shard_map/cond/branch_2_fun/ppermute | solution.py:292
  115.7 3.2 %collective-permute-done.51.low = bf16[9,128,128]{2,1,0:T(8,128)(2,1)S(1)} collective-permute-done((bf16[9,128,128]{2,1,0:T(8,128)(2,1)}, bf16[9,128,128]{2,1,0:T(8,128)(2,1)S(1)}, u32[]{:S(2)}, u32[]{:S(2)}) %collective-permute-start.51) | collective-permute-done | bytes 294944 | tf_op jit(solution)/shard_map/cond/branch_2_fun/ppermute | solution.py:292
  119.6 3.5 %update.32.refs_0_ = f32[89,128,128]{2,1,0:T(8,128)} custom-call(s32[8,128]{1,0:T(8,128)S(1)} %get-tuple-element.111.listed, s32[1]{0:T(128)} %get-tuple-element.112.slab_start, f32[9,128,128]{2,1,0:T(8,128)} %get-tuple-element.126.own, bf16[9,128,128]{2,1,0:T(8,128)(2,1)} %copy-done.53, ...), custom_call_target="tpu_custom_call", output_to_operand_aliasing={{}: (6, {})} | custom-call | tf_op jit(solution)/shard_map/cond/branch_2_fun/update/pallas_call | solution.py:396
  124.0 3.6 %update.33 = f32[89,128,128]{2,1,0:T(8,128)} custom-call(s32[8,128]{1,0:T(8,128)S(1)} %get-tuple-element.111.listed, s32[1]{0:T(128)} %get-tuple-element.112.slab_start, f32[11,128,128]{2,1,0:T(8,128)} %get-tuple-element.119.own, bf16[11,128,128]{2,1,0:T(8,128)(2,1)} %copy-done.38, bf16[11,128,128]{2,1,0:T(8,128)(2,1)} %copy-done.39, ...), custom_call_target="tpu_custom_call", output_to_operand_aliasing={{}: (6, {})} | custom-call | tf_op jit(solution)/shard_map/cond/branch_2_fun/update/pallas_call | solution.py:396
  (67 shorter events, 16.2 us)
Async XLA Ops:
  6.3 28.9 %copy-start.3 = (bf16[4,89,32,128]{3,2,1,0:T(8,128)(2,1)S(1)}, bf16[4,89,32,128]{3,2,1,0:T(8,128)(2,1)}, u32[]{:S(2)}) copy-start(bf16[4,89,32,128]{3,2,1,0:T(8,128)(2,1)} %get-tuple-element.114.legendre) | copy-start | bytes 8749060 | tf_op jit(solution)/shard_map/cond
  6.3 12.3 %collective-permute-start.30 = (bf16[4,128,128]{2,1,0:T(8,128)(2,1)S(1)}, bf16[4,128,128]{2,1,0:T(8,128)(2,1)S(1)}, u32[]{:S(2)}, u32[]{:S(2)}) collective-permute-start(bf16[4,128,128]{2,1,0:T(8,128)(2,1)S(1)} %get-tuple-element.113), channel_id=1, source_target_pairs={{0,4},{4,0},{8,12},{12,8},{16,20},{20,16},{24,28},{28,24},{1,5},{5... | collective-permute-start | bytes 393224 | tf_op jit(solution)/shard_map/cond/branch_2_fun/ppermute | solution.py:292
  12.2 25.6 %collective-permute-start.36 = (bf16[11,128,128]{2,1,0:T(8,128)(2,1)}, bf16[11,128,128]{2,1,0:T(8,128)(2,1)}, u32[]{:S(2)}, u32[]{:S(2)}) collective-permute-start(bf16[11,128,128]{2,1,0:T(8,128)(2,1)} %get-tuple-element.116.refs_0_), channel_id=1, source_target_pairs={{0,1},{3,2},{4,5},{7,6},{8,9},{11,10},{12,13},{15,14},{16,17},{19,... | collective-permute-start | bytes 1081352 | tf_op jit(solution)/shard_map/cond/branch_2_fun/ppermute | solution.py:292
  17.3 21.2 %collective-permute-start.37 = (bf16[11,128,128]{2,1,0:T(8,128)(2,1)}, bf16[11,128,128]{2,1,0:T(8,128)(2,1)}, u32[]{:S(2)}, u32[]{:S(2)}) collective-permute-start(bf16[11,128,128]{2,1,0:T(8,128)(2,1)} %get-tuple-element.116.refs_0_), channel_id=1, source_target_pairs={{1,2},{2,1},{5,6},{6,5},{9,10},{10,9},{13,14},{14,13},{17,18},{18,... | collective-permute-start | bytes 1081352 | tf_op jit(solution)/shard_map/cond/branch_2_fun/ppermute | solution.py:292
  18.7 5.7 %collective-permute-start.31 = (bf16[4,128,128]{2,1,0:T(8,128)(2,1)S(1)}, bf16[4,128,128]{2,1,0:T(8,128)(2,1)S(1)}, u32[]{:S(2)}, u32[]{:S(2)}) collective-permute-start(bf16[4,128,128]{2,1,0:T(8,128)(2,1)S(1)} %add.58), channel_id=1, source_target_pairs={{0,8},{4,12},{8,0},{12,4},{16,24},{20,28},{24,16},{28,20},{1,9},{5... | collective-permute-start | bytes 393224 | tf_op jit(solution)/shard_map/cond/branch_2_fun/ppermute | solution.py:292
  24.4 5.0 %collective-permute-start.32 = (bf16[4,128,128]{2,1,0:T(8,128)(2,1)S(1)}, bf16[4,128,128]{2,1,0:T(8,128)(2,1)S(1)}, u32[]{:S(2)}, u32[]{:S(2)}) collective-permute-start(bf16[4,128,128]{2,1,0:T(8,128)(2,1)S(1)} %add.59), channel_id=1, source_target_pairs={{0,16},{4,20},{8,24},{12,28},{16,0},{20,4},{24,8},{28,12},{1,17},{... | collective-permute-start | bytes 393224 | tf_op jit(solution)/shard_map/cond/branch_2_fun/ppermute | solution.py:292
  29.5 26.4 %copy-start.19 = (bf16[4,128,128]{2,1,0:T(8,128)(2,1)}, bf16[4,128,128]{2,1,0:T(8,128)(2,1)S(1)}, u32[]{:S(2)}) copy-start(bf16[4,128,128]{2,1,0:T(8,128)(2,1)S(1)} %add.60.refs_0_) | copy-start | bytes 393220 | tf_op jit(solution)/shard_map/cond
  29.5 25.7 %collective-permute-start.33 = (bf16[4,128,128]{2,1,0:T(8,128)(2,1)S(1)}, bf16[4,128,128]{2,1,0:T(8,128)(2,1)S(1)}, u32[]{:S(2)}, u32[]{:S(2)}) collective-permute-start(bf16[4,128,128]{2,1,0:T(8,128)(2,1)S(1)} %add.60.refs_0_), channel_id=1, source_target_pairs={{0,1},{3,2},{1,0},{2,3},{4,5},{7,6},{5,4},{6,7},{8,9},{11,10},{9,8... | collective-permute-start | bytes 393224 | tf_op jit(solution)/shard_map/cond/branch_2_fun/ppermute | solution.py:292
  30.3 27.4 %collective-permute-start.38 = (bf16[11,128,128]{2,1,0:T(8,128)(2,1)}, bf16[11,128,128]{2,1,0:T(8,128)(2,1)}, u32[]{:S(2)}, u32[]{:S(2)}) collective-permute-start(bf16[11,128,128]{2,1,0:T(8,128)(2,1)} %get-tuple-element.116.refs_0_), channel_id=1, source_target_pairs={{0,2},{3,1},{4,6},{7,5},{8,10},{11,9},{12,14},{15,13},{16,18},{19,... | collective-permute-start | bytes 1081352 | tf_op jit(solution)/shard_map/cond/branch_2_fun/ppermute | solution.py:292
  37.8 25.9 %collective-permute-start.44 = (bf16[10,128,128]{2,1,0:T(8,128)(2,1)}, bf16[10,128,128]{2,1,0:T(8,128)(2,1)}, u32[]{:S(2)}, u32[]{:S(2)}) collective-permute-start(bf16[10,128,128]{2,1,0:T(8,128)(2,1)} %design.26.refs_0_), channel_id=1, source_target_pairs={{0,1},{3,2},{1,0},{2,3},{4,5},{7,6},{5,4},{6,7},{8,9},{11,10},{9,8... | collective-permute-start | bytes 983048 | tf_op jit(solution)/shard_map/cond/branch_2_fun/ppermute | solution.py:292
  37.8 5.5 %collective-permute-start.34 = (bf16[2,128,128]{2,1,0:T(8,128)(2,1)S(1)}, bf16[2,128,128]{2,1,0:T(8,128)(2,1)S(1)}, u32[]{:S(2)}, u32[]{:S(2)}) collective-permute-start(bf16[2,128,128]{2,1,0:T(8,128)(2,1)S(1)} %slice.30), channel_id=1, source_target_pairs={{1,2},{2,1},{5,6},{6,5},{9,10},{10,9},{13,14},{14,13},{17,18},{18,... | collective-permute-start | bytes 196616 | tf_op jit(solution)/shard_map/cond/branch_2_fun/ppermute | solution.py:292
  38.5 10.4 %collective-permute-start.35 = (bf16[2,128,128]{2,1,0:T(8,128)(2,1)S(1)}, bf16[2,128,128]{2,1,0:T(8,128)(2,1)}, u32[]{:S(2)}, u32[]{:S(2)}) collective-permute-start(bf16[2,128,128]{2,1,0:T(8,128)(2,1)S(1)} %slice.30), channel_id=1, source_target_pairs={{0,2},{3,1},{1,0},{2,3},{4,6},{7,5},{5,4},{6,7},{8,10},{11,9},{9,8... | collective-permute-start | bytes 196616 | tf_op jit(solution)/shard_map/cond/branch_2_fun/ppermute | solution.py:292
  43.3 12.6 %copy-start.71 = (bf16[2,128,128]{2,1,0:T(8,128)(2,1)}, bf16[2,128,128]{2,1,0:T(8,128)(2,1)S(1)}, u32[]{:S(2)}) copy-start(bf16[2,128,128]{2,1,0:T(8,128)(2,1)S(1)} %collective-permute-done.34.refs_2_) | copy-start | bytes 196612 | tf_op jit(solution)/shard_map/cond
  43.3 21.0 %collective-permute-start.45 = (bf16[10,128,128]{2,1,0:T(8,128)(2,1)}, bf16[10,128,128]{2,1,0:T(8,128)(2,1)}, u32[]{:S(2)}, u32[]{:S(2)}) collective-permute-start(bf16[10,128,128]{2,1,0:T(8,128)(2,1)} %design.26.refs_0_), channel_id=1, source_target_pairs={{1,2},{2,1},{5,6},{6,5},{9,10},{10,9},{13,14},{14,13},{17,18},{18,... | collective-permute-start | bytes 983048 | tf_op jit(solution)/shard_map/cond/branch_2_fun/ppermute | solution.py:292
  49.0 15.4 %collective-permute-start.46 = (bf16[10,128,128]{2,1,0:T(8,128)(2,1)}, bf16[10,128,128]{2,1,0:T(8,128)(2,1)}, u32[]{:S(2)}, u32[]{:S(2)}) collective-permute-start(bf16[10,128,128]{2,1,0:T(8,128)(2,1)} %design.26.refs_0_), channel_id=1, source_target_pairs={{0,2},{3,1},{1,0},{2,3},{4,6},{7,5},{5,4},{6,7},{8,10},{11,9},{9,8... | collective-permute-start | bytes 983048 | tf_op jit(solution)/shard_map/cond/branch_2_fun/ppermute | solution.py:292
  55.2 15.8 %collective-permute-start.40 = (bf16[11,128,128]{2,1,0:T(8,128)(2,1)}, bf16[11,128,128]{2,1,0:T(8,128)(2,1)S(1)}, u32[]{:S(2)}, u32[]{:S(2)}) collective-permute-start(bf16[11,128,128]{2,1,0:T(8,128)(2,1)} %design.24.refs_4_.refs_0_), channel_id=1, source_target_pairs={{1,2},{2,1},{5,6},{6,5},{9,10},{10,9},{13,14},{14,13},{17,18},{18,... | collective-permute-start | bytes 1081352 | tf_op jit(solution)/shard_map/cond/branch_2_fun/ppermute | solution.py:292
  62.0 11.5 %collective-permute-start.39 = (bf16[11,128,128]{2,1,0:T(8,128)(2,1)}, bf16[11,128,128]{2,1,0:T(8,128)(2,1)S(1)}, u32[]{:S(2)}, u32[]{:S(2)}) collective-permute-start(bf16[11,128,128]{2,1,0:T(8,128)(2,1)} %get-tuple-element.117), channel_id=1, source_target_pairs={{1,0},{2,3},{0,1},{3,2},{5,4},{6,7},{4,5},{7,6},{9,8},{10,11},{8,9... | collective-permute-start | bytes 1081352 | tf_op jit(solution)/shard_map/cond/branch_2_fun/ppermute | solution.py:292
  63.8 17.5 %collective-permute-start.41 = (bf16[11,128,128]{2,1,0:T(8,128)(2,1)}, bf16[11,128,128]{2,1,0:T(8,128)(2,1)S(1)}, u32[]{:S(2)}, u32[]{:S(2)}) collective-permute-start(bf16[11,128,128]{2,1,0:T(8,128)(2,1)} %get-tuple-element.118), channel_id=1, source_target_pairs={{1,0},{2,3},{0,2},{3,1},{5,4},{6,7},{4,6},{7,5},{9,8},{10,11},{8,1... | collective-permute-start | bytes 1081352 | tf_op jit(solution)/shard_map/cond/branch_2_fun/ppermute | solution.py:292
  68.4 20.5 %collective-permute-start.47 = (bf16[10,128,128]{2,1,0:T(8,128)(2,1)}, bf16[10,128,128]{2,1,0:T(8,128)(2,1)S(1)}, u32[]{:S(2)}, u32[]{:S(2)}) collective-permute-start(bf16[10,128,128]{2,1,0:T(8,128)(2,1)} %get-tuple-element.124), channel_id=1, source_target_pairs={{1,0},{2,3},{0,1},{3,2},{5,4},{6,7},{4,5},{7,6},{9,8},{10,11},{8,9... | collective-permute-start | bytes 983048 | tf_op jit(solution)/shard_map/cond/branch_2_fun/ppermute | solution.py:292
  70.1 25.2 %collective-permute-start.49 = (bf16[10,128,128]{2,1,0:T(8,128)(2,1)}, bf16[10,128,128]{2,1,0:T(8,128)(2,1)S(1)}, u32[]{:S(2)}, u32[]{:S(2)}) collective-permute-start(bf16[10,128,128]{2,1,0:T(8,128)(2,1)} %get-tuple-element.125), channel_id=1, source_target_pairs={{1,0},{2,3},{0,2},{3,1},{5,4},{6,7},{4,6},{7,5},{9,8},{10,11},{8,1... | collective-permute-start | bytes 983048 | tf_op jit(solution)/shard_map/cond/branch_2_fun/ppermute | solution.py:292
  71.1 10.2 %copy-start.35 = (bf16[11,128,128]{2,1,0:T(8,128)(2,1)}, bf16[11,128,128]{2,1,0:T(8,128)(2,1)S(1)}, u32[]{:S(2)}) copy-start(bf16[11,128,128]{2,1,0:T(8,128)(2,1)S(1)} %collective-permute-done.40.refs_2_) | copy-start | bytes 1081348 | tf_op jit(solution)/shard_map/cond
  71.1 17.8 %collective-permute-start.48 = (bf16[9,128,128]{2,1,0:T(8,128)(2,1)}, bf16[9,128,128]{2,1,0:T(8,128)(2,1)S(1)}, u32[]{:S(2)}, u32[]{:S(2)}) collective-permute-start(bf16[9,128,128]{2,1,0:T(8,128)(2,1)} %get-tuple-element.123.refs_4_.refs_0_), channel_id=1, source_target_pairs={{1,2},{2,1},{5,6},{6,5},{9,10},{10,9},{13,14},{14,13},{17,18},{18,... | collective-permute-start | bytes 884744 | tf_op jit(solution)/shard_map/cond/branch_2_fun/ppermute | solution.py:292
  73.5 7.7 %copy-start.9 = (bf16[11,128,128]{2,1,0:T(8,128)(2,1)}, bf16[11,128,128]{2,1,0:T(8,128)(2,1)S(1)}, u32[]{:S(2)}) copy-start(bf16[11,128,128]{2,1,0:T(8,128)(2,1)S(1)} %collective-permute-done.39.refs_1_.high) | copy-start | bytes 1081348 | tf_op jit(solution)/shard_map/cond
  81.3 0.7 copy-start.10
  86.2 36.9 %collective-permute-start.42 = (bf16[11,128,128]{2,1,0:T(8,128)(2,1)}, bf16[11,128,128]{2,1,0:T(8,128)(2,1)S(1)}, u32[]{:S(2)}, u32[]{:S(2)}) collective-permute-start(bf16[11,128,128]{2,1,0:T(8,128)(2,1)} %get-tuple-element.120), channel_id=1, source_target_pairs={{1,0},{2,3},{0,1},{3,2},{5,4},{6,7},{4,5},{7,6},{9,8},{10,11},{8,9... | collective-permute-start | bytes 1081352 | tf_op jit(solution)/shard_map/cond/branch_2_fun/ppermute | solution.py:292
  88.2 34.9 %collective-permute-start.43 = (bf16[11,128,128]{2,1,0:T(8,128)(2,1)}, bf16[11,128,128]{2,1,0:T(8,128)(2,1)S(1)}, u32[]{:S(2)}, u32[]{:S(2)}) collective-permute-start(bf16[11,128,128]{2,1,0:T(8,128)(2,1)} %get-tuple-element.121), channel_id=1, source_target_pairs={{1,0},{2,3},{0,2},{3,1},{5,4},{6,7},{4,6},{7,5},{9,8},{10,11},{8,1... | collective-permute-start | bytes 1081352 | tf_op jit(solution)/shard_map/cond/branch_2_fun/ppermute | solution.py:292
  88.9 6.4 %copy-start.50 = (bf16[9,128,128]{2,1,0:T(8,128)(2,1)}, bf16[9,128,128]{2,1,0:T(8,128)(2,1)S(1)}, u32[]{:S(2)}) copy-start(bf16[9,128,128]{2,1,0:T(8,128)(2,1)S(1)} %collective-permute-done.48.refs_2_) | copy-start | bytes 884740 | tf_op jit(solution)/shard_map/cond
  88.9 6.4 %copy-start.15 = (bf16[10,128,128]{2,1,0:T(8,128)(2,1)}, bf16[10,128,128]{2,1,0:T(8,128)(2,1)S(1)}, u32[]{:S(2)}) copy-start(bf16[10,128,128]{2,1,0:T(8,128)(2,1)S(1)} %collective-permute-done.47.refs_1_.high) | copy-start | bytes 983044 | tf_op jit(solution)/shard_map/cond
  99.8 15.9 %collective-permute-start.50 = (bf16[9,128,128]{2,1,0:T(8,128)(2,1)}, bf16[9,128,128]{2,1,0:T(8,128)(2,1)S(1)}, u32[]{:S(2)}, u32[]{:S(2)}) collective-permute-start(bf16[9,128,128]{2,1,0:T(8,128)(2,1)} %get-tuple-element.127), channel_id=1, source_target_pairs={{1,0},{2,3},{0,1},{3,2},{5,4},{6,7},{4,5},{7,6},{9,8},{10,11},{8,9... | collective-permute-start | bytes 884744 | tf_op jit(solution)/shard_map/cond/branch_2_fun/ppermute | solution.py:292
  101.8 17.1 %collective-permute-start.51 = (bf16[9,128,128]{2,1,0:T(8,128)(2,1)}, bf16[9,128,128]{2,1,0:T(8,128)(2,1)S(1)}, u32[]{:S(2)}, u32[]{:S(2)}) collective-permute-start(bf16[9,128,128]{2,1,0:T(8,128)(2,1)} %get-tuple-element.128), channel_id=1, source_target_pairs={{1,0},{2,3},{0,2},{3,1},{5,4},{6,7},{4,6},{7,5},{9,8},{10,11},{8,1... | collective-permute-start | bytes 884744 | tf_op jit(solution)/shard_map/cond/branch_2_fun/ppermute | solution.py:292
  115.7 3.2 %copy-start.53 = (bf16[9,128,128]{2,1,0:T(8,128)(2,1)}, bf16[9,128,128]{2,1,0:T(8,128)(2,1)S(1)}, u32[]{:S(2)}) copy-start(bf16[9,128,128]{2,1,0:T(8,128)(2,1)S(1)} %collective-permute-done.50.high) | copy-start | bytes 884740 | tf_op jit(solution)/shard_map/cond
  123.1 0.9 copy-start.39
  (6 other events, 4.2 us)
